TPU v7x, 128 devices: a whole 4x4x4 slice. The times are simulated.
128 devices in a mesh: expert: 8 (over x, core), hidden: 16 (over z, y).
Axes of the slice: x: 4, y: 4, z: 4, core: 2. Of those that a mesh axis runs over, the one named last changes fastest.
Arguments:
- hidden_in: bfloat16 [2048, 6144], P(('expert', 'hidden')), may hold values from -6 to 6
- norm_gain: float32 [6144], replicated, may hold values from 0.25 to 1.75
- router_weight: bfloat16 [6144, 8], replicated, may hold values from -0.078125 to 0.078125
- expert_ids: int32 [2048, 2], P(('expert', 'hidden')), may hold values from 0 to 7, all different within a row; in each aligned block of 16 rows (0 to 15, 16 to 31, ...) at most 6 rows name the same one
- gate_proj: bfloat16 [8, 6144, 8192], P('expert', None, 'hidden'), may hold values from -0.078125 to 0.078125
- up_proj: bfloat16 [8, 6144, 8192], P('expert', None, 'hidden'), may hold values from -0.078125 to 0.078125
- down_proj: bfloat16 [8, 8192, 6144], P('expert', 'hidden'), may hold values from -0.0625 to 0.0625
Outputs:
- layer_out: bfloat16 [2048, 6144], P(('expert', 'hidden'))
Inputs may be any that keep to these rules, and one draw needn't show every extreme that they name: `expert_ids`: the two experts of a token differ. Within the rows of one device (aligned blocks of 16 tokens) no expert is named by more than 6 rows, a bound that some block reaches.
All inputs are finite; a program needn't handle non-finite values.
Results may differ from a plain program's by a relative error of at most 0.0085.
Values may be sent and summed in bfloat16 or wider, within the bound.
No kernel may reach another device: no remote copies, remote signals or barrier semaphores. Data moves between devices by JAX's collectives and lax.ppermute only.
A program may use at most 128 MiB of HBM per device.

v0:
```python
import functools

import jax
import jax.numpy as jnp
from jax import lax
from jax.experimental import pallas as pl
from jax.experimental.pallas import tpu as pltpu
from jax.sharding import PartitionSpec as P


RING = 4


PAD = 8
CHUNK = 512
MIX = 1024


def slots(ids_ref):
    first, second = ids_ref[0:1, :], ids_ref[1:2, :]
    tokens = first.shape[1]
    down = lax.broadcasted_iota(jnp.int32, (tokens, tokens), 0)
    across = lax.broadcasted_iota(jnp.int32, (tokens, tokens), 1)

    def column(row):
        return jnp.sum(jnp.where(down == across, row, 0), axis=1, keepdims=True)

    first_col, second_col = column(first), column(second)
    here = lax.axis_index("expert")
    found = []
    for ids, extra in ((first, 0), (second, (first == second).astype(jnp.int32))):
        same = (first_col == ids).astype(jnp.int32) + (second_col == ids).astype(jnp.int32)
        rank = jnp.sum(jnp.where(down < across, same, 0), axis=0, keepdims=True) + extra
        offset = ((ids >> 1) - (here >> 1)) & (RING - 1)
        place = jnp.where(offset == 0, 0, jnp.where(offset == RING - 1, 1, offset + 1))
        found.append((place, (ids & 1) ^ (here & 1), rank))
    return found


def route_kernel(hidden_ref, gain_ref, ids_ref, same_ref, other_ref, normed_ref):
    count, capacity, width = same_ref.shape
    tokens = hidden_ref.shape[0]
    values = hidden_ref[...].astype(jnp.float32)
    factor = lax.rsqrt(jnp.sum(values * values, axis=1, keepdims=True) / width + 1e-05)
    normed_ref[...] = (values * factor * gain_ref[...]).astype(jnp.bfloat16)
    first, second = [(core * count + place) * PAD + rank for place, core, rank in slots(ids_ref)]
    row = lax.broadcasted_iota(jnp.int32, (2 * count * PAD, tokens), 0)
    pick = jnp.where((row == first) | (row == second), 1.0, 0.0).astype(jnp.bfloat16)

    @pl.loop(0, width // CHUNK)
    def _(step):
        columns = pl.ds(pl.multiple_of(step * CHUNK, CHUNK), CHUNK)
        rows = jnp.dot(pick, normed_ref[:, columns], preferred_element_type=jnp.float32)
        for i in range(count):
            for core, out_ref in ((0, same_ref), (1, other_ref)):
                start = (core * count + i) * PAD
                out_ref[i, :, columns] = rows[start : start + capacity].astype(jnp.bfloat16)


def gate_kernel(capacity, normed_ref, router_ref, ids_ref, out_ref):
    logits = lax.dot_general(
        router_ref[...], normed_ref[...], (((1,), (1,)), ((), ())), preferred_element_type=jnp.float32
    )
    expert = lax.broadcasted_iota(jnp.int32, logits.shape, 0)
    chosen = [
        jnp.sum(jnp.where(expert == ids_ref[k : k + 1, :], logits, 0.0), axis=0, keepdims=True)
        for k in range(2)
    ]
    gate = 1.0 / (1.0 + jnp.exp(chosen[1] - chosen[0]))
    found = slots(ids_ref)
    row = lax.broadcasted_iota(jnp.int32, out_ref.shape[2:], 0)
    for half in range(2):
        first, second = [
            (core * RING + place) * 4 * capacity + (2 * half + core) * capacity + rank
            for place, core, rank in found
        ]
        rest = jnp.where(row == first, gate, 0.0) + jnp.where(row == second, 1.0 - gate, 0.0)
        for term in range(3):
            part = rest.astype(jnp.bfloat16)
            out_ref[half, term] = part
            rest = rest - part.astype(jnp.float32)


def mix_kernel(hidden_ref, weight_ref, own_ref, below_ref, above_ref, across_ref, other_ref, out_ref, held_ref):
    half = held_ref.shape[1]
    start = 0
    for ref in (own_ref, below_ref, above_ref, across_ref, other_ref):
        held_ref[start : start + ref.shape[0], :] = ref[...]
        start += ref.shape[0]

    @pl.loop(0, half // MIX)
    def _(step):
        rows = held_ref[:, pl.ds(pl.multiple_of(step * MIX, MIX), MIX)]
        for side in range(2):
            columns = pl.ds(pl.multiple_of(side * half + step * MIX, MIX), MIX)
            total = hidden_ref[:, columns].astype(jnp.float32)
            mixed = 0.0
            for term in (2, 1, 0):
                mixed = mixed + lax.dot_general(
                    weight_ref[side, term],
                    rows,
                    (((0,), (0,)), ((), ())),
                    preferred_element_type=jnp.float32,
                )
            out_ref[:, columns] = (total + mixed).astype(jnp.bfloat16)


def along_x(value, step):
    pairs = [(2 * x + c, 2 * ((x + step) % RING) + c) for x in range(RING) for c in range(2)]
    return lax.ppermute(value, "expert", pairs)


def other_core(value):
    return lax.ppermute(value, "expert", [(i, i ^ 1) for i in range(2 * RING)])


def shift(value, axis, step):
    def target(i):
        z, y = divmod(i, RING)
        return ((z + step) % RING) * RING + y if axis == "z" else z * RING + (y + step) % RING

    return lax.ppermute(value, "hidden", [(i, target(i)) for i in range(RING * RING)])


def gather_ring(own, first, second):
    half = own.shape[1] // 2
    below, above = shift(own, first, 1), shift(own, first, -1)
    across = [shift(below[:, :half], first, 1), shift(above[:, half:], first, -1)]
    mine = jnp.concatenate([own, below, above, jnp.concatenate(across, axis=1)], axis=0)
    mine = lax.optimization_barrier(mine)
    rows = mine.shape[0] // 2
    below, above = shift(mine, second, 1), shift(mine, second, -1)
    far = [shift(below[:rows], second, 1), shift(above[rows:], second, -1)]
    return [mine], [below, above], far


def add(*terms):
    total = terms[0].astype(jnp.float32)
    for term in terms[1:]:
        total = total + term.astype(jnp.float32)
    return total.astype(jnp.bfloat16)


def reduce_rings(stages, down, orders, rows):
    start, middle, end = stages
    both = range(2)

    def product(blocks):
        value = [block.reshape(-1, block.shape[-1]) for block in blocks]
        value = jnp.dot(jnp.concatenate(value, axis=0), down, preferred_element_type=jnp.float32)
        return lax.optimization_barrier(value.astype(jnp.bfloat16))

    def piece(value, base, count):
        return value[base * rows : (base + count) * rows]

    early = product([middle[:, :, 1:].swapaxes(1, 2), start[:, 0, 3]])
    down_one = [
        shift(jnp.concatenate([piece(early, 12 + i, 1), piece(early, 6 * i, 2)], axis=0), orders[i][0], -1)
        for i in both
    ]
    up_one = [shift(piece(early, 6 * i + 4, 2), orders[i][0], 1) for i in both]
    late = product([end[:, 0, 1:], start[:, 0, 1:3]])
    down_two = [shift(piece(late, 3 * i + 2, 1), orders[i][0], -1) for i in both]
    up_two = [
        shift(jnp.concatenate([piece(late, 7 + 2 * i, 1), piece(late, 3 * i + 1, 1)], axis=0), orders[i][0], 1)
        for i in both
    ]
    up_sum = [add(piece(early, 6 * i + 2, 2), up_one[i]) for i in both]
    down_sum = [
        jnp.concatenate(
            [add(piece(late, 6 + 2 * i, 1), down_one[i][:rows]), add(piece(late, 3 * i, 1), down_two[i])], axis=0
        )
        for i in both
    ]
    up_three = [shift(up_sum[i], orders[i][0], 1) for i in both]
    down_three = [shift(down_sum[i], orders[i][0], -1) for i in both]
    kept = [product([start[i, 0, 0], end[i, 0, 0], middle[i, :, 0]]) for i in both]
    results = []
    for i in both:
        second = orders[i][1]
        half = down.shape[1] // 2
        outer = add(kept[i][: 2 * rows], up_two[i], down_three[i])
        inner = add(kept[i][2 * rows :], up_three[i], down_one[i][rows:])
        own, across = outer[:rows], outer[rows:]
        below, above = inner[:rows], inner[rows:]
        low = shift(across[:, :half], second, 1)
        high = shift(across[:, half:], second, -1)
        above = jnp.concatenate([add(above[:, :half], low), above[:, half:]], axis=1)
        below = jnp.concatenate([below[:, :half], add(below[:, half:], high)], axis=1)
        results.append(add(own, shift(above, second, 1), shift(below, second, -1)))
    return results


def pack(value):
    half = value.shape[1] // 2
    return jnp.concatenate([value[:, :half], value[:, half:]], axis=0)


def unpack(value):
    half = value.shape[0] // 2
    return jnp.concatenate([value[:half], value[half:]], axis=1)


def per_device(hidden_in, norm_gain, router_weight, expert_ids, gate_proj, up_proj, down_proj):
    experts = lax.axis_size("expert")
    tok_rows = hidden_in.shape[0]
    width = hidden_in.shape[1]
    top_count = expert_ids.shape[1]
    capacity = 3 * tok_rows * top_count // (2 * experts)
    rows = experts * capacity
    ids = expert_ids.T
    piece = jax.ShapeDtypeStruct((RING, capacity, width), jnp.bfloat16)
    same, other, normed = pl.pallas_call(
        route_kernel,
        out_shape=(piece, piece, jax.ShapeDtypeStruct((tok_rows, width), jnp.bfloat16)),
        compiler_params=pltpu.CompilerParams(vmem_limit_bytes=8 * 1024 * 1024),
        name="route",
    )(hidden_in, norm_gain.reshape(1, width), ids)
    weights = pl.pallas_call(
        functools.partial(gate_kernel, capacity),
        out_shape=jax.ShapeDtypeStruct((2, 3, 8 * RING * capacity, tok_rows), jnp.bfloat16),
        compiler_params=pltpu.CompilerParams(vmem_limit_bytes=4 * 1024 * 1024),
    name="gates",
    )(normed, router_weight.T, ids)
    gate_local = gate_proj[0]
    up_local = up_proj[0]
    down_local = down_proj[0]
    other = other_core(other)
    both = [jnp.concatenate([same[i], other[i]], axis=0) for i in range(RING)]
    moved = [unpack(along_x(pack(both[i]), step)) for i, step in ((2, 1), (1, -1), (3, 2))]
    arrived = [jnp.concatenate([both[0], moved[0]], axis=0), jnp.concatenate(moved[1:], axis=0)]
    arrived = [lax.optimization_barrier(value) for value in arrived]
    part = rows // 2
    orders = (("z", "y"), ("y", "z"))
    gathered = [gather_ring(arrived[i], *orders[i]) for i in range(2)]
    stages = []
    for stage in range(3):
        value = jnp.concatenate(gathered[0][stage] + gathered[1][stage], axis=0)
        gate = jnp.dot(value, gate_local, preferred_element_type=jnp.float32)
        upper = jnp.dot(value, up_local, preferred_element_type=jnp.float32)
        act = (jax.nn.silu(gate) * upper).astype(jnp.bfloat16)
        stages.append(act.reshape(2, -1, RING, part, act.shape[1]))
    answers = reduce_rings(stages, down_local, orders, part)
    half = part // 2
    back = [
        pack(answers[0][:half]),
        along_x(pack(answers[1][:half]), 1),
        along_x(pack(answers[0][half:]), -1),
        along_x(pack(answers[1][half:]), 2),
    ]
    back[0] = lax.optimization_barrier(back[0])
    crossed = other_core(jnp.concatenate(back, axis=0))
    return pl.pallas_call(
        mix_kernel,
        out_shape=jax.ShapeDtypeStruct((tok_rows, width), jnp.bfloat16),
        scratch_shapes=[pltpu.VMEM((8 * RING * capacity, width // 2), jnp.bfloat16)],
        compiler_params=pltpu.CompilerParams(vmem_limit_bytes=8 * 1024 * 1024),
        name="mix",
    )(hidden_in, weights, *back, crossed)


def solution(mesh):
    placed = (
        P(("expert", "hidden"), None),
        P(),
        P(),
        P(("expert", "hidden"), None),
        P("expert", None, "hidden"),
        P("expert", None, "hidden"),
        P("expert", "hidden", None),
    )

    return jax.shard_map(
        per_device,
        mesh=mesh,
        in_specs=placed,
        out_specs=P(("expert", "hidden"), None),
        check_vma=False,
    )
```

profile of v0, /device:TPU:1, one launch (start us, length us, event | category | flops | bytes accessed | tf_op | source)
XLA Modules:
  0.0 189.6 jit_solution(759562365007627778)
XLA Ops:
  7.1 2.9 %collective-permute-start.7 = (bf16[24,3072]{1,0:T(8,128)(2,1)S(1)}, bf16[24,3072]{1,0:T(8,128)(2,1)S(1)}, u32[]{:S(2)}, u32[]{:S(2)}) collective-permute-start(bf16[24,3072]{1,0:T(8,128)(2,1)S(1)} %fusion.28), channel_id=1, source_target_pairs={{0,64},{16,80},{32,96},{48,112},{64,0},{80,16},{96,32},{112,48},{1... | collective-permute-start | bytes 442376 | tf_op jit(solution)/shard_map/ppermute | solution.py:110
  13.1 4.3 %collective-permute-done.1 = bf16[24,3072]{1,0:T(8,128)(2,1)S(1)} collective-permute-done((bf16[24,3072]{1,0:T(8,128)(2,1)S(1)}, bf16[24,3072]{1,0:T(8,128)(2,1)S(1)}, u32[]{:S(2)}, u32[]{:S(2)}) %collective-permute-start.1) | collective-permute-done | bytes 147488 | tf_op jit(solution)/shard_map/ppermute | solution.py:110
  17.5 3.9 %collective-permute-start.3 = (bf16[24,6144]{1,0:T(8,128)(2,1)S(1)}, bf16[24,6144]{1,0:T(8,128)(2,1)S(1)}, u32[]{:S(2)}, u32[]{:S(2)}) collective-permute-start(bf16[24,6144]{1,0:T(8,128)(2,1)S(1)} %maximum_maximum_fusion.2), channel_id=1, source_target_pairs={{0,12},{1,13},{2,14},{3,15},{4,0},{5,1},{6,2},{7,3},{8,4},{9,5},{1... | collective-permute-start | bytes 884744 | tf_op jit(solution)/shard_map/ppermute | solution.py:122
  21.6 2.8 %collective-permute-start.9 = (bf16[24,6144]{1,0:T(8,128)(2,1)S(1)}, bf16[24,6144]{1,0:T(8,128)(2,1)S(1)}, u32[]{:S(2)}, u32[]{:S(2)}) collective-permute-start(bf16[24,6144]{1,0:T(8,128)(2,1)S(1)} %maximum_maximum_fusion.3), channel_id=1, source_target_pairs={{0,3},{1,0},{2,1},{3,2},{4,7},{5,4},{6,5},{7,6},{8,11},{9,8},{10,9... | collective-permute-start | bytes 884744 | tf_op jit(solution)/shard_map/ppermute | solution.py:122
  26.8 3.5 %collective-permute-start.5 = (bf16[24,3072]{1,0:T(8,128)(2,1)S(1)}, bf16[24,3072]{1,0:T(8,128)(2,1)S(1)}, u32[]{:S(2)}, u32[]{:S(2)}) collective-permute-start(bf16[24,3072]{1,0:T(8,128)(2,1)S(1)} %slice.381), channel_id=1, source_target_pairs={{0,12},{1,13},{2,14},{3,15},{4,0},{5,1},{6,2},{7,3},{8,4},{9,5},{1... | collective-permute-start | bytes 442376 | tf_op jit(solution)/shard_map/ppermute | solution.py:122
  30.4 2.8 %collective-permute-start.11 = (bf16[24,3072]{1,0:T(8,128)(2,1)S(1)}, bf16[24,3072]{1,0:T(8,128)(2,1)S(1)}, u32[]{:S(2)}, u32[]{:S(2)}) collective-permute-start(bf16[24,3072]{1,0:T(8,128)(2,1)S(1)} %slice.393), channel_id=1, source_target_pairs={{0,3},{1,0},{2,1},{3,2},{4,7},{5,4},{6,5},{7,6},{8,11},{9,8},{10,9... | collective-permute-start | bytes 442376 | tf_op jit(solution)/shard_map/ppermute | solution.py:122
  38.8 2.9 %collective-permute-start.18 = (bf16[96,6144]{1,0:T(8,128)(2,1)S(1)}, bf16[96,6144]{1,0:T(8,128)(2,1)S(1)}, u32[]{:S(2)}, u32[]{:S(2)}) collective-permute-start(bf16[96,6144]{1,0:T(8,128)(2,1)S(1)} %maximum_maximum_fusion.1), channel_id=1, source_target_pairs={{0,12},{1,13},{2,14},{3,15},{4,0},{5,1},{6,2},{7,3},{8,4},{9,5},{1... | collective-permute-start | bytes 3538952 | tf_op jit(solution)/shard_map/ppermute | solution.py:122
  44.5 20.1 %collective-permute-done.12 = bf16[96,6144]{1,0:T(8,128)(2,1)S(1)} collective-permute-done((bf16[96,6144]{1,0:T(8,128)(2,1)S(1)}, bf16[96,6144]{1,0:T(8,128)(2,1)S(1)}, u32[]{:S(2)}, u32[]{:S(2)}) %collective-permute-start.12) | collective-permute-done | bytes 1179680 | tf_op jit(solution)/shard_map/ppermute | solution.py:122
  67.5 2.6 %multiply_convert_fusion = bf16[384,512]{1,0:T(8,128)(2,1)S(1)} fusion(f32[384,512]{1,0:T(8,128)S(1)} %fusion.10, bf16[384,6144]{1,0:T(8,128)(2,1)S(1)} %constant_dynamic-update-slice_fusion.4, bf16[1,6144,512]{2,1,0:T(8,128)(2,1)S(1)} %bitcast.93), kind=kOutput, calls=%fused_computation.33 | convolution fusion | flops 2417098752 | bytes 12189696 | tf_op jit(solution)/shard_map/dot_general | solution.py:240
  73.1 2.7 %collective-permute-start.21 = (bf16[72,6144]{1,0:T(8,128)(2,1)S(1)}, bf16[72,6144]{1,0:T(8,128)(2,1)S(1)}, u32[]{:S(2)}, u32[]{:S(2)}) collective-permute-start(bf16[72,6144]{1,0:T(8,128)(2,1)S(1)} %pad_maximum_fusion.7), channel_id=1, source_target_pairs={{0,12},{1,13},{2,14},{3,15},{4,0},{5,1},{6,2},{7,3},{8,4},{9,5},{1... | collective-permute-start | bytes 2654216 | tf_op jit(solution)/shard_map/ppermute | solution.py:122
  78.9 19.2 %collective-permute-done.13 = bf16[48,6144]{1,0:T(8,128)(2,1)S(1)} collective-permute-done((bf16[48,6144]{1,0:T(8,128)(2,1)S(1)}, bf16[48,6144]{1,0:T(8,128)(2,1)S(1)}, u32[]{:S(2)}, u32[]{:S(2)}) %collective-permute-start.13) | collective-permute-done | bytes 589856 | tf_op jit(solution)/shard_map/ppermute | solution.py:122
  98.1 2.7 %collective-permute-start.19 = (bf16[48,6144]{1,0:T(8,128)(2,1)S(1)}, bf16[48,6144]{1,0:T(8,128)(2,1)S(1)}, u32[]{:S(2)}, u32[]{:S(2)}) collective-permute-start(bf16[48,6144]{1,0:T(8,128)(2,1)S(1)} %slice.398), channel_id=1, source_target_pairs={{0,12},{1,13},{2,14},{3,15},{4,0},{5,1},{6,2},{7,3},{8,4},{9,5},{1... | collective-permute-start | bytes 1769480 | tf_op jit(solution)/shard_map/ppermute | solution.py:122
  100.9 8.8 %collective-permute-done.17 = bf16[48,6144]{1,0:T(8,128)(2,1)S(1)} collective-permute-done((bf16[48,6144]{1,0:T(8,128)(2,1)S(1)}, bf16[48,6144]{1,0:T(8,128)(2,1)S(1)}, u32[]{:S(2)}, u32[]{:S(2)}) %collective-permute-start.17) | collective-permute-done | bytes 589856 | tf_op jit(solution)/shard_map/ppermute | solution.py:122
  116.1 2.7 %collective-permute-start.22 = (bf16[24,6144]{1,0:T(8,128)(2,1)S(1)}, bf16[24,6144]{1,0:T(8,128)(2,1)S(1)}, u32[]{:S(2)}, u32[]{:S(2)}) collective-permute-start(bf16[24,6144]{1,0:T(8,128)(2,1)S(1)} %get-tuple-element.22), channel_id=1, source_target_pairs={{0,12},{1,13},{2,14},{3,15},{4,0},{5,1},{6,2},{7,3},{8,4},{9,5},{1... | collective-permute-start | bytes 884744 | tf_op jit(solution)/shard_map/ppermute | solution.py:122
  120.1 5.4 %collective-permute-done.31 = bf16[72,6144]{1,0:T(8,128)(2,1)S(1)} collective-permute-done((bf16[72,6144]{1,0:T(8,128)(2,1)S(1)}, bf16[72,6144]{1,0:T(8,128)(2,1)S(1)}, u32[]{:S(2)}, u32[]{:S(2)}) %collective-permute-start.31) | collective-permute-done | bytes 884768 | tf_op jit(solution)/shard_map/ppermute | solution.py:122
  125.6 6.3 %collective-permute-done.32 = bf16[24,6144]{1,0:T(8,128)(2,1)S(1)} collective-permute-done((bf16[24,6144]{1,0:T(8,128)(2,1)S(1)}, bf16[24,6144]{1,0:T(8,128)(2,1)S(1)}, u32[]{:S(2)}, u32[]{:S(2)}) %collective-permute-start.32) | collective-permute-done | bytes 294944 | tf_op jit(solution)/shard_map/ppermute | solution.py:122
  132.3 2.7 %collective-permute-start.33 = (bf16[48,6144]{1,0:T(8,128)(2,1)S(1)}, bf16[48,6144]{1,0:T(8,128)(2,1)S(1)}, u32[]{:S(2)}, u32[]{:S(2)}) collective-permute-start(bf16[48,6144]{1,0:T(8,128)(2,1)S(1)} %pad_maximum_fusion.12), channel_id=1, source_target_pairs={{0,3},{1,0},{2,1},{3,2},{4,7},{5,4},{6,5},{7,6},{8,11},{9,8},{10,9... | collective-permute-start | bytes 1769480 | tf_op jit(solution)/shard_map/ppermute | solution.py:122
  136.7 4.6 %collective-permute-done.23 = bf16[48,6144]{1,0:T(8,128)(2,1)S(1)} collective-permute-done((bf16[48,6144]{1,0:T(8,128)(2,1)S(1)}, bf16[48,6144]{1,0:T(8,128)(2,1)S(1)}, u32[]{:S(2)}, u32[]{:S(2)}) %collective-permute-start.23) | collective-permute-done | bytes 589856 | tf_op jit(solution)/shard_map/ppermute | solution.py:122
  141.8 2.7 %collective-permute-start.28 = (bf16[24,3072]{1,0:T(8,128)(2,1)S(1)}, bf16[24,3072]{1,0:T(8,128)(2,1)S(1)}, u32[]{:S(2)}, u32[]{:S(2)}) collective-permute-start(bf16[24,3072]{1,0:T(8,128)(2,1)S(1)} %get-tuple-element.42), channel_id=1, source_target_pairs={{0,3},{1,0},{2,1},{3,2},{4,7},{5,4},{6,5},{7,6},{8,11},{9,8},{10,9... | collective-permute-start | bytes 442376 | tf_op jit(solution)/shard_map/ppermute | solution.py:122
  145.5 2.7 %collective-permute-start.38 = (bf16[24,3072]{1,0:T(8,128)(2,1)S(1)}, bf16[24,3072]{1,0:T(8,128)(2,1)S(1)}, u32[]{:S(2)}, u32[]{:S(2)}) collective-permute-start(bf16[24,3072]{1,0:T(8,128)(2,1)S(1)} %get-tuple-element.36), channel_id=1, source_target_pairs={{0,12},{1,13},{2,14},{3,15},{4,0},{5,1},{6,2},{7,3},{8,4},{9,5},{1... | collective-permute-start | bytes 442376 | tf_op jit(solution)/shard_map/ppermute | solution.py:122
  149.0 3.1 %collective-permute-start.29 = (bf16[24,6144]{1,0:T(8,128)(2,1)S(1)}, bf16[24,6144]{1,0:T(8,128)(2,1)S(1)}, u32[]{:S(2)}, u32[]{:S(2)}) collective-permute-start(bf16[24,6144]{1,0:T(8,128)(2,1)S(1)} %pad_maximum_fusion.15), channel_id=1, source_target_pairs={{0,3},{1,0},{2,1},{3,2},{4,7},{5,4},{6,5},{7,6},{8,11},{9,8},{10,9... | collective-permute-start | bytes 884744 | tf_op jit(solution)/shard_map/ppermute | solution.py:122
  156.1 4.7 %collective-permute-done.27 = bf16[24,6144]{1,0:T(8,128)(2,1)S(1)} collective-permute-done((bf16[24,6144]{1,0:T(8,128)(2,1)S(1)}, bf16[24,6144]{1,0:T(8,128)(2,1)S(1)}, u32[]{:S(2)}, u32[]{:S(2)}) %collective-permute-start.27) | collective-permute-done | bytes 294944 | tf_op jit(solution)/shard_map/ppermute | solution.py:122
  161.4 2.7 %collective-permute-start.41 = (bf16[24,3072]{1,0:T(8,128)(2,1)S(1)}, bf16[24,3072]{1,0:T(8,128)(2,1)S(1)}, u32[]{:S(2)}, u32[]{:S(2)}) collective-permute-start(bf16[24,3072]{1,0:T(8,128)(2,1)S(1)} %pad_maximum_fusion.23), channel_id=1, source_target_pairs={{0,96},{16,112},{32,0},{48,16},{64,32},{80,48},{96,64},{112,80},{1... | collective-permute-start | bytes 442376 | tf_op jit(solution)/shard_map/ppermute | solution.py:110
  169.7 16.1 %collective-permute-start.43 = (bf16[96,3072]{1,0:T(8,128)(2,1)S(1)}, bf16[96,3072]{1,0:T(8,128)(2,1)S(1)}, u32[]{:S(2)}, u32[]{:S(2)}) collective-permute-start(bf16[96,3072]{1,0:T(8,128)(2,1)S(1)} %pad_maximum_fusion.13), channel_id=1, source_target_pairs={{0,16},{16,0},{32,48},{48,32},{64,80},{80,64},{96,112},{112,96},{1... | collective-permute-start | bytes 1769480 | tf_op jit(solution)/shard_map/ppermute | solution.py:114
  (171 shorter events, 55.7 us)
Async XLA Ops:
  7.1 14.3 %collective-permute-start.7 = (bf16[24,3072]{1,0:T(8,128)(2,1)S(1)}, bf16[24,3072]{1,0:T(8,128)(2,1)S(1)}, u32[]{:S(2)}, u32[]{:S(2)}) collective-permute-start(bf16[24,3072]{1,0:T(8,128)(2,1)S(1)} %fusion.28), channel_id=1, source_target_pairs={{0,64},{16,80},{32,96},{48,112},{64,0},{80,16},{96,32},{112,48},{1... | collective-permute-start | bytes 442376 | tf_op jit(solution)/shard_map/ppermute | solution.py:110
  10.6 10.8 %collective-permute-start.6 = (bf16[24,3072]{1,0:T(8,128)(2,1)S(1)}, bf16[24,3072]{1,0:T(8,128)(2,1)S(1)}, u32[]{:S(2)}, u32[]{:S(2)}) collective-permute-start(bf16[24,3072]{1,0:T(8,128)(2,1)S(1)} %fusion.29), channel_id=1, source_target_pairs={{0,96},{16,112},{32,0},{48,16},{64,32},{80,48},{96,64},{112,80},{1... | collective-permute-start | bytes 442376 | tf_op jit(solution)/shard_map/ppermute | solution.py:110
  17.5 9.3 %collective-permute-start.3 = (bf16[24,6144]{1,0:T(8,128)(2,1)S(1)}, bf16[24,6144]{1,0:T(8,128)(2,1)S(1)}, u32[]{:S(2)}, u32[]{:S(2)}) collective-permute-start(bf16[24,6144]{1,0:T(8,128)(2,1)S(1)} %maximum_maximum_fusion.2), channel_id=1, source_target_pairs={{0,12},{1,13},{2,14},{3,15},{4,0},{5,1},{6,2},{7,3},{8,4},{9,5},{1... | collective-permute-start | bytes 884744 | tf_op jit(solution)/shard_map/ppermute | solution.py:122
  35.7 28.9 %collective-permute-start.12 = (bf16[96,6144]{1,0:T(8,128)(2,1)S(1)}, bf16[96,6144]{1,0:T(8,128)(2,1)S(1)}, u32[]{:S(2)}, u32[]{:S(2)}) collective-permute-start(bf16[96,6144]{1,0:T(8,128)(2,1)S(1)} %maximum_maximum_fusion), channel_id=1, source_target_pairs={{0,1},{1,2},{2,3},{3,0},{4,5},{5,6},{6,7},{7,4},{8,9},{9,10},{10,1... | collective-permute-start | bytes 3538952 | tf_op jit(solution)/shard_map/ppermute | solution.py:122
  37.0 27.6 %collective-permute-start.14 = (bf16[96,6144]{1,0:T(8,128)(2,1)S(1)}, bf16[96,6144]{1,0:T(8,128)(2,1)S(1)}, u32[]{:S(2)}, u32[]{:S(2)}) collective-permute-start(bf16[96,6144]{1,0:T(8,128)(2,1)S(1)} %maximum_maximum_fusion), channel_id=1, source_target_pairs={{0,3},{1,0},{2,1},{3,2},{4,7},{5,4},{6,5},{7,6},{8,11},{9,8},{10,9... | collective-permute-start | bytes 3538952 | tf_op jit(solution)/shard_map/ppermute | solution.py:122
  38.7 26.0 %collective-permute-start.16 = (bf16[96,6144]{1,0:T(8,128)(2,1)S(1)}, bf16[96,6144]{1,0:T(8,128)(2,1)S(1)}, u32[]{:S(2)}, u32[]{:S(2)}) collective-permute-start(bf16[96,6144]{1,0:T(8,128)(2,1)S(1)} %maximum_maximum_fusion.1), channel_id=1, source_target_pairs={{0,4},{1,5},{2,6},{3,7},{4,8},{5,9},{6,10},{7,11},{8,12},{9,13},{1... | collective-permute-start | bytes 3538952 | tf_op jit(solution)/shard_map/ppermute | solution.py:122
  38.8 26.1 %collective-permute-start.18 = (bf16[96,6144]{1,0:T(8,128)(2,1)S(1)}, bf16[96,6144]{1,0:T(8,128)(2,1)S(1)}, u32[]{:S(2)}, u32[]{:S(2)}) collective-permute-start(bf16[96,6144]{1,0:T(8,128)(2,1)S(1)} %maximum_maximum_fusion.1), channel_id=1, source_target_pairs={{0,12},{1,13},{2,14},{3,15},{4,0},{5,1},{6,2},{7,3},{8,4},{9,5},{1... | collective-permute-start | bytes 3538952 | tf_op jit(solution)/shard_map/ppermute | solution.py:122
  72.8 39.7 %collective-permute-start.34 = (bf16[48,6144]{1,0:T(8,128)(2,1)S(1)}, bf16[48,6144]{1,0:T(8,128)(2,1)S(1)}, u32[]{:S(2)}, u32[]{:S(2)}) collective-permute-start(bf16[48,6144]{1,0:T(8,128)(2,1)S(1)} %get-tuple-element.13), channel_id=1, source_target_pairs={{0,1},{1,2},{2,3},{3,0},{4,5},{5,6},{6,7},{7,4},{8,9},{9,10},{10,1... | collective-permute-start | bytes 1769480 | tf_op jit(solution)/shard_map/ppermute | solution.py:122
  72.9 39.7 %collective-permute-start.24 = (bf16[48,6144]{1,0:T(8,128)(2,1)S(1)}, bf16[48,6144]{1,0:T(8,128)(2,1)S(1)}, u32[]{:S(2)}, u32[]{:S(2)}) collective-permute-start(bf16[48,6144]{1,0:T(8,128)(2,1)S(1)} %get-tuple-element.15), channel_id=1, source_target_pairs={{0,4},{1,5},{2,6},{3,7},{4,8},{5,9},{6,10},{7,11},{8,12},{9,13},{1... | collective-permute-start | bytes 1769480 | tf_op jit(solution)/shard_map/ppermute | solution.py:122
  73.1 47.0 %collective-permute-start.21 = (bf16[72,6144]{1,0:T(8,128)(2,1)S(1)}, bf16[72,6144]{1,0:T(8,128)(2,1)S(1)}, u32[]{:S(2)}, u32[]{:S(2)}) collective-permute-start(bf16[72,6144]{1,0:T(8,128)(2,1)S(1)} %pad_maximum_fusion.7), channel_id=1, source_target_pairs={{0,12},{1,13},{2,14},{3,15},{4,0},{5,1},{6,2},{7,3},{8,4},{9,5},{1... | collective-permute-start | bytes 2654216 | tf_op jit(solution)/shard_map/ppermute | solution.py:122
  75.9 22.2 %collective-permute-start.13 = (bf16[48,6144]{1,0:T(8,128)(2,1)S(1)}, bf16[48,6144]{1,0:T(8,128)(2,1)S(1)}, u32[]{:S(2)}, u32[]{:S(2)}) collective-permute-start(bf16[48,6144]{1,0:T(8,128)(2,1)S(1)} %slice.395), channel_id=1, source_target_pairs={{0,1},{1,2},{2,3},{3,0},{4,5},{5,6},{6,7},{7,4},{8,9},{9,10},{10,1... | collective-permute-start | bytes 1769480 | tf_op jit(solution)/shard_map/ppermute | solution.py:122
  76.1 22.0 %collective-permute-start.15 = (bf16[48,6144]{1,0:T(8,128)(2,1)S(1)}, bf16[48,6144]{1,0:T(8,128)(2,1)S(1)}, u32[]{:S(2)}, u32[]{:S(2)}) collective-permute-start(bf16[48,6144]{1,0:T(8,128)(2,1)S(1)} %slice.396), channel_id=1, source_target_pairs={{0,3},{1,0},{2,1},{3,2},{4,7},{5,4},{6,5},{7,6},{8,11},{9,8},{10,9... | collective-permute-start | bytes 1769480 | tf_op jit(solution)/shard_map/ppermute | solution.py:122
  98.0 11.6 %collective-permute-start.17 = (bf16[48,6144]{1,0:T(8,128)(2,1)S(1)}, bf16[48,6144]{1,0:T(8,128)(2,1)S(1)}, u32[]{:S(2)}, u32[]{:S(2)}) collective-permute-start(bf16[48,6144]{1,0:T(8,128)(2,1)S(1)} %slice.397), channel_id=1, source_target_pairs={{0,4},{1,5},{2,6},{3,7},{4,8},{5,9},{6,10},{7,11},{8,12},{9,13},{1... | collective-permute-start | bytes 1769480 | tf_op jit(solution)/shard_map/ppermute | solution.py:122
  98.1 11.6 %collective-permute-start.19 = (bf16[48,6144]{1,0:T(8,128)(2,1)S(1)}, bf16[48,6144]{1,0:T(8,128)(2,1)S(1)}, u32[]{:S(2)}, u32[]{:S(2)}) collective-permute-start(bf16[48,6144]{1,0:T(8,128)(2,1)S(1)} %slice.398), channel_id=1, source_target_pairs={{0,12},{1,13},{2,14},{3,15},{4,0},{5,1},{6,2},{7,3},{8,4},{9,5},{1... | collective-permute-start | bytes 1769480 | tf_op jit(solution)/shard_map/ppermute | solution.py:122
  109.7 15.9 %collective-permute-start.31 = (bf16[72,6144]{1,0:T(8,128)(2,1)S(1)}, bf16[72,6144]{1,0:T(8,128)(2,1)S(1)}, u32[]{:S(2)}, u32[]{:S(2)}) collective-permute-start(bf16[72,6144]{1,0:T(8,128)(2,1)S(1)} %pad_maximum_fusion.8), channel_id=1, source_target_pairs={{0,3},{1,0},{2,1},{3,2},{4,7},{5,4},{6,5},{7,6},{8,11},{9,8},{10,9... | collective-permute-start | bytes 2654216 | tf_op jit(solution)/shard_map/ppermute | solution.py:122
  112.9 19.4 %collective-permute-start.25 = (bf16[48,6144]{1,0:T(8,128)(2,1)S(1)}, bf16[48,6144]{1,0:T(8,128)(2,1)S(1)}, u32[]{:S(2)}, u32[]{:S(2)}) collective-permute-start(bf16[48,6144]{1,0:T(8,128)(2,1)S(1)} %get-tuple-element.12), channel_id=1, source_target_pairs={{0,4},{1,5},{2,6},{3,7},{4,8},{5,9},{6,10},{7,11},{8,12},{9,13},{1... | collective-permute-start | bytes 1769480 | tf_op jit(solution)/shard_map/ppermute | solution.py:122
  116.0 15.9 %collective-permute-start.32 = (bf16[24,6144]{1,0:T(8,128)(2,1)S(1)}, bf16[24,6144]{1,0:T(8,128)(2,1)S(1)}, u32[]{:S(2)}, u32[]{:S(2)}) collective-permute-start(bf16[24,6144]{1,0:T(8,128)(2,1)S(1)} %get-tuple-element.20), channel_id=1, source_target_pairs={{0,3},{1,0},{2,1},{3,2},{4,7},{5,4},{6,5},{7,6},{8,11},{9,8},{10,9... | collective-permute-start | bytes 884744 | tf_op jit(solution)/shard_map/ppermute | solution.py:122
  116.1 15.8 %collective-permute-start.22 = (bf16[24,6144]{1,0:T(8,128)(2,1)S(1)}, bf16[24,6144]{1,0:T(8,128)(2,1)S(1)}, u32[]{:S(2)}, u32[]{:S(2)}) collective-permute-start(bf16[24,6144]{1,0:T(8,128)(2,1)S(1)} %get-tuple-element.22), channel_id=1, source_target_pairs={{0,12},{1,13},{2,14},{3,15},{4,0},{5,1},{6,2},{7,3},{8,4},{9,5},{1... | collective-permute-start | bytes 884744 | tf_op jit(solution)/shard_map/ppermute | solution.py:122
  120.0 16.6 %collective-permute-start.20 = (bf16[48,6144]{1,0:T(8,128)(2,1)S(1)}, bf16[48,6144]{1,0:T(8,128)(2,1)S(1)}, u32[]{:S(2)}, u32[]{:S(2)}) collective-permute-start(bf16[48,6144]{1,0:T(8,128)(2,1)S(1)} %pad_maximum_fusion.9), channel_id=1, source_target_pairs={{0,4},{1,5},{2,6},{3,7},{4,8},{5,9},{6,10},{7,11},{8,12},{9,13},{1... | collective-permute-start | bytes 1769480 | tf_op jit(solution)/shard_map/ppermute | solution.py:122
  125.5 19.1 %collective-permute-start.35 = (bf16[48,6144]{1,0:T(8,128)(2,1)S(1)}, bf16[48,6144]{1,0:T(8,128)(2,1)S(1)}, u32[]{:S(2)}, u32[]{:S(2)}) collective-permute-start(bf16[48,6144]{1,0:T(8,128)(2,1)S(1)} %get-tuple-element.11), channel_id=1, source_target_pairs={{0,1},{1,2},{2,3},{3,0},{4,5},{5,6},{6,7},{7,4},{8,9},{9,10},{10,1... | collective-permute-start | bytes 1769480 | tf_op jit(solution)/shard_map/ppermute | solution.py:122
  131.9 13.1 %collective-permute-start.30 = (bf16[48,6144]{1,0:T(8,128)(2,1)S(1)}, bf16[48,6144]{1,0:T(8,128)(2,1)S(1)}, u32[]{:S(2)}, u32[]{:S(2)}) collective-permute-start(bf16[48,6144]{1,0:T(8,128)(2,1)S(1)} %pad_maximum_fusion.11), channel_id=1, source_target_pairs={{0,1},{1,2},{2,3},{3,0},{4,5},{5,6},{6,7},{7,4},{8,9},{9,10},{10,1... | collective-permute-start | bytes 1769480 | tf_op jit(solution)/shard_map/ppermute | solution.py:122
  132.2 9.1 %collective-permute-start.23 = (bf16[48,6144]{1,0:T(8,128)(2,1)S(1)}, bf16[48,6144]{1,0:T(8,128)(2,1)S(1)}, u32[]{:S(2)}, u32[]{:S(2)}) collective-permute-start(bf16[48,6144]{1,0:T(8,128)(2,1)S(1)} %pad_maximum_fusion.10), channel_id=1, source_target_pairs={{0,12},{1,13},{2,14},{3,15},{4,0},{5,1},{6,2},{7,3},{8,4},{9,5},{1... | collective-permute-start | bytes 1769480 | tf_op jit(solution)/shard_map/ppermute | solution.py:122
  132.3 12.6 %collective-permute-start.33 = (bf16[48,6144]{1,0:T(8,128)(2,1)S(1)}, bf16[48,6144]{1,0:T(8,128)(2,1)S(1)}, u32[]{:S(2)}, u32[]{:S(2)}) collective-permute-start(bf16[48,6144]{1,0:T(8,128)(2,1)S(1)} %pad_maximum_fusion.12), channel_id=1, source_target_pairs={{0,3},{1,0},{2,1},{3,2},{4,7},{5,4},{6,5},{7,6},{8,11},{9,8},{10,9... | collective-permute-start | bytes 1769480 | tf_op jit(solution)/shard_map/ppermute | solution.py:122
  169.7 17.7 %collective-permute-start.43 = (bf16[96,3072]{1,0:T(8,128)(2,1)S(1)}, bf16[96,3072]{1,0:T(8,128)(2,1)S(1)}, u32[]{:S(2)}, u32[]{:S(2)}) collective-permute-start(bf16[96,3072]{1,0:T(8,128)(2,1)S(1)} %pad_maximum_fusion.13), channel_id=1, source_target_pairs={{0,16},{16,0},{32,48},{48,32},{64,80},{80,64},{96,112},{112,96},{1... | collective-permute-start | bytes 1769480 | tf_op jit(solution)/shard_map/ppermute | solution.py:114
  (31 other events, 253.9 us)
where the time goes:
time: 190 us
  waiting for transfers between devices  90.9 us (48%)
  starting transfers between devices  69.6 us (37%)
  matrix products  17.1 us (9%)
  Pallas kernels  4.22 us (2%)
  local copies, waits for them, and re-layouts  3.82 us (2%)
  other arithmetic  3 us (2%)
    ppermute x36, waiting for transfers between devices, shift(): lax.ppermute(value, 'hidden', [(i, target(i)) for i in range(RING * RING)])  78.6 us
    ppermute x36, starting transfers between devices, shift(): lax.ppermute(value, 'hidden', [(i, target(i)) for i in range(RING * RING)])  43.5 us
    ppermute x2, starting transfers between devices, other_core(): return lax.ppermute(value, 'expert', [(i, i ^ 1) for i in range(2 * RING)])  17.5 us
    ppermute x6, waiting for transfers between devices, along_x(): return lax.ppermute(value, 'expert', pairs)  9.74 us
    ppermute x6, starting transfers between devices, along_x(): return lax.ppermute(value, 'expert', pairs)  8.64 us
    dot_general x4, matrix products, product(): jnp.dot(jnp.concatenate(value, axis=0), down, preferred_element_type=jnp....  6.29 us
    dot_general x3, matrix products, per_device(): upper = jnp.dot(value, up_local, preferred_element_type=jnp.float32)  5.43 us
    dot_general x3, matrix products, per_device(): gate = jnp.dot(value, gate_local, preferred_element_type=jnp.float32)  5.33 us
  transfers between devices with their start and end apart: 44, of which 19 were waited for; matrix products, arithmetic and copies ran while one was open for 7% of the time, Pallas kernels for 0%

commit v1 on v0

--- a/solution.py
+++ b/solution.py
@@ -126,12 +126,16 @@
     half = own.shape[1] // 2
     below, above = shift(own, first, 1), shift(own, first, -1)
     across = [shift(below[:, :half], first, 1), shift(above[:, half:], first, -1)]
-    mine = jnp.concatenate([own, below, above, jnp.concatenate(across, axis=1)], axis=0)
-    mine = lax.optimization_barrier(mine)
-    rows = mine.shape[0] // 2
-    below, above = shift(mine, second, 1), shift(mine, second, -1)
-    far = [shift(below[:rows], second, 1), shift(above[rows:], second, -1)]
-    return [mine], [below, above], far
+    near = lax.optimization_barrier(jnp.concatenate([own, below, above], axis=0))
+    far = jnp.concatenate(across, axis=1)
+    rows = own.shape[0]
+    below = [shift(near, second, 1), shift(far, second, 1)]
+    above = [shift(near, second, -1), shift(far, second, -1)]
+    last = [
+        shift(below[0][: 2 * rows], second, 1),
+        shift(jnp.concatenate([above[0][2 * rows :], above[1]], axis=0), second, -1),
+    ]
+    return [near, far], below + above, last
 
 
 def add(*terms):
@@ -153,41 +157,36 @@
     def piece(value, base, count):
         return value[base * rows : (base + count) * rows]
 
-    early = product([middle[:, :, 1:].swapaxes(1, 2), start[:, 0, 3]])
+    early = product([middle[:, :, 1:].swapaxes(1, 2), start[:, 0, 2:]])
+    up_one = [shift(piece(early, 6 * i + 4, 2), orders[i][0], 1) for i in both]
     down_one = [
-        shift(jnp.concatenate([piece(early, 12 + i, 1), piece(early, 6 * i, 2)], axis=0), orders[i][0], -1)
+        shift(jnp.concatenate([piece(early, 13 + 2 * i, 1), piece(early, 6 * i, 2)], axis=0), orders[i][0], -1)
         for i in both
     ]
-    up_one = [shift(piece(early, 6 * i + 4, 2), orders[i][0], 1) for i in both]
-    late = product([end[:, 0, 1:], start[:, 0, 1:3]])
+    up_own = [shift(piece(early, 12 + 2 * i, 1), orders[i][0], 1) for i in both]
+    late = product([end[:, 0, 1:], start[:, 0, 1]])
     down_two = [shift(piece(late, 3 * i + 2, 1), orders[i][0], -1) for i in both]
-    up_two = [
-        shift(jnp.concatenate([piece(late, 7 + 2 * i, 1), piece(late, 3 * i + 1, 1)], axis=0), orders[i][0], 1)
-        for i in both
-    ]
     up_sum = [add(piece(early, 6 * i + 2, 2), up_one[i]) for i in both]
+    up_three = [shift(up_sum[i], orders[i][0], 1) for i in both]
+    up_two = [shift(piece(late, 3 * i + 1, 1), orders[i][0], 1) for i in both]
     down_sum = [
         jnp.concatenate(
-            [add(piece(late, 6 + 2 * i, 1), down_one[i][:rows]), add(piece(late, 3 * i, 1), down_two[i])], axis=0
+            [add(piece(late, 6 + i, 1), down_one[i][:rows]), add(piece(late, 3 * i, 1), down_two[i])], axis=0
         )
         for i in both
     ]
-    up_three = [shift(up_sum[i], orders[i][0], 1) for i in both]
     down_three = [shift(down_sum[i], orders[i][0], -1) for i in both]
     kept = [product([start[i, 0, 0], end[i, 0, 0], middle[i, :, 0]]) for i in both]
+    sides = []
+    for i in both:
+        inner = add(kept[i][2 * rows :], up_three[i], down_one[i][rows:])
+        sides.append((shift(inner[rows:], orders[i][1], 1), shift(inner[:rows], orders[i][1], -1)))
     results = []
     for i in both:
-        second = orders[i][1]
-        half = down.shape[1] // 2
-        outer = add(kept[i][: 2 * rows], up_two[i], down_three[i])
-        inner = add(kept[i][2 * rows :], up_three[i], down_one[i][rows:])
-        own, across = outer[:rows], outer[rows:]
-        below, above = inner[:rows], inner[rows:]
-        low = shift(across[:, :half], second, 1)
-        high = shift(across[:, half:], second, -1)
-        above = jnp.concatenate([add(above[:, :half], low), above[:, half:]], axis=1)
-        below = jnp.concatenate([below[:, :half], add(below[:, half:], high)], axis=1)
-        results.append(add(own, shift(above, second, 1), shift(below, second, -1)))
+        across = add(kept[i][rows : 2 * rows], up_two[i], down_three[i][rows:])
+        across = shift(across, orders[i][1], 2)
+        own = lax.optimization_barrier(add(kept[i][:rows], up_own[i], down_three[i][:rows]))
+        results.append(add(own, *sides[i], across))
     return results
 
 

time: 190 us -> 198 us (1.042)
  waiting for transfers between devices: 90.9 us -> 98.4 us
    ppermute x36 -> x40, waiting for transfers between devices: 78.6 us -> 89 us  [shift(): lax.ppermute(value, 'hidden', [(i, target(i)) for i in range(RING * RING)])]
    ppermute x6, waiting for transfers between devices: 9.74 us -> 6.7 us  [along_x(): return lax.ppermute(value, 'expert', pairs)]
    ppermute x2, starting transfers between devices: 17.5 us -> 20.1 us  [other_core(): return lax.ppermute(value, 'expert', [(i, i ^ 1) for i in range(2 * RING)])]
    ppermute x6, starting transfers between devices: 8.64 us -> 6.23 us  [along_x(): return lax.ppermute(value, 'expert', pairs)]
    unnamed x29 -> x35, local copies, waits for them, and re-layouts: 2.77 us -> 4.3 us
    ppermute x36 -> x40, starting transfers between devices: 43.5 us -> 42.3 us  [shift(): lax.ppermute(value, 'hidden', [(i, target(i)) for i in range(RING * RING)])]
  transfers between devices with their start and end apart: 44 -> 48, of which waited for: 19 -> 23; matrix products, arithmetic and copies ran while one was open for 7% -> 7% of each run, Pallas kernels for 0% -> 0%
where the time goes in v1:
time: 198 us; the launch traced here: 197 us
  waiting for transfers between devices  98.4 us (50%)
  starting transfers between devices  68.6 us (35%)
  matrix products  17.2 us (9%)
  local copies, waits for them, and re-layouts  5.27 us (3%)
  Pallas kernels  4.22 us (2%)
  other arithmetic  2.84 us (1%)
    ppermute x40, waiting for transfers between devices, shift(): lax.ppermute(value, 'hidden', [(i, target(i)) for i in range(RING * RING)])  89 us
    ppermute x40, starting transfers between devices, shift(): lax.ppermute(value, 'hidden', [(i, target(i)) for i in range(RING * RING)])  42.3 us
    ppermute x2, starting transfers between devices, other_core(): return lax.ppermute(value, 'expert', [(i, i ^ 1) for i in range(2 * RING)])  20.1 us
    ppermute x6, waiting for transfers between devices, along_x(): return lax.ppermute(value, 'expert', pairs)  6.7 us
    dot_general x4, matrix products, product(): jnp.dot(jnp.concatenate(value, axis=0), down, preferred_element_type=jnp....  6.49 us
    ppermute x6, starting transfers between devices, along_x(): return lax.ppermute(value, 'expert', pairs)  6.23 us
    dot_general x3, matrix products, per_device(): upper = jnp.dot(value, up_local, preferred_element_type=jnp.float32)  5.41 us
    dot_general x3, matrix products, per_device(): gate = jnp.dot(value, gate_local, preferred_element_type=jnp.float32)  5.34 us
  transfers between devices with their start and end apart: 48, of which 23 were waited for; matrix products, arithmetic and copies ran while one was open for 7% of the time, Pallas kernels for 0%

profile of v1, /device:TPU:1, one launch (start us, length us, event | category | flops | bytes accessed | tf_op | source)
XLA Modules:
  0.0 197.3 jit_solution(2158314710804281522)
XLA Ops:
  20.7 3.0 %collective-permute-done.2 = bf16[24,6144]{1,0:T(8,128)(2,1)S(1)} collective-permute-done((bf16[24,6144]{1,0:T(8,128)(2,1)S(1)}, bf16[24,6144]{1,0:T(8,128)(2,1)S(1)}, u32[]{:S(2)}, u32[]{:S(2)}) %collective-permute-start.2) | collective-permute-done | bytes 294944 | tf_op jit(solution)/shard_map/ppermute | solution.py:122
  23.7 2.8 %collective-permute-start.14 = (bf16[72,6144]{1,0:T(8,128)(2,1)S(1)}, bf16[72,6144]{1,0:T(8,128)(2,1)S(1)}, u32[]{:S(2)}, u32[]{:S(2)}) collective-permute-start(bf16[72,6144]{1,0:T(8,128)(2,1)S(1)} %pad_maximum_fusion.1), channel_id=1, source_target_pairs={{0,3},{1,0},{2,1},{3,2},{4,7},{5,4},{6,5},{7,6},{8,11},{9,8},{10,9... | collective-permute-start | bytes 2654216 | tf_op jit(solution)/shard_map/ppermute | solution.py:122
  31.9 18.2 %collective-permute-done.10 = bf16[24,3072]{1,0:T(8,128)(2,1)S(1)} collective-permute-done((bf16[24,3072]{1,0:T(8,128)(2,1)S(1)}, bf16[24,3072]{1,0:T(8,128)(2,1)S(1)}, u32[]{:S(2)}, u32[]{:S(2)}) %collective-permute-start.10) | collective-permute-done | bytes 147488 | tf_op jit(solution)/shard_map/ppermute | solution.py:122
  56.0 2.3 %collective-permute-done.11 = bf16[24,3072]{1,0:T(8,128)(2,1)S(1)} collective-permute-done((bf16[24,3072]{1,0:T(8,128)(2,1)S(1)}, bf16[24,3072]{1,0:T(8,128)(2,1)S(1)}, u32[]{:S(2)}, u32[]{:S(2)}) %collective-permute-start.11) | collective-permute-done | bytes 147488 | tf_op jit(solution)/shard_map/ppermute | solution.py:122
  58.3 2.9 %collective-permute-start.15 = (bf16[24,6144]{1,0:T(8,128)(2,1)S(1)}, bf16[24,6144]{1,0:T(8,128)(2,1)S(1)}, u32[]{:S(2)}, u32[]{:S(2)}) collective-permute-start(bf16[24,6144]{1,0:T(8,128)(2,1)S(1)} %constant_dynamic-update-slice_fusion), channel_id=1, source_target_pairs={{0,3},{1,0},{2,1},{3,2},{4,7},{5,4},{6,5},{7,6},{8,11},{9,8},{10,9... | collective-permute-start | bytes 884744 | tf_op jit(solution)/shard_map/ppermute | solution.py:122
  65.7 6.7 %collective-permute-done.22 = bf16[24,6144]{1,0:T(8,128)(2,1)S(1)} collective-permute-done((bf16[24,6144]{1,0:T(8,128)(2,1)S(1)}, bf16[24,6144]{1,0:T(8,128)(2,1)S(1)}, u32[]{:S(2)}, u32[]{:S(2)}) %collective-permute-start.22) | collective-permute-done | bytes 294944 | tf_op jit(solution)/shard_map/ppermute | solution.py:122
  72.4 3.1 %collective-permute-start.20 = (bf16[24,6144]{1,0:T(8,128)(2,1)S(1)}, bf16[24,6144]{1,0:T(8,128)(2,1)S(1)}, u32[]{:S(2)}, u32[]{:S(2)}) collective-permute-start(bf16[24,6144]{1,0:T(8,128)(2,1)S(1)} %constant_dynamic-update-slice_fusion.2), channel_id=1, source_target_pairs={{0,12},{1,13},{2,14},{3,15},{4,0},{5,1},{6,2},{7,3},{8,4},{9,5},{1... | collective-permute-start | bytes 884744 | tf_op jit(solution)/shard_map/ppermute | solution.py:122
  75.9 6.6 %collective-permute-done.23 = bf16[24,6144]{1,0:T(8,128)(2,1)S(1)} collective-permute-done((bf16[24,6144]{1,0:T(8,128)(2,1)S(1)}, bf16[24,6144]{1,0:T(8,128)(2,1)S(1)}, u32[]{:S(2)}, u32[]{:S(2)}) %collective-permute-start.23) | collective-permute-done | bytes 294944 | tf_op jit(solution)/shard_map/ppermute | solution.py:122
  82.7 2.6 %fusion.10 = f32[384,512]{1,0:T(8,128)S(1)} fusion(bf16[384,6144]{1,0:T(8,128)(2,1)S(1)} %constant_dynamic-update-slice_fusion.8, bf16[1,6144,512]{2,1,0:T(8,128)(2,1)S(1)} %copy-done.6), kind=kOutput, calls=%fused_computation.14 | convolution fusion | flops 2415919104 | bytes 11796480 | tf_op jit(solution)/shard_map/dot_general | solution.py:238
  85.3 2.6 %multiply_convert_fusion = bf16[384,512]{1,0:T(8,128)(2,1)S(1)} fusion(f32[384,512]{1,0:T(8,128)S(1)} %fusion.10, bf16[384,6144]{1,0:T(8,128)(2,1)S(1)} %constant_dynamic-update-slice_fusion.8, bf16[1,6144,512]{2,1,0:T(8,128)(2,1)S(1)} %bitcast.91), kind=kOutput, calls=%fused_computation.29 | convolution fusion | flops 2417098752 | bytes 12189696 | tf_op jit(solution)/shard_map/dot_general | solution.py:239
  88.0 2.8 %convolution_convert_fusion = bf16[384,6144]{1,0:T(8,128)(2,1)S(1)} fusion(bf16[1,512,6144]{2,1,0:T(8,128)(2,1)S(1)} %bitcast.76, bf16[96,512]{1,0:T(8,128)(2,1)S(1)} %bitcast.88, bf16[288,512]{1,0:T(8,128)(2,1)S(1)} %bitcast.79), kind=kOutput, calls=%fused_computation | convolution fusion | flops 2419064832 | bytes 11403264 | tf_op jit(solution)/shard_map/dot_general | solution.py:154
  93.1 2.7 %collective-permute-start.21 = (bf16[48,6144]{1,0:T(8,128)(2,1)S(1)}, bf16[48,6144]{1,0:T(8,128)(2,1)S(1)}, u32[]{:S(2)}, u32[]{:S(2)}) collective-permute-start(bf16[48,6144]{1,0:T(8,128)(2,1)S(1)} %pad_maximum_fusion.6), channel_id=1, source_target_pairs={{0,12},{1,13},{2,14},{3,15},{4,0},{5,1},{6,2},{7,3},{8,4},{9,5},{1... | collective-permute-start | bytes 1769480 | tf_op jit(solution)/shard_map/ppermute | solution.py:122
  95.9 5.4 %collective-permute-done.13 = bf16[48,6144]{1,0:T(8,128)(2,1)S(1)} collective-permute-done((bf16[48,6144]{1,0:T(8,128)(2,1)S(1)}, bf16[48,6144]{1,0:T(8,128)(2,1)S(1)}, u32[]{:S(2)}, u32[]{:S(2)}) %collective-permute-start.13) | collective-permute-done | bytes 589856 | tf_op jit(solution)/shard_map/ppermute | solution.py:122
  110.2 3.8 %collective-permute-done.28 = bf16[48,6144]{1,0:T(8,128)(2,1)S(1)} collective-permute-done((bf16[48,6144]{1,0:T(8,128)(2,1)S(1)}, bf16[48,6144]{1,0:T(8,128)(2,1)S(1)}, u32[]{:S(2)}, u32[]{:S(2)}) %collective-permute-start.28) | collective-permute-done | bytes 589856 | tf_op jit(solution)/shard_map/ppermute | solution.py:122
  118.5 4.8 %collective-permute-done.25 = bf16[72,6144]{1,0:T(8,128)(2,1)S(1)} collective-permute-done((bf16[72,6144]{1,0:T(8,128)(2,1)S(1)}, bf16[72,6144]{1,0:T(8,128)(2,1)S(1)}, u32[]{:S(2)}, u32[]{:S(2)}) %collective-permute-start.25) | collective-permute-done | bytes 884768 | tf_op jit(solution)/shard_map/ppermute | solution.py:122
  123.3 6.3 %collective-permute-done.26 = bf16[24,6144]{1,0:T(8,128)(2,1)S(1)} collective-permute-done((bf16[24,6144]{1,0:T(8,128)(2,1)S(1)}, bf16[24,6144]{1,0:T(8,128)(2,1)S(1)}, u32[]{:S(2)}, u32[]{:S(2)}) %collective-permute-start.26) | collective-permute-done | bytes 294944 | tf_op jit(solution)/shard_map/ppermute | solution.py:122
  130.0 4.3 %collective-permute-done.39 = bf16[48,6144]{1,0:T(8,128)(2,1)S(1)} collective-permute-done((bf16[48,6144]{1,0:T(8,128)(2,1)S(1)}, bf16[48,6144]{1,0:T(8,128)(2,1)S(1)}, u32[]{:S(2)}, u32[]{:S(2)}) %collective-permute-start.39) | collective-permute-done | bytes 589856 | tf_op jit(solution)/shard_map/ppermute | solution.py:122
  134.6 10.4 %collective-permute-done.29 = bf16[48,6144]{1,0:T(8,128)(2,1)S(1)} collective-permute-done((bf16[48,6144]{1,0:T(8,128)(2,1)S(1)}, bf16[48,6144]{1,0:T(8,128)(2,1)S(1)}, u32[]{:S(2)}, u32[]{:S(2)}) %collective-permute-start.29) | collective-permute-done | bytes 589856 | tf_op jit(solution)/shard_map/ppermute | solution.py:122
  145.0 3.3 %collective-permute-start.37 = (bf16[48,6144]{1,0:T(8,128)(2,1)S(1)}, bf16[48,6144]{1,0:T(8,128)(2,1)S(1)}, u32[]{:S(2)}, u32[]{:S(2)}) collective-permute-start(bf16[48,6144]{1,0:T(8,128)(2,1)S(1)} %pad_maximum_fusion.8), channel_id=1, source_target_pairs={{0,3},{1,0},{2,1},{3,2},{4,7},{5,4},{6,5},{7,6},{8,11},{9,8},{10,9... | collective-permute-start | bytes 1769480 | tf_op jit(solution)/shard_map/ppermute | solution.py:122
  150.1 5.0 %collective-permute-done.37 = bf16[48,6144]{1,0:T(8,128)(2,1)S(1)} collective-permute-done((bf16[48,6144]{1,0:T(8,128)(2,1)S(1)}, bf16[48,6144]{1,0:T(8,128)(2,1)S(1)}, u32[]{:S(2)}, u32[]{:S(2)}) %collective-permute-start.37) | collective-permute-done | bytes 589856 | tf_op jit(solution)/shard_map/ppermute | solution.py:122
  155.4 3.5 %collective-permute-start.31 = (bf16[24,6144]{1,0:T(8,128)(2,1)S(1)}, bf16[24,6144]{1,0:T(8,128)(2,1)S(1)}, u32[]{:S(2)}, u32[]{:S(2)}) collective-permute-start(bf16[24,6144]{1,0:T(8,128)(2,1)S(1)} %get-tuple-element.36), channel_id=1, source_target_pairs={{0,3},{1,0},{2,1},{3,2},{4,7},{5,4},{6,5},{7,6},{8,11},{9,8},{10,9... | collective-permute-start | bytes 884744 | tf_op jit(solution)/shard_map/ppermute | solution.py:122
  161.0 6.5 %collective-permute-done.43 = bf16[24,6144]{1,0:T(8,128)(2,1)S(1)} collective-permute-done((bf16[24,6144]{1,0:T(8,128)(2,1)S(1)}, bf16[24,6144]{1,0:T(8,128)(2,1)S(1)}, u32[]{:S(2)}, u32[]{:S(2)}) %collective-permute-start.43) | collective-permute-done | bytes 294944 | tf_op jit(solution)/shard_map/ppermute | solution.py:122
  169.9 3.5 %collective-permute-done.46.across_ref = bf16[24,3072]{1,0:T(8,128)(2,1)S(1)} collective-permute-done((bf16[24,3072]{1,0:T(8,128)(2,1)S(1)}, bf16[24,3072]{1,0:T(8,128)(2,1)S(1)}, u32[]{:S(2)}, u32[]{:S(2)}) %collective-permute-start.46) | collective-permute-done | bytes 147488 | tf_op jit(solution)/shard_map/ppermute | solution.py:110
  175.0 18.6 %collective-permute-start.47 = (bf16[96,3072]{1,0:T(8,128)(2,1)S(1)}, bf16[96,3072]{1,0:T(8,128)(2,1)S(1)}, u32[]{:S(2)}, u32[]{:S(2)}) collective-permute-start(bf16[96,3072]{1,0:T(8,128)(2,1)S(1)} %pad_maximum_fusion.9), channel_id=1, source_target_pairs={{0,16},{16,0},{32,48},{48,32},{64,80},{80,64},{96,112},{112,96},{1... | collective-permute-start | bytes 1769480 | tf_op jit(solution)/shard_map/ppermute | solution.py:114
  (181 shorter events, 64.7 us)
Async XLA Ops:
  23.7 51.7 %collective-permute-start.14 = (bf16[72,6144]{1,0:T(8,128)(2,1)S(1)}, bf16[72,6144]{1,0:T(8,128)(2,1)S(1)}, u32[]{:S(2)}, u32[]{:S(2)}) collective-permute-start(bf16[72,6144]{1,0:T(8,128)(2,1)S(1)} %pad_maximum_fusion.1), channel_id=1, source_target_pairs={{0,3},{1,0},{2,1},{3,2},{4,7},{5,4},{6,5},{7,6},{8,11},{9,8},{10,9... | collective-permute-start | bytes 2654216 | tf_op jit(solution)/shard_map/ppermute | solution.py:122
  26.5 38.9 %collective-permute-start.12 = (bf16[72,6144]{1,0:T(8,128)(2,1)S(1)}, bf16[72,6144]{1,0:T(8,128)(2,1)S(1)}, u32[]{:S(2)}, u32[]{:S(2)}) collective-permute-start(bf16[72,6144]{1,0:T(8,128)(2,1)S(1)} %pad_maximum_fusion.1), channel_id=1, source_target_pairs={{0,1},{1,2},{2,3},{3,0},{4,5},{5,6},{6,7},{7,4},{8,9},{9,10},{10,1... | collective-permute-start | bytes 2654216 | tf_op jit(solution)/shard_map/ppermute | solution.py:122
  27.1 48.7 %collective-permute-start.17 = (bf16[72,6144]{1,0:T(8,128)(2,1)S(1)}, bf16[72,6144]{1,0:T(8,128)(2,1)S(1)}, u32[]{:S(2)}, u32[]{:S(2)}) collective-permute-start(bf16[72,6144]{1,0:T(8,128)(2,1)S(1)} %pad_maximum_fusion.2), channel_id=1, source_target_pairs={{0,4},{1,5},{2,6},{3,7},{4,8},{5,9},{6,10},{7,11},{8,12},{9,13},{1... | collective-permute-start | bytes 2654216 | tf_op jit(solution)/shard_map/ppermute | solution.py:122
  28.5 54.0 %collective-permute-start.19 = (bf16[72,6144]{1,0:T(8,128)(2,1)S(1)}, bf16[72,6144]{1,0:T(8,128)(2,1)S(1)}, u32[]{:S(2)}, u32[]{:S(2)}) collective-permute-start(bf16[72,6144]{1,0:T(8,128)(2,1)S(1)} %pad_maximum_fusion.2), channel_id=1, source_target_pairs={{0,12},{1,13},{2,14},{3,15},{4,0},{5,1},{6,2},{7,3},{8,4},{9,5},{1... | collective-permute-start | bytes 2654216 | tf_op jit(solution)/shard_map/ppermute | solution.py:122
  31.8 18.2 %collective-permute-start.10 = (bf16[24,3072]{1,0:T(8,128)(2,1)S(1)}, bf16[24,3072]{1,0:T(8,128)(2,1)S(1)}, u32[]{:S(2)}, u32[]{:S(2)}) collective-permute-start(bf16[24,3072]{1,0:T(8,128)(2,1)S(1)} %slice.358), channel_id=1, source_target_pairs={{0,1},{1,2},{2,3},{3,0},{4,5},{5,6},{6,7},{7,4},{8,9},{9,10},{10,1... | collective-permute-start | bytes 442376 | tf_op jit(solution)/shard_map/ppermute | solution.py:122
  58.3 17.5 %collective-permute-start.15 = (bf16[24,6144]{1,0:T(8,128)(2,1)S(1)}, bf16[24,6144]{1,0:T(8,128)(2,1)S(1)}, u32[]{:S(2)}, u32[]{:S(2)}) collective-permute-start(bf16[24,6144]{1,0:T(8,128)(2,1)S(1)} %constant_dynamic-update-slice_fusion), channel_id=1, source_target_pairs={{0,3},{1,0},{2,1},{3,2},{4,7},{5,4},{6,5},{7,6},{8,11},{9,8},{10,9... | collective-permute-start | bytes 884744 | tf_op jit(solution)/shard_map/ppermute | solution.py:122
  91.2 10.7 %collective-permute-start.16 = (bf16[48,6144]{1,0:T(8,128)(2,1)S(1)}, bf16[48,6144]{1,0:T(8,128)(2,1)S(1)}, u32[]{:S(2)}, u32[]{:S(2)}) collective-permute-start(bf16[48,6144]{1,0:T(8,128)(2,1)S(1)} %pad_maximum_fusion.5), channel_id=1, source_target_pairs={{0,3},{1,0},{2,1},{3,2},{4,7},{5,4},{6,5},{7,6},{8,11},{9,8},{10,9... | collective-permute-start | bytes 1769480 | tf_op jit(solution)/shard_map/ppermute | solution.py:122
  92.9 11.3 %collective-permute-start.18 = (bf16[48,6144]{1,0:T(8,128)(2,1)S(1)}, bf16[48,6144]{1,0:T(8,128)(2,1)S(1)}, u32[]{:S(2)}, u32[]{:S(2)}) collective-permute-start(bf16[48,6144]{1,0:T(8,128)(2,1)S(1)} %slice.363), channel_id=1, source_target_pairs={{0,4},{1,5},{2,6},{3,7},{4,8},{5,9},{6,10},{7,11},{8,12},{9,13},{1... | collective-permute-start | bytes 1769480 | tf_op jit(solution)/shard_map/ppermute | solution.py:122
  93.1 11.3 %collective-permute-start.21 = (bf16[48,6144]{1,0:T(8,128)(2,1)S(1)}, bf16[48,6144]{1,0:T(8,128)(2,1)S(1)}, u32[]{:S(2)}, u32[]{:S(2)}) collective-permute-start(bf16[48,6144]{1,0:T(8,128)(2,1)S(1)} %pad_maximum_fusion.6), channel_id=1, source_target_pairs={{0,12},{1,13},{2,14},{3,15},{4,0},{5,1},{6,2},{7,3},{8,4},{9,5},{1... | collective-permute-start | bytes 1769480 | tf_op jit(solution)/shard_map/ppermute | solution.py:122
  95.8 18.2 %collective-permute-start.28 = (bf16[48,6144]{1,0:T(8,128)(2,1)S(1)}, bf16[48,6144]{1,0:T(8,128)(2,1)S(1)}, u32[]{:S(2)}, u32[]{:S(2)}) collective-permute-start(bf16[48,6144]{1,0:T(8,128)(2,1)S(1)} %get-tuple-element.19), channel_id=1, source_target_pairs={{0,4},{1,5},{2,6},{3,7},{4,8},{5,9},{6,10},{7,11},{8,12},{9,13},{1... | collective-permute-start | bytes 1769480 | tf_op jit(solution)/shard_map/ppermute | solution.py:122
  101.4 14.3 %collective-permute-start.38 = (bf16[48,6144]{1,0:T(8,128)(2,1)S(1)}, bf16[48,6144]{1,0:T(8,128)(2,1)S(1)}, u32[]{:S(2)}, u32[]{:S(2)}) collective-permute-start(bf16[48,6144]{1,0:T(8,128)(2,1)S(1)} %get-tuple-element.17), channel_id=1, source_target_pairs={{0,1},{1,2},{2,3},{3,0},{4,5},{5,6},{6,7},{7,4},{8,9},{9,10},{10,1... | collective-permute-start | bytes 1769480 | tf_op jit(solution)/shard_map/ppermute | solution.py:122
  102.0 15.5 %collective-permute-start.35 = (bf16[72,6144]{1,0:T(8,128)(2,1)S(1)}, bf16[72,6144]{1,0:T(8,128)(2,1)S(1)}, u32[]{:S(2)}, u32[]{:S(2)}) collective-permute-start(bf16[72,6144]{1,0:T(8,128)(2,1)S(1)} %pad_maximum_fusion.4), channel_id=1, source_target_pairs={{0,3},{1,0},{2,1},{3,2},{4,7},{5,4},{6,5},{7,6},{8,11},{9,8},{10,9... | collective-permute-start | bytes 2654216 | tf_op jit(solution)/shard_map/ppermute | solution.py:122
  104.2 19.1 %collective-permute-start.25 = (bf16[72,6144]{1,0:T(8,128)(2,1)S(1)}, bf16[72,6144]{1,0:T(8,128)(2,1)S(1)}, u32[]{:S(2)}, u32[]{:S(2)}) collective-permute-start(bf16[72,6144]{1,0:T(8,128)(2,1)S(1)} %pad_maximum_fusion.3), channel_id=1, source_target_pairs={{0,12},{1,13},{2,14},{3,15},{4,0},{5,1},{6,2},{7,3},{8,4},{9,5},{1... | collective-permute-start | bytes 2654216 | tf_op jit(solution)/shard_map/ppermute | solution.py:122
  104.4 44.2 %collective-permute-start.34 = (bf16[24,6144]{1,0:T(8,128)(2,1)S(1)}, bf16[24,6144]{1,0:T(8,128)(2,1)S(1)}, u32[]{:S(2)}, u32[]{:S(2)}) collective-permute-start(bf16[24,6144]{1,0:T(8,128)(2,1)S(1)} %get-tuple-element.11), channel_id=1, source_target_pairs={{0,1},{1,2},{2,3},{3,0},{4,5},{5,6},{6,7},{7,4},{8,9},{9,10},{10,1... | collective-permute-start | bytes 884744 | tf_op jit(solution)/shard_map/ppermute | solution.py:122
  114.0 15.6 %collective-permute-start.26 = (bf16[24,6144]{1,0:T(8,128)(2,1)S(1)}, bf16[24,6144]{1,0:T(8,128)(2,1)S(1)}, u32[]{:S(2)}, u32[]{:S(2)}) collective-permute-start(bf16[24,6144]{1,0:T(8,128)(2,1)S(1)} %get-tuple-element.28), channel_id=1, source_target_pairs={{0,12},{1,13},{2,14},{3,15},{4,0},{5,1},{6,2},{7,3},{8,4},{9,5},{1... | collective-permute-start | bytes 884744 | tf_op jit(solution)/shard_map/ppermute | solution.py:122
  115.6 14.0 %collective-permute-start.36 = (bf16[24,6144]{1,0:T(8,128)(2,1)S(1)}, bf16[24,6144]{1,0:T(8,128)(2,1)S(1)}, u32[]{:S(2)}, u32[]{:S(2)}) collective-permute-start(bf16[24,6144]{1,0:T(8,128)(2,1)S(1)} %get-tuple-element.25), channel_id=1, source_target_pairs={{0,3},{1,0},{2,1},{3,2},{4,7},{5,4},{6,5},{7,6},{8,11},{9,8},{10,9... | collective-permute-start | bytes 884744 | tf_op jit(solution)/shard_map/ppermute | solution.py:122
  117.5 37.9 %collective-permute-start.24 = (bf16[24,6144]{1,0:T(8,128)(2,1)S(1)}, bf16[24,6144]{1,0:T(8,128)(2,1)S(1)}, u32[]{:S(2)}, u32[]{:S(2)}) collective-permute-start(bf16[24,6144]{1,0:T(8,128)(2,1)S(1)} %get-tuple-element.14), channel_id=1, source_target_pairs={{0,4},{1,5},{2,6},{3,7},{4,8},{5,9},{6,10},{7,11},{8,12},{9,13},{1... | collective-permute-start | bytes 884744 | tf_op jit(solution)/shard_map/ppermute | solution.py:122
  123.3 11.0 %collective-permute-start.39 = (bf16[48,6144]{1,0:T(8,128)(2,1)S(1)}, bf16[48,6144]{1,0:T(8,128)(2,1)S(1)}, u32[]{:S(2)}, u32[]{:S(2)}) collective-permute-start(bf16[48,6144]{1,0:T(8,128)(2,1)S(1)} %get-tuple-element.15), channel_id=1, source_target_pairs={{0,1},{1,2},{2,3},{3,0},{4,5},{5,6},{6,7},{7,4},{8,9},{9,10},{10,1... | collective-permute-start | bytes 1769480 | tf_op jit(solution)/shard_map/ppermute | solution.py:122
  129.6 19.0 %collective-permute-start.42 = (bf16[24,6144]{1,0:T(8,128)(2,1)S(1)}, bf16[24,6144]{1,0:T(8,128)(2,1)S(1)}, u32[]{:S(2)}, u32[]{:S(2)}) collective-permute-start(bf16[24,6144]{1,0:T(8,128)(2,1)S(1)} %get-tuple-element.26), channel_id=1, source_target_pairs={{0,1},{1,2},{2,3},{3,0},{4,5},{5,6},{6,7},{7,4},{8,9},{9,10},{10,1... | collective-permute-start | bytes 884744 | tf_op jit(solution)/shard_map/ppermute | solution.py:122
  129.6 15.4 %collective-permute-start.29 = (bf16[48,6144]{1,0:T(8,128)(2,1)S(1)}, bf16[48,6144]{1,0:T(8,128)(2,1)S(1)}, u32[]{:S(2)}, u32[]{:S(2)}) collective-permute-start(bf16[48,6144]{1,0:T(8,128)(2,1)S(1)} %get-tuple-element.16), channel_id=1, source_target_pairs={{0,4},{1,5},{2,6},{3,7},{4,8},{5,9},{6,10},{7,11},{8,12},{9,13},{1... | collective-permute-start | bytes 1769480 | tf_op jit(solution)/shard_map/ppermute | solution.py:122
  134.3 21.1 %collective-permute-start.32 = (bf16[24,6144]{1,0:T(8,128)(2,1)S(1)}, bf16[24,6144]{1,0:T(8,128)(2,1)S(1)}, u32[]{:S(2)}, u32[]{:S(2)}) collective-permute-start(bf16[24,6144]{1,0:T(8,128)(2,1)S(1)} %get-tuple-element.27), channel_id=1, source_target_pairs={{0,4},{1,5},{2,6},{3,7},{4,8},{5,9},{6,10},{7,11},{8,12},{9,13},{1... | collective-permute-start | bytes 884744 | tf_op jit(solution)/shard_map/ppermute | solution.py:122
  155.3 12.6 %collective-permute-start.30 = (bf16[24,6144]{1,0:T(8,128)(2,1)S(1)}, bf16[24,6144]{1,0:T(8,128)(2,1)S(1)}, u32[]{:S(2)}, u32[]{:S(2)}) collective-permute-start(bf16[24,6144]{1,0:T(8,128)(2,1)S(1)} %get-tuple-element.35), channel_id=1, source_target_pairs={{0,1},{1,2},{2,3},{3,0},{4,5},{5,6},{6,7},{7,4},{8,9},{9,10},{10,1... | collective-permute-start | bytes 884744 | tf_op jit(solution)/shard_map/ppermute | solution.py:122
  155.4 12.5 %collective-permute-start.31 = (bf16[24,6144]{1,0:T(8,128)(2,1)S(1)}, bf16[24,6144]{1,0:T(8,128)(2,1)S(1)}, u32[]{:S(2)}, u32[]{:S(2)}) collective-permute-start(bf16[24,6144]{1,0:T(8,128)(2,1)S(1)} %get-tuple-element.36), channel_id=1, source_target_pairs={{0,3},{1,0},{2,1},{3,2},{4,7},{5,4},{6,5},{7,6},{8,11},{9,8},{10,9... | collective-permute-start | bytes 884744 | tf_op jit(solution)/shard_map/ppermute | solution.py:122
  175.0 20.2 %collective-permute-start.47 = (bf16[96,3072]{1,0:T(8,128)(2,1)S(1)}, bf16[96,3072]{1,0:T(8,128)(2,1)S(1)}, u32[]{:S(2)}, u32[]{:S(2)}) collective-permute-start(bf16[96,3072]{1,0:T(8,128)(2,1)S(1)} %pad_maximum_fusion.9), channel_id=1, source_target_pairs={{0,16},{16,0},{32,48},{48,32},{64,80},{80,64},{96,112},{112,96},{1... | collective-permute-start | bytes 1769480 | tf_op jit(solution)/shard_map/ppermute | solution.py:114
  (35 other events, 317.9 us)

commit v2 on v1

--- a/solution.py
+++ b/solution.py
@@ -37,7 +37,15 @@
     return found
 
 
-def route_kernel(hidden_ref, gain_ref, ids_ref, same_ref, other_ref, normed_ref):
+def route_kernel(
+    hidden_hbm, gain_hbm, ids_hbm, same_ref, other_ref, normed_ref, hidden_ref, gain_ref, ids_ref, sems
+):
+    pairs = ((hidden_hbm, hidden_ref), (gain_hbm, gain_ref), (ids_hbm, ids_ref))
+    copies = [pltpu.make_async_copy(source, target, sems.at[i]) for i, (source, target) in enumerate(pairs)]
+    for copy in copies:
+        copy.start()
+    for copy in copies:
+        copy.wait()
     count, capacity, width = same_ref.shape
     tokens = hidden_ref.shape[0]
     values = hidden_ref[...].astype(jnp.float32)
@@ -129,8 +137,9 @@
     near = lax.optimization_barrier(jnp.concatenate([own, below, above], axis=0))
     far = jnp.concatenate(across, axis=1)
     rows = own.shape[0]
-    below = [shift(near, second, 1), shift(far, second, 1)]
-    above = [shift(near, second, -1), shift(far, second, -1)]
+    below, above = [shift(near, second, 1)], [shift(near, second, -1)]
+    below.append(shift(far, second, 1))
+    above.append(shift(far, second, -1))
     last = [
         shift(below[0][: 2 * rows], second, 1),
         shift(jnp.concatenate([above[0][2 * rows :], above[1]], axis=0), second, -1),
@@ -212,9 +221,16 @@
     same, other, normed = pl.pallas_call(
         route_kernel,
         out_shape=(piece, piece, jax.ShapeDtypeStruct((tok_rows, width), jnp.bfloat16)),
+        in_specs=[pl.BlockSpec(memory_space=pltpu.HBM)] * 3,
+        scratch_shapes=[
+            pltpu.VMEM((tok_rows, width), jnp.bfloat16),
+            pltpu.VMEM((1, width), jnp.float32),
+            pltpu.VMEM((top_count, tok_rows), jnp.int32),
+            pltpu.SemaphoreType.DMA((3,)),
+        ],
         compiler_params=pltpu.CompilerParams(vmem_limit_bytes=8 * 1024 * 1024),
         name="route",
-    )(hidden_in, norm_gain.reshape(1, width), ids)
+    )(*[pltpu.with_memory_space_constraint(x, pltpu.HBM) for x in (hidden_in, norm_gain.reshape(1, width), ids)])
     weights = pl.pallas_call(
         functools.partial(gate_kernel, capacity),
         out_shape=jax.ShapeDtypeStruct((2, 3, 8 * RING * capacity, tok_rows), jnp.bfloat16),

time: 198 us -> 196 us (0.990)
  local copies, waits for them, and re-layouts: 5.27 us -> 2.93 us
    unnamed x35 -> x29, local copies, waits for them, and re-layouts: 4.3 us -> 1.96 us
where the time goes in v2:
time: 196 us
  waiting for transfers between devices  98.4 us (50%)
  starting transfers between devices  68.6 us (35%)
  matrix products  17.2 us (9%)
  Pallas kernels  5.18 us (3%)
  local copies, waits for them, and re-layouts  2.93 us (1%)
  other arithmetic  2.84 us (1%)
    ppermute x40, waiting for transfers between devices, shift(): lax.ppermute(value, 'hidden', [(i, target(i)) for i in range(RING * RING)])  89 us
    ppermute x40, starting transfers between devices, shift(): lax.ppermute(value, 'hidden', [(i, target(i)) for i in range(RING * RING)])  42.3 us
    ppermute x2, starting transfers between devices, other_core(): return lax.ppermute(value, 'expert', [(i, i ^ 1) for i in range(2 * RING)])  20.1 us
    ppermute x6, waiting for transfers between devices, along_x(): return lax.ppermute(value, 'expert', pairs)  6.69 us
    dot_general x4, matrix products, product(): jnp.dot(jnp.concatenate(value, axis=0), down, preferred_element_type=jnp....  6.49 us
    ppermute x6, starting transfers between devices, along_x(): return lax.ppermute(value, 'expert', pairs)  6.23 us
    dot_general x3, matrix products, per_device(): upper = jnp.dot(value, up_local, preferred_element_type=jnp.float32)  5.41 us
    dot_general x3, matrix products, per_device(): gate = jnp.dot(value, gate_local, preferred_element_type=jnp.float32)  5.34 us
  transfers between devices with their start and end apart: 48, of which 23 were waited for; matrix products, arithmetic and copies ran while one was open for 7% of the time, Pallas kernels for 0%

profile of v2, /device:TPU:1, one launch (start us, length us, event | category | flops | bytes accessed | tf_op | source)
XLA Modules:
  0.0 196.0 jit_solution(10979210534933541197)
XLA Ops:
  0.0 2.8 %route.1 = (bf16[4,6,6144]{2,1,0:T(8,128)(2,1)S(1)}, bf16[4,6,6144]{2,1,0:T(8,128)(2,1)S(1)}, bf16[16,6144]{1,0:T(8,128)(2,1)S(1)}) custom-call(bf16[16,6144]{1,0:T(8,128)(2,1)} %hidden_ref.1, f32[1,6144]{1,0:T(1,128)} %bitcast.89, s32[2,16]{1,0:T(2,128)} %bitcast.72), custom_call_target="tpu_custom_call" | custom-call | tf_op jit(solution)/shard_map/route/pallas_call | solution.py:221
  19.3 3.0 %collective-permute-done.2 = bf16[24,6144]{1,0:T(8,128)(2,1)S(1)} collective-permute-done((bf16[24,6144]{1,0:T(8,128)(2,1)S(1)}, bf16[24,6144]{1,0:T(8,128)(2,1)S(1)}, u32[]{:S(2)}, u32[]{:S(2)}) %collective-permute-start.2) | collective-permute-done | bytes 294944 | tf_op jit(solution)/shard_map/ppermute | solution.py:130
  22.4 2.8 %collective-permute-start.14 = (bf16[72,6144]{1,0:T(8,128)(2,1)S(1)}, bf16[72,6144]{1,0:T(8,128)(2,1)S(1)}, u32[]{:S(2)}, u32[]{:S(2)}) collective-permute-start(bf16[72,6144]{1,0:T(8,128)(2,1)S(1)} %pad_maximum_fusion.1), channel_id=1, source_target_pairs={{0,3},{1,0},{2,1},{3,2},{4,7},{5,4},{6,5},{7,6},{8,11},{9,8},{10,9... | collective-permute-start | bytes 2654216 | tf_op jit(solution)/shard_map/ppermute | solution.py:130
  30.5 18.2 %collective-permute-done.10 = bf16[24,3072]{1,0:T(8,128)(2,1)S(1)} collective-permute-done((bf16[24,3072]{1,0:T(8,128)(2,1)S(1)}, bf16[24,3072]{1,0:T(8,128)(2,1)S(1)}, u32[]{:S(2)}, u32[]{:S(2)}) %collective-permute-start.10) | collective-permute-done | bytes 147488 | tf_op jit(solution)/shard_map/ppermute | solution.py:130
  56.9 2.9 %collective-permute-start.15 = (bf16[24,6144]{1,0:T(8,128)(2,1)S(1)}, bf16[24,6144]{1,0:T(8,128)(2,1)S(1)}, u32[]{:S(2)}, u32[]{:S(2)}) collective-permute-start(bf16[24,6144]{1,0:T(8,128)(2,1)S(1)} %constant_dynamic-update-slice_fusion), channel_id=1, source_target_pairs={{0,3},{1,0},{2,1},{3,2},{4,7},{5,4},{6,5},{7,6},{8,11},{9,8},{10,9... | collective-permute-start | bytes 884744 | tf_op jit(solution)/shard_map/ppermute | solution.py:130
  64.3 6.7 %collective-permute-done.22 = bf16[24,6144]{1,0:T(8,128)(2,1)S(1)} collective-permute-done((bf16[24,6144]{1,0:T(8,128)(2,1)S(1)}, bf16[24,6144]{1,0:T(8,128)(2,1)S(1)}, u32[]{:S(2)}, u32[]{:S(2)}) %collective-permute-start.22) | collective-permute-done | bytes 294944 | tf_op jit(solution)/shard_map/ppermute | solution.py:130
  71.0 3.1 %collective-permute-start.20 = (bf16[24,6144]{1,0:T(8,128)(2,1)S(1)}, bf16[24,6144]{1,0:T(8,128)(2,1)S(1)}, u32[]{:S(2)}, u32[]{:S(2)}) collective-permute-start(bf16[24,6144]{1,0:T(8,128)(2,1)S(1)} %constant_dynamic-update-slice_fusion.2), channel_id=1, source_target_pairs={{0,12},{1,13},{2,14},{3,15},{4,0},{5,1},{6,2},{7,3},{8,4},{9,5},{1... | collective-permute-start | bytes 884744 | tf_op jit(solution)/shard_map/ppermute | solution.py:130
  74.6 6.6 %collective-permute-done.23 = bf16[24,6144]{1,0:T(8,128)(2,1)S(1)} collective-permute-done((bf16[24,6144]{1,0:T(8,128)(2,1)S(1)}, bf16[24,6144]{1,0:T(8,128)(2,1)S(1)}, u32[]{:S(2)}, u32[]{:S(2)}) %collective-permute-start.23) | collective-permute-done | bytes 294944 | tf_op jit(solution)/shard_map/ppermute | solution.py:130
  81.3 2.6 %fusion.10 = f32[384,512]{1,0:T(8,128)S(1)} fusion(bf16[384,6144]{1,0:T(8,128)(2,1)S(1)} %constant_dynamic-update-slice_fusion.8, bf16[1,6144,512]{2,1,0:T(8,128)(2,1)S(1)} %copy-done.3), kind=kOutput, calls=%fused_computation.14 | convolution fusion | flops 2415919104 | bytes 11796480 | tf_op jit(solution)/shard_map/dot_general | solution.py:254
  83.9 2.6 %multiply_convert_fusion = bf16[384,512]{1,0:T(8,128)(2,1)S(1)} fusion(f32[384,512]{1,0:T(8,128)S(1)} %fusion.10, bf16[384,6144]{1,0:T(8,128)(2,1)S(1)} %constant_dynamic-update-slice_fusion.8, bf16[1,6144,512]{2,1,0:T(8,128)(2,1)S(1)} %bitcast.91), kind=kOutput, calls=%fused_computation.29 | convolution fusion | flops 2417098752 | bytes 12189696 | tf_op jit(solution)/shard_map/dot_general | solution.py:255
  86.7 2.8 %convolution_convert_fusion = bf16[384,6144]{1,0:T(8,128)(2,1)S(1)} fusion(bf16[1,512,6144]{2,1,0:T(8,128)(2,1)S(1)} %bitcast.75, bf16[96,512]{1,0:T(8,128)(2,1)S(1)} %bitcast.87, bf16[288,512]{1,0:T(8,128)(2,1)S(1)} %bitcast.78), kind=kOutput, calls=%fused_computation | convolution fusion | flops 2419064832 | bytes 11403264 | tf_op jit(solution)/shard_map/dot_general | solution.py:163
  91.7 2.7 %collective-permute-start.21 = (bf16[48,6144]{1,0:T(8,128)(2,1)S(1)}, bf16[48,6144]{1,0:T(8,128)(2,1)S(1)}, u32[]{:S(2)}, u32[]{:S(2)}) collective-permute-start(bf16[48,6144]{1,0:T(8,128)(2,1)S(1)} %pad_maximum_fusion.6), channel_id=1, source_target_pairs={{0,12},{1,13},{2,14},{3,15},{4,0},{5,1},{6,2},{7,3},{8,4},{9,5},{1... | collective-permute-start | bytes 1769480 | tf_op jit(solution)/shard_map/ppermute | solution.py:130
  94.6 5.4 %collective-permute-done.13 = bf16[48,6144]{1,0:T(8,128)(2,1)S(1)} collective-permute-done((bf16[48,6144]{1,0:T(8,128)(2,1)S(1)}, bf16[48,6144]{1,0:T(8,128)(2,1)S(1)}, u32[]{:S(2)}, u32[]{:S(2)}) %collective-permute-start.13) | collective-permute-done | bytes 589856 | tf_op jit(solution)/shard_map/ppermute | solution.py:130
  108.8 3.8 %collective-permute-done.28 = bf16[48,6144]{1,0:T(8,128)(2,1)S(1)} collective-permute-done((bf16[48,6144]{1,0:T(8,128)(2,1)S(1)}, bf16[48,6144]{1,0:T(8,128)(2,1)S(1)}, u32[]{:S(2)}, u32[]{:S(2)}) %collective-permute-start.28) | collective-permute-done | bytes 589856 | tf_op jit(solution)/shard_map/ppermute | solution.py:130
  117.1 4.8 %collective-permute-done.25 = bf16[72,6144]{1,0:T(8,128)(2,1)S(1)} collective-permute-done((bf16[72,6144]{1,0:T(8,128)(2,1)S(1)}, bf16[72,6144]{1,0:T(8,128)(2,1)S(1)}, u32[]{:S(2)}, u32[]{:S(2)}) %collective-permute-start.25) | collective-permute-done | bytes 884768 | tf_op jit(solution)/shard_map/ppermute | solution.py:130
  121.9 6.3 %collective-permute-done.26 = bf16[24,6144]{1,0:T(8,128)(2,1)S(1)} collective-permute-done((bf16[24,6144]{1,0:T(8,128)(2,1)S(1)}, bf16[24,6144]{1,0:T(8,128)(2,1)S(1)}, u32[]{:S(2)}, u32[]{:S(2)}) %collective-permute-start.26) | collective-permute-done | bytes 294944 | tf_op jit(solution)/shard_map/ppermute | solution.py:130
  128.6 4.3 %collective-permute-done.39 = bf16[48,6144]{1,0:T(8,128)(2,1)S(1)} collective-permute-done((bf16[48,6144]{1,0:T(8,128)(2,1)S(1)}, bf16[48,6144]{1,0:T(8,128)(2,1)S(1)}, u32[]{:S(2)}, u32[]{:S(2)}) %collective-permute-start.39) | collective-permute-done | bytes 589856 | tf_op jit(solution)/shard_map/ppermute | solution.py:130
  133.2 10.4 %collective-permute-done.29 = bf16[48,6144]{1,0:T(8,128)(2,1)S(1)} collective-permute-done((bf16[48,6144]{1,0:T(8,128)(2,1)S(1)}, bf16[48,6144]{1,0:T(8,128)(2,1)S(1)}, u32[]{:S(2)}, u32[]{:S(2)}) %collective-permute-start.29) | collective-permute-done | bytes 589856 | tf_op jit(solution)/shard_map/ppermute | solution.py:130
  143.6 3.3 %collective-permute-start.37 = (bf16[48,6144]{1,0:T(8,128)(2,1)S(1)}, bf16[48,6144]{1,0:T(8,128)(2,1)S(1)}, u32[]{:S(2)}, u32[]{:S(2)}) collective-permute-start(bf16[48,6144]{1,0:T(8,128)(2,1)S(1)} %pad_maximum_fusion.8), channel_id=1, source_target_pairs={{0,3},{1,0},{2,1},{3,2},{4,7},{5,4},{6,5},{7,6},{8,11},{9,8},{10,9... | collective-permute-start | bytes 1769480 | tf_op jit(solution)/shard_map/ppermute | solution.py:130
  148.7 5.0 %collective-permute-done.37 = bf16[48,6144]{1,0:T(8,128)(2,1)S(1)} collective-permute-done((bf16[48,6144]{1,0:T(8,128)(2,1)S(1)}, bf16[48,6144]{1,0:T(8,128)(2,1)S(1)}, u32[]{:S(2)}, u32[]{:S(2)}) %collective-permute-start.37) | collective-permute-done | bytes 589856 | tf_op jit(solution)/shard_map/ppermute | solution.py:130
  154.0 3.5 %collective-permute-start.31 = (bf16[24,6144]{1,0:T(8,128)(2,1)S(1)}, bf16[24,6144]{1,0:T(8,128)(2,1)S(1)}, u32[]{:S(2)}, u32[]{:S(2)}) collective-permute-start(bf16[24,6144]{1,0:T(8,128)(2,1)S(1)} %get-tuple-element.36), channel_id=1, source_target_pairs={{0,3},{1,0},{2,1},{3,2},{4,7},{5,4},{6,5},{7,6},{8,11},{9,8},{10,9... | collective-permute-start | bytes 884744 | tf_op jit(solution)/shard_map/ppermute | solution.py:130
  159.6 6.5 %collective-permute-done.43 = bf16[24,6144]{1,0:T(8,128)(2,1)S(1)} collective-permute-done((bf16[24,6144]{1,0:T(8,128)(2,1)S(1)}, bf16[24,6144]{1,0:T(8,128)(2,1)S(1)}, u32[]{:S(2)}, u32[]{:S(2)}) %collective-permute-start.43) | collective-permute-done | bytes 294944 | tf_op jit(solution)/shard_map/ppermute | solution.py:130
  168.5 3.5 %collective-permute-done.46.across_ref = bf16[24,3072]{1,0:T(8,128)(2,1)S(1)} collective-permute-done((bf16[24,3072]{1,0:T(8,128)(2,1)S(1)}, bf16[24,3072]{1,0:T(8,128)(2,1)S(1)}, u32[]{:S(2)}, u32[]{:S(2)}) %collective-permute-start.46) | collective-permute-done | bytes 147488 | tf_op jit(solution)/shard_map/ppermute | solution.py:118
  173.6 18.6 %collective-permute-start.47 = (bf16[96,3072]{1,0:T(8,128)(2,1)S(1)}, bf16[96,3072]{1,0:T(8,128)(2,1)S(1)}, u32[]{:S(2)}, u32[]{:S(2)}) collective-permute-start(bf16[96,3072]{1,0:T(8,128)(2,1)S(1)} %pad_maximum_fusion.9), channel_id=1, source_target_pairs={{0,16},{16,0},{32,48},{48,32},{64,80},{80,64},{96,112},{112,96},{1... | collective-permute-start | bytes 1769480 | tf_op jit(solution)/shard_map/ppermute | solution.py:122
  (175 shorter events, 62.9 us)
Async XLA Ops:
  22.4 51.7 %collective-permute-start.14 = (bf16[72,6144]{1,0:T(8,128)(2,1)S(1)}, bf16[72,6144]{1,0:T(8,128)(2,1)S(1)}, u32[]{:S(2)}, u32[]{:S(2)}) collective-permute-start(bf16[72,6144]{1,0:T(8,128)(2,1)S(1)} %pad_maximum_fusion.1), channel_id=1, source_target_pairs={{0,3},{1,0},{2,1},{3,2},{4,7},{5,4},{6,5},{7,6},{8,11},{9,8},{10,9... | collective-permute-start | bytes 2654216 | tf_op jit(solution)/shard_map/ppermute | solution.py:130
  25.2 38.9 %collective-permute-start.12 = (bf16[72,6144]{1,0:T(8,128)(2,1)S(1)}, bf16[72,6144]{1,0:T(8,128)(2,1)S(1)}, u32[]{:S(2)}, u32[]{:S(2)}) collective-permute-start(bf16[72,6144]{1,0:T(8,128)(2,1)S(1)} %pad_maximum_fusion.1), channel_id=1, source_target_pairs={{0,1},{1,2},{2,3},{3,0},{4,5},{5,6},{6,7},{7,4},{8,9},{9,10},{10,1... | collective-permute-start | bytes 2654216 | tf_op jit(solution)/shard_map/ppermute | solution.py:130
  25.7 48.7 %collective-permute-start.17 = (bf16[72,6144]{1,0:T(8,128)(2,1)S(1)}, bf16[72,6144]{1,0:T(8,128)(2,1)S(1)}, u32[]{:S(2)}, u32[]{:S(2)}) collective-permute-start(bf16[72,6144]{1,0:T(8,128)(2,1)S(1)} %pad_maximum_fusion.2), channel_id=1, source_target_pairs={{0,4},{1,5},{2,6},{3,7},{4,8},{5,9},{6,10},{7,11},{8,12},{9,13},{1... | collective-permute-start | bytes 2654216 | tf_op jit(solution)/shard_map/ppermute | solution.py:130
  27.1 54.0 %collective-permute-start.19 = (bf16[72,6144]{1,0:T(8,128)(2,1)S(1)}, bf16[72,6144]{1,0:T(8,128)(2,1)S(1)}, u32[]{:S(2)}, u32[]{:S(2)}) collective-permute-start(bf16[72,6144]{1,0:T(8,128)(2,1)S(1)} %pad_maximum_fusion.2), channel_id=1, source_target_pairs={{0,12},{1,13},{2,14},{3,15},{4,0},{5,1},{6,2},{7,3},{8,4},{9,5},{1... | collective-permute-start | bytes 2654216 | tf_op jit(solution)/shard_map/ppermute | solution.py:130
  30.5 18.2 %collective-permute-start.10 = (bf16[24,3072]{1,0:T(8,128)(2,1)S(1)}, bf16[24,3072]{1,0:T(8,128)(2,1)S(1)}, u32[]{:S(2)}, u32[]{:S(2)}) collective-permute-start(bf16[24,3072]{1,0:T(8,128)(2,1)S(1)} %slice.358), channel_id=1, source_target_pairs={{0,1},{1,2},{2,3},{3,0},{4,5},{5,6},{6,7},{7,4},{8,9},{9,10},{10,1... | collective-permute-start | bytes 442376 | tf_op jit(solution)/shard_map/ppermute | solution.py:130
  56.9 17.5 %collective-permute-start.15 = (bf16[24,6144]{1,0:T(8,128)(2,1)S(1)}, bf16[24,6144]{1,0:T(8,128)(2,1)S(1)}, u32[]{:S(2)}, u32[]{:S(2)}) collective-permute-start(bf16[24,6144]{1,0:T(8,128)(2,1)S(1)} %constant_dynamic-update-slice_fusion), channel_id=1, source_target_pairs={{0,3},{1,0},{2,1},{3,2},{4,7},{5,4},{6,5},{7,6},{8,11},{9,8},{10,9... | collective-permute-start | bytes 884744 | tf_op jit(solution)/shard_map/ppermute | solution.py:130
  89.8 10.7 %collective-permute-start.16 = (bf16[48,6144]{1,0:T(8,128)(2,1)S(1)}, bf16[48,6144]{1,0:T(8,128)(2,1)S(1)}, u32[]{:S(2)}, u32[]{:S(2)}) collective-permute-start(bf16[48,6144]{1,0:T(8,128)(2,1)S(1)} %pad_maximum_fusion.5), channel_id=1, source_target_pairs={{0,3},{1,0},{2,1},{3,2},{4,7},{5,4},{6,5},{7,6},{8,11},{9,8},{10,9... | collective-permute-start | bytes 1769480 | tf_op jit(solution)/shard_map/ppermute | solution.py:130
  91.5 11.3 %collective-permute-start.18 = (bf16[48,6144]{1,0:T(8,128)(2,1)S(1)}, bf16[48,6144]{1,0:T(8,128)(2,1)S(1)}, u32[]{:S(2)}, u32[]{:S(2)}) collective-permute-start(bf16[48,6144]{1,0:T(8,128)(2,1)S(1)} %slice.363), channel_id=1, source_target_pairs={{0,4},{1,5},{2,6},{3,7},{4,8},{5,9},{6,10},{7,11},{8,12},{9,13},{1... | collective-permute-start | bytes 1769480 | tf_op jit(solution)/shard_map/ppermute | solution.py:130
  91.7 11.3 %collective-permute-start.21 = (bf16[48,6144]{1,0:T(8,128)(2,1)S(1)}, bf16[48,6144]{1,0:T(8,128)(2,1)S(1)}, u32[]{:S(2)}, u32[]{:S(2)}) collective-permute-start(bf16[48,6144]{1,0:T(8,128)(2,1)S(1)} %pad_maximum_fusion.6), channel_id=1, source_target_pairs={{0,12},{1,13},{2,14},{3,15},{4,0},{5,1},{6,2},{7,3},{8,4},{9,5},{1... | collective-permute-start | bytes 1769480 | tf_op jit(solution)/shard_map/ppermute | solution.py:130
  94.4 18.2 %collective-permute-start.28 = (bf16[48,6144]{1,0:T(8,128)(2,1)S(1)}, bf16[48,6144]{1,0:T(8,128)(2,1)S(1)}, u32[]{:S(2)}, u32[]{:S(2)}) collective-permute-start(bf16[48,6144]{1,0:T(8,128)(2,1)S(1)} %get-tuple-element.19), channel_id=1, source_target_pairs={{0,4},{1,5},{2,6},{3,7},{4,8},{5,9},{6,10},{7,11},{8,12},{9,13},{1... | collective-permute-start | bytes 1769480 | tf_op jit(solution)/shard_map/ppermute | solution.py:130
  100.0 14.3 %collective-permute-start.38 = (bf16[48,6144]{1,0:T(8,128)(2,1)S(1)}, bf16[48,6144]{1,0:T(8,128)(2,1)S(1)}, u32[]{:S(2)}, u32[]{:S(2)}) collective-permute-start(bf16[48,6144]{1,0:T(8,128)(2,1)S(1)} %get-tuple-element.17), channel_id=1, source_target_pairs={{0,1},{1,2},{2,3},{3,0},{4,5},{5,6},{6,7},{7,4},{8,9},{9,10},{10,1... | collective-permute-start | bytes 1769480 | tf_op jit(solution)/shard_map/ppermute | solution.py:130
  100.6 15.5 %collective-permute-start.35 = (bf16[72,6144]{1,0:T(8,128)(2,1)S(1)}, bf16[72,6144]{1,0:T(8,128)(2,1)S(1)}, u32[]{:S(2)}, u32[]{:S(2)}) collective-permute-start(bf16[72,6144]{1,0:T(8,128)(2,1)S(1)} %pad_maximum_fusion.4), channel_id=1, source_target_pairs={{0,3},{1,0},{2,1},{3,2},{4,7},{5,4},{6,5},{7,6},{8,11},{9,8},{10,9... | collective-permute-start | bytes 2654216 | tf_op jit(solution)/shard_map/ppermute | solution.py:130
  102.8 19.1 %collective-permute-start.25 = (bf16[72,6144]{1,0:T(8,128)(2,1)S(1)}, bf16[72,6144]{1,0:T(8,128)(2,1)S(1)}, u32[]{:S(2)}, u32[]{:S(2)}) collective-permute-start(bf16[72,6144]{1,0:T(8,128)(2,1)S(1)} %pad_maximum_fusion.3), channel_id=1, source_target_pairs={{0,12},{1,13},{2,14},{3,15},{4,0},{5,1},{6,2},{7,3},{8,4},{9,5},{1... | collective-permute-start | bytes 2654216 | tf_op jit(solution)/shard_map/ppermute | solution.py:130
  103.0 44.2 %collective-permute-start.34 = (bf16[24,6144]{1,0:T(8,128)(2,1)S(1)}, bf16[24,6144]{1,0:T(8,128)(2,1)S(1)}, u32[]{:S(2)}, u32[]{:S(2)}) collective-permute-start(bf16[24,6144]{1,0:T(8,128)(2,1)S(1)} %get-tuple-element.11), channel_id=1, source_target_pairs={{0,1},{1,2},{2,3},{3,0},{4,5},{5,6},{6,7},{7,4},{8,9},{9,10},{10,1... | collective-permute-start | bytes 884744 | tf_op jit(solution)/shard_map/ppermute | solution.py:130
  112.6 15.6 %collective-permute-start.26 = (bf16[24,6144]{1,0:T(8,128)(2,1)S(1)}, bf16[24,6144]{1,0:T(8,128)(2,1)S(1)}, u32[]{:S(2)}, u32[]{:S(2)}) collective-permute-start(bf16[24,6144]{1,0:T(8,128)(2,1)S(1)} %get-tuple-element.28), channel_id=1, source_target_pairs={{0,12},{1,13},{2,14},{3,15},{4,0},{5,1},{6,2},{7,3},{8,4},{9,5},{1... | collective-permute-start | bytes 884744 | tf_op jit(solution)/shard_map/ppermute | solution.py:130
  114.2 14.0 %collective-permute-start.36 = (bf16[24,6144]{1,0:T(8,128)(2,1)S(1)}, bf16[24,6144]{1,0:T(8,128)(2,1)S(1)}, u32[]{:S(2)}, u32[]{:S(2)}) collective-permute-start(bf16[24,6144]{1,0:T(8,128)(2,1)S(1)} %get-tuple-element.25), channel_id=1, source_target_pairs={{0,3},{1,0},{2,1},{3,2},{4,7},{5,4},{6,5},{7,6},{8,11},{9,8},{10,9... | collective-permute-start | bytes 884744 | tf_op jit(solution)/shard_map/ppermute | solution.py:130
  116.1 37.9 %collective-permute-start.24 = (bf16[24,6144]{1,0:T(8,128)(2,1)S(1)}, bf16[24,6144]{1,0:T(8,128)(2,1)S(1)}, u32[]{:S(2)}, u32[]{:S(2)}) collective-permute-start(bf16[24,6144]{1,0:T(8,128)(2,1)S(1)} %get-tuple-element.14), channel_id=1, source_target_pairs={{0,4},{1,5},{2,6},{3,7},{4,8},{5,9},{6,10},{7,11},{8,12},{9,13},{1... | collective-permute-start | bytes 884744 | tf_op jit(solution)/shard_map/ppermute | solution.py:130
  121.9 11.0 %collective-permute-start.39 = (bf16[48,6144]{1,0:T(8,128)(2,1)S(1)}, bf16[48,6144]{1,0:T(8,128)(2,1)S(1)}, u32[]{:S(2)}, u32[]{:S(2)}) collective-permute-start(bf16[48,6144]{1,0:T(8,128)(2,1)S(1)} %get-tuple-element.15), channel_id=1, source_target_pairs={{0,1},{1,2},{2,3},{3,0},{4,5},{5,6},{6,7},{7,4},{8,9},{9,10},{10,1... | collective-permute-start | bytes 1769480 | tf_op jit(solution)/shard_map/ppermute | solution.py:130
  128.2 19.0 %collective-permute-start.42 = (bf16[24,6144]{1,0:T(8,128)(2,1)S(1)}, bf16[24,6144]{1,0:T(8,128)(2,1)S(1)}, u32[]{:S(2)}, u32[]{:S(2)}) collective-permute-start(bf16[24,6144]{1,0:T(8,128)(2,1)S(1)} %get-tuple-element.26), channel_id=1, source_target_pairs={{0,1},{1,2},{2,3},{3,0},{4,5},{5,6},{6,7},{7,4},{8,9},{9,10},{10,1... | collective-permute-start | bytes 884744 | tf_op jit(solution)/shard_map/ppermute | solution.py:130
  128.2 15.4 %collective-permute-start.29 = (bf16[48,6144]{1,0:T(8,128)(2,1)S(1)}, bf16[48,6144]{1,0:T(8,128)(2,1)S(1)}, u32[]{:S(2)}, u32[]{:S(2)}) collective-permute-start(bf16[48,6144]{1,0:T(8,128)(2,1)S(1)} %get-tuple-element.16), channel_id=1, source_target_pairs={{0,4},{1,5},{2,6},{3,7},{4,8},{5,9},{6,10},{7,11},{8,12},{9,13},{1... | collective-permute-start | bytes 1769480 | tf_op jit(solution)/shard_map/ppermute | solution.py:130
  132.9 21.1 %collective-permute-start.32 = (bf16[24,6144]{1,0:T(8,128)(2,1)S(1)}, bf16[24,6144]{1,0:T(8,128)(2,1)S(1)}, u32[]{:S(2)}, u32[]{:S(2)}) collective-permute-start(bf16[24,6144]{1,0:T(8,128)(2,1)S(1)} %get-tuple-element.27), channel_id=1, source_target_pairs={{0,4},{1,5},{2,6},{3,7},{4,8},{5,9},{6,10},{7,11},{8,12},{9,13},{1... | collective-permute-start | bytes 884744 | tf_op jit(solution)/shard_map/ppermute | solution.py:130
  153.9 12.6 %collective-permute-start.30 = (bf16[24,6144]{1,0:T(8,128)(2,1)S(1)}, bf16[24,6144]{1,0:T(8,128)(2,1)S(1)}, u32[]{:S(2)}, u32[]{:S(2)}) collective-permute-start(bf16[24,6144]{1,0:T(8,128)(2,1)S(1)} %get-tuple-element.35), channel_id=1, source_target_pairs={{0,1},{1,2},{2,3},{3,0},{4,5},{5,6},{6,7},{7,4},{8,9},{9,10},{10,1... | collective-permute-start | bytes 884744 | tf_op jit(solution)/shard_map/ppermute | solution.py:130
  154.0 12.5 %collective-permute-start.31 = (bf16[24,6144]{1,0:T(8,128)(2,1)S(1)}, bf16[24,6144]{1,0:T(8,128)(2,1)S(1)}, u32[]{:S(2)}, u32[]{:S(2)}) collective-permute-start(bf16[24,6144]{1,0:T(8,128)(2,1)S(1)} %get-tuple-element.36), channel_id=1, source_target_pairs={{0,3},{1,0},{2,1},{3,2},{4,7},{5,4},{6,5},{7,6},{8,11},{9,8},{10,9... | collective-permute-start | bytes 884744 | tf_op jit(solution)/shard_map/ppermute | solution.py:130
  173.6 20.3 %collective-permute-start.47 = (bf16[96,3072]{1,0:T(8,128)(2,1)S(1)}, bf16[96,3072]{1,0:T(8,128)(2,1)S(1)}, u32[]{:S(2)}, u32[]{:S(2)}) collective-permute-start(bf16[96,3072]{1,0:T(8,128)(2,1)S(1)} %pad_maximum_fusion.9), channel_id=1, source_target_pairs={{0,16},{16,0},{32,48},{48,32},{64,80},{80,64},{96,112},{112,96},{1... | collective-permute-start | bytes 1769480 | tf_op jit(solution)/shard_map/ppermute | solution.py:122
  (32 other events, 315.5 us)

commit v3 on v2

--- a/solution.py
+++ b/solution.py
@@ -131,11 +131,9 @@
 
 
 def gather_ring(own, first, second):
-    half = own.shape[1] // 2
     below, above = shift(own, first, 1), shift(own, first, -1)
-    across = [shift(below[:, :half], first, 1), shift(above[:, half:], first, -1)]
+    far = shift(own, first, 2)
     near = lax.optimization_barrier(jnp.concatenate([own, below, above], axis=0))
-    far = jnp.concatenate(across, axis=1)
     rows = own.shape[0]
     below, above = [shift(near, second, 1)], [shift(near, second, -1)]
     below.append(shift(far, second, 1))
@@ -178,13 +176,10 @@
     up_sum = [add(piece(early, 6 * i + 2, 2), up_one[i]) for i in both]
     up_three = [shift(up_sum[i], orders[i][0], 1) for i in both]
     up_two = [shift(piece(late, 3 * i + 1, 1), orders[i][0], 1) for i in both]
-    down_sum = [
-        jnp.concatenate(
-            [add(piece(late, 6 + i, 1), down_one[i][:rows]), add(piece(late, 3 * i, 1), down_two[i])], axis=0
-        )
-        for i in both
-    ]
-    down_three = [shift(down_sum[i], orders[i][0], -1) for i in both]
+    soon = [lax.optimization_barrier(piece(late, 6 + i, 1)) for i in both]
+    down_own = [shift(add(soon[i], down_one[i][:rows]), orders[i][0], -1) for i in both]
+    down_sum = [add(piece(late, 3 * i, 1), down_two[i]) for i in both]
+    down_far = [shift(down_sum[i], orders[i][0], -1) for i in both]
     kept = [product([start[i, 0, 0], end[i, 0, 0], middle[i, :, 0]]) for i in both]
     sides = []
     for i in both:
@@ -192,9 +187,9 @@
         sides.append((shift(inner[rows:], orders[i][1], 1), shift(inner[:rows], orders[i][1], -1)))
     results = []
     for i in both:
-        across = add(kept[i][rows : 2 * rows], up_two[i], down_three[i][rows:])
+        across = add(kept[i][rows : 2 * rows], up_two[i], down_far[i])
         across = shift(across, orders[i][1], 2)
-        own = lax.optimization_barrier(add(kept[i][:rows], up_own[i], down_three[i][:rows]))
+        own = lax.optimization_barrier(add(kept[i][:rows], up_own[i], down_own[i]))
         results.append(add(own, *sides[i], across))
     return results
 

time: 196 us -> 206 us (1.051)
  waiting for transfers between devices: 98.4 us -> 108 us
  starting transfers between devices: 68.6 us -> 71 us
    ppermute x40, waiting for transfers between devices: 89 us -> 94 us  [shift(): lax.ppermute(value, 'hidden', [(i, target(i)) for i in range(RING * RING)])]
    ppermute x6, waiting for transfers between devices: 6.69 us -> 11.2 us  [along_x(): return lax.ppermute(value, 'expert', pairs)]
    ppermute x40, starting transfers between devices: 42.3 us -> 44.6 us  [shift(): lax.ppermute(value, 'hidden', [(i, target(i)) for i in range(RING * RING)])]
  transfers between devices with their start and end apart: 48 -> 48, of which waited for: 23 -> 24; matrix products, arithmetic and copies ran while one was open for 7% -> 6% of each run, Pallas kernels for 0% -> 0%
where the time goes in v3:
time: 206 us
  waiting for transfers between devices  108 us (52%)
  starting transfers between devices  71 us (34%)
  matrix products  17.3 us (8%)
  Pallas kernels  5.18 us (3%)
  other arithmetic  2.75 us (1%)
    ppermute x40, waiting for transfers between devices, shift(): lax.ppermute(value, 'hidden', [(i, target(i)) for i in range(RING * RING)])  94 us
    ppermute x40, starting transfers between devices, shift(): lax.ppermute(value, 'hidden', [(i, target(i)) for i in range(RING * RING)])  44.6 us
    ppermute x2, starting transfers between devices, other_core(): return lax.ppermute(value, 'expert', [(i, i ^ 1) for i in range(2 * RING)])  19.5 us
    ppermute x6, waiting for transfers between devices, along_x(): return lax.ppermute(value, 'expert', pairs)  11.2 us
    ppermute x6, starting transfers between devices, along_x(): return lax.ppermute(value, 'expert', pairs)  6.95 us
    dot_general x4, matrix products, product(): jnp.dot(jnp.concatenate(value, axis=0), down, preferred_element_type=jnp....  6.49 us
    dot_general x3, matrix products, per_device(): upper = jnp.dot(value, up_local, preferred_element_type=jnp.float32)  5.42 us
    dot_general x3, matrix products, per_device(): gate = jnp.dot(value, gate_local, preferred_element_type=jnp.float32)  5.34 us
  transfers between devices with their start and end apart: 48, of which 24 were waited for; matrix products, arithmetic and copies ran while one was open for 6% of the time, Pallas kernels for 0%

profile of v3, /device:TPU:1, one launch (start us, length us, event | category | flops | bytes accessed | tf_op | source)
XLA Modules:
  0.0 206.3 jit_solution(14174001222259079425)
XLA Ops:
  11.3 5.5 %collective-permute-done.6 = bf16[24,3072]{1,0:T(8,128)(2,1)S(1)} collective-permute-done((bf16[24,3072]{1,0:T(8,128)(2,1)S(1)}, bf16[24,3072]{1,0:T(8,128)(2,1)S(1)}, u32[]{:S(2)}, u32[]{:S(2)}) %collective-permute-start.6) | collective-permute-done | bytes 147488 | tf_op jit(solution)/shard_map/ppermute | solution.py:118
  17.0 3.0 %collective-permute-start.9 = (bf16[24,6144]{1,0:T(8,128)(2,1)S(1)}, bf16[24,6144]{1,0:T(8,128)(2,1)S(1)}, u32[]{:S(2)}, u32[]{:S(2)}) collective-permute-start(bf16[24,6144]{1,0:T(8,128)(2,1)S(1)} %maximum_maximum_fusion.1), channel_id=1, source_target_pairs={{0,2},{1,3},{2,0},{3,1},{4,6},{5,7},{6,4},{7,5},{8,10},{9,11},{10,... | collective-permute-start | bytes 884744 | tf_op jit(solution)/shard_map/ppermute | solution.py:130
  21.6 3.7 %collective-permute-start.4 = (bf16[24,6144]{1,0:T(8,128)(2,1)S(1)}, bf16[24,6144]{1,0:T(8,128)(2,1)S(1)}, u32[]{:S(2)}, u32[]{:S(2)}) collective-permute-start(bf16[24,6144]{1,0:T(8,128)(2,1)S(1)} %maximum_maximum_fusion), channel_id=1, source_target_pairs={{0,8},{1,9},{2,10},{3,11},{4,12},{5,13},{6,14},{7,15},{8,0},{9,1},... | collective-permute-start | bytes 884744 | tf_op jit(solution)/shard_map/ppermute | solution.py:130
  25.7 7.4 %collective-permute-done.8 = bf16[24,6144]{1,0:T(8,128)(2,1)S(1)} collective-permute-done((bf16[24,6144]{1,0:T(8,128)(2,1)S(1)}, bf16[24,6144]{1,0:T(8,128)(2,1)S(1)}, u32[]{:S(2)}, u32[]{:S(2)}) %collective-permute-start.8) | collective-permute-done | bytes 294944 | tf_op jit(solution)/shard_map/ppermute | solution.py:130
  34.8 3.9 %collective-permute-done.3 = bf16[24,6144]{1,0:T(8,128)(2,1)S(1)} collective-permute-done((bf16[24,6144]{1,0:T(8,128)(2,1)S(1)}, bf16[24,6144]{1,0:T(8,128)(2,1)S(1)}, u32[]{:S(2)}, u32[]{:S(2)}) %collective-permute-start.3) | collective-permute-done | bytes 294944 | tf_op jit(solution)/shard_map/ppermute | solution.py:130
  38.7 4.0 %collective-permute-done.2 = bf16[24,6144]{1,0:T(8,128)(2,1)S(1)} collective-permute-done((bf16[24,6144]{1,0:T(8,128)(2,1)S(1)}, bf16[24,6144]{1,0:T(8,128)(2,1)S(1)}, u32[]{:S(2)}, u32[]{:S(2)}) %collective-permute-start.2) | collective-permute-done | bytes 294944 | tf_op jit(solution)/shard_map/ppermute | solution.py:130
  42.8 3.1 %collective-permute-start.10 = (bf16[72,6144]{1,0:T(8,128)(2,1)S(1)}, bf16[72,6144]{1,0:T(8,128)(2,1)S(1)}, u32[]{:S(2)}, u32[]{:S(2)}) collective-permute-start(bf16[72,6144]{1,0:T(8,128)(2,1)S(1)} %pad_maximum_fusion.1), channel_id=1, source_target_pairs={{0,1},{1,2},{2,3},{3,0},{4,5},{5,6},{6,7},{7,4},{8,9},{9,10},{10,1... | collective-permute-start | bytes 2654216 | tf_op jit(solution)/shard_map/ppermute | solution.py:130
  48.7 2.8 %collective-permute-start.12 = (bf16[72,6144]{1,0:T(8,128)(2,1)S(1)}, bf16[72,6144]{1,0:T(8,128)(2,1)S(1)}, u32[]{:S(2)}, u32[]{:S(2)}) collective-permute-start(bf16[72,6144]{1,0:T(8,128)(2,1)S(1)} %pad_maximum_fusion.1), channel_id=1, source_target_pairs={{0,3},{1,0},{2,1},{3,2},{4,7},{5,4},{6,5},{7,6},{8,11},{9,8},{10,9... | collective-permute-start | bytes 2654216 | tf_op jit(solution)/shard_map/ppermute | solution.py:130
  53.0 13.2 %collective-permute-done.10 = bf16[72,6144]{1,0:T(8,128)(2,1)S(1)} collective-permute-done((bf16[72,6144]{1,0:T(8,128)(2,1)S(1)}, bf16[72,6144]{1,0:T(8,128)(2,1)S(1)}, u32[]{:S(2)}, u32[]{:S(2)}) %collective-permute-start.10) | collective-permute-done | bytes 884768 | tf_op jit(solution)/shard_map/ppermute | solution.py:130
  66.3 8.1 %collective-permute-done.20 = bf16[24,6144]{1,0:T(8,128)(2,1)S(1)} collective-permute-done((bf16[24,6144]{1,0:T(8,128)(2,1)S(1)}, bf16[24,6144]{1,0:T(8,128)(2,1)S(1)}, u32[]{:S(2)}, u32[]{:S(2)}) %collective-permute-start.20) | collective-permute-done | bytes 294944 | tf_op jit(solution)/shard_map/ppermute | solution.py:130
  75.4 5.8 %collective-permute-done.13 = bf16[24,6144]{1,0:T(8,128)(2,1)S(1)} collective-permute-done((bf16[24,6144]{1,0:T(8,128)(2,1)S(1)}, bf16[24,6144]{1,0:T(8,128)(2,1)S(1)}, u32[]{:S(2)}, u32[]{:S(2)}) %collective-permute-start.13) | collective-permute-done | bytes 294944 | tf_op jit(solution)/shard_map/ppermute | solution.py:130
  86.8 2.8 %convolution_convert_fusion = bf16[384,6144]{1,0:T(8,128)(2,1)S(1)} fusion(bf16[1,512,6144]{2,1,0:T(8,128)(2,1)S(1)} %bitcast.75, bf16[96,512]{1,0:T(8,128)(2,1)S(1)} %bitcast.87, bf16[288,512]{1,0:T(8,128)(2,1)S(1)} %bitcast.78), kind=kOutput, calls=%fused_computation | convolution fusion | flops 2419064832 | bytes 11403264 | tf_op jit(solution)/shard_map/dot_general | solution.py:161
  93.5 9.2 %collective-permute-done.11 = bf16[48,6144]{1,0:T(8,128)(2,1)S(1)} collective-permute-done((bf16[48,6144]{1,0:T(8,128)(2,1)S(1)}, bf16[48,6144]{1,0:T(8,128)(2,1)S(1)}, u32[]{:S(2)}, u32[]{:S(2)}) %collective-permute-start.11) | collective-permute-done | bytes 589856 | tf_op jit(solution)/shard_map/ppermute | solution.py:130
  104.2 2.9 %collective-permute-start.23 = (bf16[72,6144]{1,0:T(8,128)(2,1)S(1)}, bf16[72,6144]{1,0:T(8,128)(2,1)S(1)}, u32[]{:S(2)}, u32[]{:S(2)}) collective-permute-start(bf16[72,6144]{1,0:T(8,128)(2,1)S(1)} %pad_maximum_fusion.3), channel_id=1, source_target_pairs={{0,12},{1,13},{2,14},{3,15},{4,0},{5,1},{6,2},{7,3},{8,4},{9,5},{1... | collective-permute-start | bytes 2654216 | tf_op jit(solution)/shard_map/ppermute | solution.py:130
  112.7 9.0 %collective-permute-done.36 = bf16[48,6144]{1,0:T(8,128)(2,1)S(1)} collective-permute-done((bf16[48,6144]{1,0:T(8,128)(2,1)S(1)}, bf16[48,6144]{1,0:T(8,128)(2,1)S(1)}, u32[]{:S(2)}, u32[]{:S(2)}) %collective-permute-start.36) | collective-permute-done | bytes 589856 | tf_op jit(solution)/shard_map/ppermute | solution.py:130
  123.2 4.4 %collective-permute-done.41 = bf16[24,6144]{1,0:T(8,128)(2,1)S(1)} collective-permute-done((bf16[24,6144]{1,0:T(8,128)(2,1)S(1)}, bf16[24,6144]{1,0:T(8,128)(2,1)S(1)}, u32[]{:S(2)}, u32[]{:S(2)}) %collective-permute-start.41) | collective-permute-done | bytes 294944 | tf_op jit(solution)/shard_map/ppermute | solution.py:130
  133.2 12.5 %collective-permute-done.34 = bf16[72,6144]{1,0:T(8,128)(2,1)S(1)} collective-permute-done((bf16[72,6144]{1,0:T(8,128)(2,1)S(1)}, bf16[72,6144]{1,0:T(8,128)(2,1)S(1)}, u32[]{:S(2)}, u32[]{:S(2)}) %collective-permute-start.34) | collective-permute-done | bytes 884768 | tf_op jit(solution)/shard_map/ppermute | solution.py:130
  148.6 2.9 %collective-permute-done.24 = bf16[24,6144]{1,0:T(8,128)(2,1)S(1)} collective-permute-done((bf16[24,6144]{1,0:T(8,128)(2,1)S(1)}, bf16[24,6144]{1,0:T(8,128)(2,1)S(1)}, u32[]{:S(2)}, u32[]{:S(2)}) %collective-permute-start.24) | collective-permute-done | bytes 294944 | tf_op jit(solution)/shard_map/ppermute | solution.py:130
  155.2 3.1 %collective-permute-done.35 = bf16[24,6144]{1,0:T(8,128)(2,1)S(1)} collective-permute-done((bf16[24,6144]{1,0:T(8,128)(2,1)S(1)}, bf16[24,6144]{1,0:T(8,128)(2,1)S(1)}, u32[]{:S(2)}, u32[]{:S(2)}) %collective-permute-start.35) | collective-permute-done | bytes 294944 | tf_op jit(solution)/shard_map/ppermute | solution.py:130
  158.6 3.3 %collective-permute-start.43 = (bf16[24,6144]{1,0:T(8,128)(2,1)S(1)}, bf16[24,6144]{1,0:T(8,128)(2,1)S(1)}, u32[]{:S(2)}, u32[]{:S(2)}) collective-permute-start(bf16[24,6144]{1,0:T(8,128)(2,1)S(1)} %get-tuple-element.30), channel_id=1, source_target_pairs={{0,8},{1,9},{2,10},{3,11},{4,12},{5,13},{6,14},{7,15},{8,0},{9,1},... | collective-permute-start | bytes 884744 | tf_op jit(solution)/shard_map/ppermute | solution.py:130
  163.3 3.5 %collective-permute-start.27 = (bf16[24,6144]{1,0:T(8,128)(2,1)S(1)}, bf16[24,6144]{1,0:T(8,128)(2,1)S(1)}, u32[]{:S(2)}, u32[]{:S(2)}) collective-permute-start(bf16[24,6144]{1,0:T(8,128)(2,1)S(1)} %get-tuple-element.35), channel_id=1, source_target_pairs={{0,1},{1,2},{2,3},{3,0},{4,5},{5,6},{6,7},{7,4},{8,9},{9,10},{10,1... | collective-permute-start | bytes 884744 | tf_op jit(solution)/shard_map/ppermute | solution.py:130
  169.8 3.8 %collective-permute-done.27 = bf16[24,6144]{1,0:T(8,128)(2,1)S(1)} collective-permute-done((bf16[24,6144]{1,0:T(8,128)(2,1)S(1)}, bf16[24,6144]{1,0:T(8,128)(2,1)S(1)}, u32[]{:S(2)}, u32[]{:S(2)}) %collective-permute-start.27) | collective-permute-done | bytes 294944 | tf_op jit(solution)/shard_map/ppermute | solution.py:130
  180.5 4.0 %collective-permute-done.44.below_ref = bf16[24,3072]{1,0:T(8,128)(2,1)S(1)} collective-permute-done((bf16[24,3072]{1,0:T(8,128)(2,1)S(1)}, bf16[24,3072]{1,0:T(8,128)(2,1)S(1)}, u32[]{:S(2)}, u32[]{:S(2)}) %collective-permute-start.44) | collective-permute-done | bytes 147488 | tf_op jit(solution)/shard_map/ppermute | solution.py:118
  184.5 18.0 %collective-permute-start.47 = (bf16[96,3072]{1,0:T(8,128)(2,1)S(1)}, bf16[96,3072]{1,0:T(8,128)(2,1)S(1)}, u32[]{:S(2)}, u32[]{:S(2)}) collective-permute-start(bf16[96,3072]{1,0:T(8,128)(2,1)S(1)} %pad_maximum_fusion.7), channel_id=1, source_target_pairs={{0,16},{16,0},{32,48},{48,32},{64,80},{80,64},{96,112},{112,96},{1... | collective-permute-start | bytes 1769480 | tf_op jit(solution)/shard_map/ppermute | solution.py:122
  (167 shorter events, 65.5 us)
Async XLA Ops:
  8.6 12.8 %collective-permute-start.1 = (bf16[24,3072]{1,0:T(8,128)(2,1)S(1)}, bf16[24,3072]{1,0:T(8,128)(2,1)S(1)}, u32[]{:S(2)}, u32[]{:S(2)}) collective-permute-start(bf16[24,3072]{1,0:T(8,128)(2,1)S(1)} %fusion.24), channel_id=1, source_target_pairs={{0,32},{16,48},{32,64},{48,80},{64,96},{80,112},{96,0},{112,16},{1... | collective-permute-start | bytes 442376 | tf_op jit(solution)/shard_map/ppermute | solution.py:118
  17.0 28.9 %collective-permute-start.9 = (bf16[24,6144]{1,0:T(8,128)(2,1)S(1)}, bf16[24,6144]{1,0:T(8,128)(2,1)S(1)}, u32[]{:S(2)}, u32[]{:S(2)}) collective-permute-start(bf16[24,6144]{1,0:T(8,128)(2,1)S(1)} %maximum_maximum_fusion.1), channel_id=1, source_target_pairs={{0,2},{1,3},{2,0},{3,1},{4,6},{5,7},{6,4},{7,5},{8,10},{9,11},{10,... | collective-permute-start | bytes 884744 | tf_op jit(solution)/shard_map/ppermute | solution.py:130
  19.9 13.2 %collective-permute-start.8 = (bf16[24,6144]{1,0:T(8,128)(2,1)S(1)}, bf16[24,6144]{1,0:T(8,128)(2,1)S(1)}, u32[]{:S(2)}, u32[]{:S(2)}) collective-permute-start(bf16[24,6144]{1,0:T(8,128)(2,1)S(1)} %maximum_maximum_fusion.1), channel_id=1, source_target_pairs={{0,3},{1,0},{2,1},{3,2},{4,7},{5,4},{6,5},{7,6},{8,11},{9,8},{10,9... | collective-permute-start | bytes 884744 | tf_op jit(solution)/shard_map/ppermute | solution.py:130
  20.7 14.0 %collective-permute-start.7 = (bf16[24,6144]{1,0:T(8,128)(2,1)S(1)}, bf16[24,6144]{1,0:T(8,128)(2,1)S(1)}, u32[]{:S(2)}, u32[]{:S(2)}) collective-permute-start(bf16[24,6144]{1,0:T(8,128)(2,1)S(1)} %maximum_maximum_fusion.1), channel_id=1, source_target_pairs={{0,1},{1,2},{2,3},{3,0},{4,5},{5,6},{6,7},{7,4},{8,9},{9,10},{10,1... | collective-permute-start | bytes 884744 | tf_op jit(solution)/shard_map/ppermute | solution.py:130
  21.6 24.3 %collective-permute-start.4 = (bf16[24,6144]{1,0:T(8,128)(2,1)S(1)}, bf16[24,6144]{1,0:T(8,128)(2,1)S(1)}, u32[]{:S(2)}, u32[]{:S(2)}) collective-permute-start(bf16[24,6144]{1,0:T(8,128)(2,1)S(1)} %maximum_maximum_fusion), channel_id=1, source_target_pairs={{0,8},{1,9},{2,10},{3,11},{4,12},{5,13},{6,14},{7,15},{8,0},{9,1},... | collective-permute-start | bytes 884744 | tf_op jit(solution)/shard_map/ppermute | solution.py:130
  25.3 13.5 %collective-permute-start.3 = (bf16[24,6144]{1,0:T(8,128)(2,1)S(1)}, bf16[24,6144]{1,0:T(8,128)(2,1)S(1)}, u32[]{:S(2)}, u32[]{:S(2)}) collective-permute-start(bf16[24,6144]{1,0:T(8,128)(2,1)S(1)} %maximum_maximum_fusion), channel_id=1, source_target_pairs={{0,12},{1,13},{2,14},{3,15},{4,0},{5,1},{6,2},{7,3},{8,4},{9,5},{1... | collective-permute-start | bytes 884744 | tf_op jit(solution)/shard_map/ppermute | solution.py:130
  42.8 23.5 %collective-permute-start.10 = (bf16[72,6144]{1,0:T(8,128)(2,1)S(1)}, bf16[72,6144]{1,0:T(8,128)(2,1)S(1)}, u32[]{:S(2)}, u32[]{:S(2)}) collective-permute-start(bf16[72,6144]{1,0:T(8,128)(2,1)S(1)} %pad_maximum_fusion.1), channel_id=1, source_target_pairs={{0,1},{1,2},{2,3},{3,0},{4,5},{5,6},{6,7},{7,4},{8,9},{9,10},{10,1... | collective-permute-start | bytes 2654216 | tf_op jit(solution)/shard_map/ppermute | solution.py:130
  48.7 26.3 %collective-permute-start.12 = (bf16[72,6144]{1,0:T(8,128)(2,1)S(1)}, bf16[72,6144]{1,0:T(8,128)(2,1)S(1)}, u32[]{:S(2)}, u32[]{:S(2)}) collective-permute-start(bf16[72,6144]{1,0:T(8,128)(2,1)S(1)} %pad_maximum_fusion.1), channel_id=1, source_target_pairs={{0,3},{1,0},{2,1},{3,2},{4,7},{5,4},{6,5},{7,6},{8,11},{9,8},{10,9... | collective-permute-start | bytes 2654216 | tf_op jit(solution)/shard_map/ppermute | solution.py:130
  51.5 29.8 %collective-permute-start.17 = (bf16[72,6144]{1,0:T(8,128)(2,1)S(1)}, bf16[72,6144]{1,0:T(8,128)(2,1)S(1)}, u32[]{:S(2)}, u32[]{:S(2)}) collective-permute-start(bf16[72,6144]{1,0:T(8,128)(2,1)S(1)} %pad_maximum_fusion.2), channel_id=1, source_target_pairs={{0,12},{1,13},{2,14},{3,15},{4,0},{5,1},{6,2},{7,3},{8,4},{9,5},{1... | collective-permute-start | bytes 2654216 | tf_op jit(solution)/shard_map/ppermute | solution.py:130
  52.7 28.5 %collective-permute-start.15 = (bf16[72,6144]{1,0:T(8,128)(2,1)S(1)}, bf16[72,6144]{1,0:T(8,128)(2,1)S(1)}, u32[]{:S(2)}, u32[]{:S(2)}) collective-permute-start(bf16[72,6144]{1,0:T(8,128)(2,1)S(1)} %pad_maximum_fusion.2), channel_id=1, source_target_pairs={{0,4},{1,5},{2,6},{3,7},{4,8},{5,9},{6,10},{7,11},{8,12},{9,13},{1... | collective-permute-start | bytes 2654216 | tf_op jit(solution)/shard_map/ppermute | solution.py:130
  53.0 28.3 %collective-permute-start.21 = (bf16[24,6144]{1,0:T(8,128)(2,1)S(1)}, bf16[24,6144]{1,0:T(8,128)(2,1)S(1)}, u32[]{:S(2)}, u32[]{:S(2)}) collective-permute-start(bf16[24,6144]{1,0:T(8,128)(2,1)S(1)} %collective-permute-done.9), channel_id=1, source_target_pairs={{0,4},{1,5},{2,6},{3,7},{4,8},{5,9},{6,10},{7,11},{8,12},{9,13},{1... | collective-permute-start | bytes 884744 | tf_op jit(solution)/shard_map/ppermute | solution.py:130
  90.0 13.9 %collective-permute-start.14 = (bf16[48,6144]{1,0:T(8,128)(2,1)S(1)}, bf16[48,6144]{1,0:T(8,128)(2,1)S(1)}, u32[]{:S(2)}, u32[]{:S(2)}) collective-permute-start(bf16[48,6144]{1,0:T(8,128)(2,1)S(1)} %pad_maximum_fusion.5), channel_id=1, source_target_pairs={{0,3},{1,0},{2,1},{3,2},{4,7},{5,4},{6,5},{7,6},{8,11},{9,8},{10,9... | collective-permute-start | bytes 1769480 | tf_op jit(solution)/shard_map/ppermute | solution.py:130
  93.4 59.3 %collective-permute-start.33 = (bf16[24,6144]{1,0:T(8,128)(2,1)S(1)}, bf16[24,6144]{1,0:T(8,128)(2,1)S(1)}, u32[]{:S(2)}, u32[]{:S(2)}) collective-permute-start(bf16[24,6144]{1,0:T(8,128)(2,1)S(1)} %get-tuple-element.11), channel_id=1, source_target_pairs={{0,1},{1,2},{2,3},{3,0},{4,5},{5,6},{6,7},{7,4},{8,9},{9,10},{10,1... | collective-permute-start | bytes 884744 | tf_op jit(solution)/shard_map/ppermute | solution.py:130
  102.8 43.0 %collective-permute-start.22 = (bf16[24,6144]{1,0:T(8,128)(2,1)S(1)}, bf16[24,6144]{1,0:T(8,128)(2,1)S(1)}, u32[]{:S(2)}, u32[]{:S(2)}) collective-permute-start(bf16[24,6144]{1,0:T(8,128)(2,1)S(1)} %get-tuple-element.14), channel_id=1, source_target_pairs={{0,4},{1,5},{2,6},{3,7},{4,8},{5,9},{6,10},{7,11},{8,12},{9,13},{1... | collective-permute-start | bytes 884744 | tf_op jit(solution)/shard_map/ppermute | solution.py:130
  103.9 17.8 %collective-permute-start.36 = (bf16[48,6144]{1,0:T(8,128)(2,1)S(1)}, bf16[48,6144]{1,0:T(8,128)(2,1)S(1)}, u32[]{:S(2)}, u32[]{:S(2)}) collective-permute-start(bf16[48,6144]{1,0:T(8,128)(2,1)S(1)} %get-tuple-element.16), channel_id=1, source_target_pairs={{0,1},{1,2},{2,3},{3,0},{4,5},{5,6},{6,7},{7,4},{8,9},{9,10},{10,1... | collective-permute-start | bytes 1769480 | tf_op jit(solution)/shard_map/ppermute | solution.py:130
  104.1 17.6 %collective-permute-start.25 = (bf16[48,6144]{1,0:T(8,128)(2,1)S(1)}, bf16[48,6144]{1,0:T(8,128)(2,1)S(1)}, u32[]{:S(2)}, u32[]{:S(2)}) collective-permute-start(bf16[48,6144]{1,0:T(8,128)(2,1)S(1)} %get-tuple-element.17), channel_id=1, source_target_pairs={{0,4},{1,5},{2,6},{3,7},{4,8},{5,9},{6,10},{7,11},{8,12},{9,13},{1... | collective-permute-start | bytes 1769480 | tf_op jit(solution)/shard_map/ppermute | solution.py:130
  104.2 27.8 %collective-permute-start.23 = (bf16[72,6144]{1,0:T(8,128)(2,1)S(1)}, bf16[72,6144]{1,0:T(8,128)(2,1)S(1)}, u32[]{:S(2)}, u32[]{:S(2)}) collective-permute-start(bf16[72,6144]{1,0:T(8,128)(2,1)S(1)} %pad_maximum_fusion.3), channel_id=1, source_target_pairs={{0,12},{1,13},{2,14},{3,15},{4,0},{5,1},{6,2},{7,3},{8,4},{9,5},{1... | collective-permute-start | bytes 2654216 | tf_op jit(solution)/shard_map/ppermute | solution.py:130
  127.6 18.1 %collective-permute-start.34 = (bf16[72,6144]{1,0:T(8,128)(2,1)S(1)}, bf16[72,6144]{1,0:T(8,128)(2,1)S(1)}, u32[]{:S(2)}, u32[]{:S(2)}) collective-permute-start(bf16[72,6144]{1,0:T(8,128)(2,1)S(1)} %pad_maximum_fusion.4), channel_id=1, source_target_pairs={{0,3},{1,0},{2,1},{3,2},{4,7},{5,4},{6,5},{7,6},{8,11},{9,8},{10,9... | collective-permute-start | bytes 2654216 | tf_op jit(solution)/shard_map/ppermute | solution.py:130
  130.3 15.6 %collective-permute-start.29 = (bf16[24,6144]{1,0:T(8,128)(2,1)S(1)}, bf16[24,6144]{1,0:T(8,128)(2,1)S(1)}, u32[]{:S(2)}, u32[]{:S(2)}) collective-permute-start(bf16[24,6144]{1,0:T(8,128)(2,1)S(1)} %get-tuple-element.25), channel_id=1, source_target_pairs={{0,4},{1,5},{2,6},{3,7},{4,8},{5,9},{6,10},{7,11},{8,12},{9,13},{1... | collective-permute-start | bytes 884744 | tf_op jit(solution)/shard_map/ppermute | solution.py:130
  132.0 13.9 %collective-permute-start.31 = (bf16[24,6144]{1,0:T(8,128)(2,1)S(1)}, bf16[24,6144]{1,0:T(8,128)(2,1)S(1)}, u32[]{:S(2)}, u32[]{:S(2)}) collective-permute-start(bf16[24,6144]{1,0:T(8,128)(2,1)S(1)} %get-tuple-element.28), channel_id=1, source_target_pairs={{0,12},{1,13},{2,14},{3,15},{4,0},{5,1},{6,2},{7,3},{8,4},{9,5},{1... | collective-permute-start | bytes 884744 | tf_op jit(solution)/shard_map/ppermute | solution.py:130
  145.9 20.9 %collective-permute-start.37 = (bf16[48,6144]{1,0:T(8,128)(2,1)S(1)}, bf16[48,6144]{1,0:T(8,128)(2,1)S(1)}, u32[]{:S(2)}, u32[]{:S(2)}) collective-permute-start(bf16[48,6144]{1,0:T(8,128)(2,1)S(1)} %get-tuple-element.19), channel_id=1, source_target_pairs={{0,1},{1,2},{2,3},{3,0},{4,5},{5,6},{6,7},{7,4},{8,9},{9,10},{10,1... | collective-permute-start | bytes 1769480 | tf_op jit(solution)/shard_map/ppermute | solution.py:130
  153.9 13.2 %collective-permute-start.32 = (bf16[24,6144]{1,0:T(8,128)(2,1)S(1)}, bf16[24,6144]{1,0:T(8,128)(2,1)S(1)}, u32[]{:S(2)}, u32[]{:S(2)}) collective-permute-start(bf16[24,6144]{1,0:T(8,128)(2,1)S(1)} %get-tuple-element.32), channel_id=1, source_target_pairs={{0,2},{1,3},{2,0},{3,1},{4,6},{5,7},{6,4},{7,5},{8,10},{9,11},{10,... | collective-permute-start | bytes 884744 | tf_op jit(solution)/shard_map/ppermute | solution.py:130
  158.6 18.1 %collective-permute-start.43 = (bf16[24,6144]{1,0:T(8,128)(2,1)S(1)}, bf16[24,6144]{1,0:T(8,128)(2,1)S(1)}, u32[]{:S(2)}, u32[]{:S(2)}) collective-permute-start(bf16[24,6144]{1,0:T(8,128)(2,1)S(1)} %get-tuple-element.30), channel_id=1, source_target_pairs={{0,8},{1,9},{2,10},{3,11},{4,12},{5,13},{6,14},{7,15},{8,0},{9,1},... | collective-permute-start | bytes 884744 | tf_op jit(solution)/shard_map/ppermute | solution.py:130
  184.5 19.7 %collective-permute-start.47 = (bf16[96,3072]{1,0:T(8,128)(2,1)S(1)}, bf16[96,3072]{1,0:T(8,128)(2,1)S(1)}, u32[]{:S(2)}, u32[]{:S(2)}) collective-permute-start(bf16[96,3072]{1,0:T(8,128)(2,1)S(1)} %pad_maximum_fusion.7), channel_id=1, source_target_pairs={{0,16},{16,0},{32,48},{48,32},{64,80},{80,64},{96,112},{112,96},{1... | collective-permute-start | bytes 1769480 | tf_op jit(solution)/shard_map/ppermute | solution.py:122
  (32 other events, 331.3 us)

commit v4 on v2

--- a/solution.py
+++ b/solution.py
@@ -12,7 +12,7 @@
 
 
 PAD = 8
-CHUNK = 512
+CHUNK = 1536
 MIX = 1024
 
 
@@ -96,21 +96,21 @@
         held_ref[start : start + ref.shape[0], :] = ref[...]
         start += ref.shape[0]
 
+    tokens = hidden_ref.shape[0]
+
     @pl.loop(0, half // MIX)
     def _(step):
         rows = held_ref[:, pl.ds(pl.multiple_of(step * MIX, MIX), MIX)]
+        terms = lax.dot_general(
+            weight_ref[...], rows, (((0,), (0,)), ((), ())), preferred_element_type=jnp.float32
+        )
         for side in range(2):
             columns = pl.ds(pl.multiple_of(side * half + step * MIX, MIX), MIX)
-            total = hidden_ref[:, columns].astype(jnp.float32)
             mixed = 0.0
             for term in (2, 1, 0):
-                mixed = mixed + lax.dot_general(
-                    weight_ref[side, term],
-                    rows,
-                    (((0,), (0,)), ((), ())),
-                    preferred_element_type=jnp.float32,
-                )
-            out_ref[:, columns] = (total + mixed).astype(jnp.bfloat16)
+                first = (3 * side + term) * tokens
+                mixed = mixed + terms[first : first + tokens]
+            out_ref[:, columns] = (hidden_ref[:, columns].astype(jnp.float32) + mixed).astype(jnp.bfloat16)
 
 
 def along_x(value, step):
@@ -237,6 +237,7 @@
         compiler_params=pltpu.CompilerParams(vmem_limit_bytes=4 * 1024 * 1024),
     name="gates",
     )(normed, router_weight.T, ids)
+    weights = weights.transpose(2, 0, 1, 3).reshape(weights.shape[2], -1)
     gate_local = gate_proj[0]
     up_local = up_proj[0]
     down_local = down_proj[0]

time: 196 us -> 194 us (0.990)
  transfers between devices with their start and end apart: 48 -> 48, of which waited for: 23 -> 24; matrix products, arithmetic and copies ran while one was open for 7% -> 7% of each run, Pallas kernels for 0% -> 0%
where the time goes in v4:
time: 194 us
  waiting for transfers between devices  98.1 us (51%)
  starting transfers between devices  68.4 us (35%)
  matrix products  17.2 us (9%)
  Pallas kernels  3.7 us (2%)
  local copies, waits for them, and re-layouts  3.19 us (2%)
  other arithmetic  2.85 us (1%)
    ppermute x40, waiting for transfers between devices, shift(): lax.ppermute(value, 'hidden', [(i, target(i)) for i in range(RING * RING)])  89 us
    ppermute x40, starting transfers between devices, shift(): lax.ppermute(value, 'hidden', [(i, target(i)) for i in range(RING * RING)])  42.3 us
    ppermute x2, starting transfers between devices, other_core(): return lax.ppermute(value, 'expert', [(i, i ^ 1) for i in range(2 * RING)])  19.9 us
    ppermute x6, waiting for transfers between devices, along_x(): return lax.ppermute(value, 'expert', pairs)  6.71 us
    dot_general x4, matrix products, product(): jnp.dot(jnp.concatenate(value, axis=0), down, preferred_element_type=jnp....  6.49 us
    ppermute x6, starting transfers between devices, along_x(): return lax.ppermute(value, 'expert', pairs)  6.22 us
    dot_general x3, matrix products, per_device(): upper = jnp.dot(value, up_local, preferred_element_type=jnp.float32)  5.41 us
    dot_general x3, matrix products, per_device(): gate = jnp.dot(value, gate_local, preferred_element_type=jnp.float32)  5.34 us
  transfers between devices with their start and end apart: 48, of which 24 were waited for; matrix products, arithmetic and copies ran while one was open for 7% of the time, Pallas kernels for 0%

profile of v4, /device:TPU:1, one launch (start us, length us, event | category | flops | bytes accessed | tf_op | source)
XLA Modules:
  0.0 194.3 jit_solution(7185982787428168710)
XLA Ops:
  18.4 3.0 %collective-permute-done.2 = bf16[24,6144]{1,0:T(8,128)(2,1)S(1)} collective-permute-done((bf16[24,6144]{1,0:T(8,128)(2,1)S(1)}, bf16[24,6144]{1,0:T(8,128)(2,1)S(1)}, u32[]{:S(2)}, u32[]{:S(2)}) %collective-permute-start.2) | collective-permute-done | bytes 294944 | tf_op jit(solution)/shard_map/ppermute | solution.py:130
  21.5 2.8 %collective-permute-start.14 = (bf16[72,6144]{1,0:T(8,128)(2,1)S(1)}, bf16[72,6144]{1,0:T(8,128)(2,1)S(1)}, u32[]{:S(2)}, u32[]{:S(2)}) collective-permute-start(bf16[72,6144]{1,0:T(8,128)(2,1)S(1)} %pad_maximum_fusion.1), channel_id=1, source_target_pairs={{0,3},{1,0},{2,1},{3,2},{4,7},{5,4},{6,5},{7,6},{8,11},{9,8},{10,9... | collective-permute-start | bytes 2654216 | tf_op jit(solution)/shard_map/ppermute | solution.py:130
  29.6 18.2 %collective-permute-done.10 = bf16[24,3072]{1,0:T(8,128)(2,1)S(1)} collective-permute-done((bf16[24,3072]{1,0:T(8,128)(2,1)S(1)}, bf16[24,3072]{1,0:T(8,128)(2,1)S(1)}, u32[]{:S(2)}, u32[]{:S(2)}) %collective-permute-start.10) | collective-permute-done | bytes 147488 | tf_op jit(solution)/shard_map/ppermute | solution.py:130
  53.7 2.3 %collective-permute-done.11 = bf16[24,3072]{1,0:T(8,128)(2,1)S(1)} collective-permute-done((bf16[24,3072]{1,0:T(8,128)(2,1)S(1)}, bf16[24,3072]{1,0:T(8,128)(2,1)S(1)}, u32[]{:S(2)}, u32[]{:S(2)}) %collective-permute-start.11) | collective-permute-done | bytes 147488 | tf_op jit(solution)/shard_map/ppermute | solution.py:130
  56.1 2.9 %collective-permute-start.15 = (bf16[24,6144]{1,0:T(8,128)(2,1)S(1)}, bf16[24,6144]{1,0:T(8,128)(2,1)S(1)}, u32[]{:S(2)}, u32[]{:S(2)}) collective-permute-start(bf16[24,6144]{1,0:T(8,128)(2,1)S(1)} %constant_dynamic-update-slice_fusion), channel_id=1, source_target_pairs={{0,3},{1,0},{2,1},{3,2},{4,7},{5,4},{6,5},{7,6},{8,11},{9,8},{10,9... | collective-permute-start | bytes 884744 | tf_op jit(solution)/shard_map/ppermute | solution.py:130
  63.4 6.7 %collective-permute-done.22 = bf16[24,6144]{1,0:T(8,128)(2,1)S(1)} collective-permute-done((bf16[24,6144]{1,0:T(8,128)(2,1)S(1)}, bf16[24,6144]{1,0:T(8,128)(2,1)S(1)}, u32[]{:S(2)}, u32[]{:S(2)}) %collective-permute-start.22) | collective-permute-done | bytes 294944 | tf_op jit(solution)/shard_map/ppermute | solution.py:130
  70.1 3.1 %collective-permute-start.20 = (bf16[24,6144]{1,0:T(8,128)(2,1)S(1)}, bf16[24,6144]{1,0:T(8,128)(2,1)S(1)}, u32[]{:S(2)}, u32[]{:S(2)}) collective-permute-start(bf16[24,6144]{1,0:T(8,128)(2,1)S(1)} %constant_dynamic-update-slice_fusion.2), channel_id=1, source_target_pairs={{0,12},{1,13},{2,14},{3,15},{4,0},{5,1},{6,2},{7,3},{8,4},{9,5},{1... | collective-permute-start | bytes 884744 | tf_op jit(solution)/shard_map/ppermute | solution.py:130
  73.7 6.6 %collective-permute-done.23 = bf16[24,6144]{1,0:T(8,128)(2,1)S(1)} collective-permute-done((bf16[24,6144]{1,0:T(8,128)(2,1)S(1)}, bf16[24,6144]{1,0:T(8,128)(2,1)S(1)}, u32[]{:S(2)}, u32[]{:S(2)}) %collective-permute-start.23) | collective-permute-done | bytes 294944 | tf_op jit(solution)/shard_map/ppermute | solution.py:130
  80.4 2.6 %fusion.10 = f32[384,512]{1,0:T(8,128)S(1)} fusion(bf16[384,6144]{1,0:T(8,128)(2,1)S(1)} %constant_dynamic-update-slice_fusion.8, bf16[1,6144,512]{2,1,0:T(8,128)(2,1)S(1)} %copy-done.3), kind=kOutput, calls=%fused_computation.14 | convolution fusion | flops 2415919104 | bytes 11796480 | tf_op jit(solution)/shard_map/dot_general | solution.py:255
  83.0 2.6 %multiply_convert_fusion = bf16[384,512]{1,0:T(8,128)(2,1)S(1)} fusion(f32[384,512]{1,0:T(8,128)S(1)} %fusion.10, bf16[384,6144]{1,0:T(8,128)(2,1)S(1)} %constant_dynamic-update-slice_fusion.8, bf16[1,6144,512]{2,1,0:T(8,128)(2,1)S(1)} %bitcast.95), kind=kOutput, calls=%fused_computation.29 | convolution fusion | flops 2417098752 | bytes 12189696 | tf_op jit(solution)/shard_map/dot_general | solution.py:256
  85.8 2.8 %convolution_convert_fusion = bf16[384,6144]{1,0:T(8,128)(2,1)S(1)} fusion(bf16[1,512,6144]{2,1,0:T(8,128)(2,1)S(1)} %bitcast.78, bf16[96,512]{1,0:T(8,128)(2,1)S(1)} %bitcast.91, bf16[288,512]{1,0:T(8,128)(2,1)S(1)} %bitcast.81), kind=kOutput, calls=%fused_computation | convolution fusion | flops 2419064832 | bytes 11403264 | tf_op jit(solution)/shard_map/dot_general | solution.py:163
  90.8 2.7 %collective-permute-start.21 = (bf16[48,6144]{1,0:T(8,128)(2,1)S(1)}, bf16[48,6144]{1,0:T(8,128)(2,1)S(1)}, u32[]{:S(2)}, u32[]{:S(2)}) collective-permute-start(bf16[48,6144]{1,0:T(8,128)(2,1)S(1)} %pad_maximum_fusion.6), channel_id=1, source_target_pairs={{0,12},{1,13},{2,14},{3,15},{4,0},{5,1},{6,2},{7,3},{8,4},{9,5},{1... | collective-permute-start | bytes 1769480 | tf_op jit(solution)/shard_map/ppermute | solution.py:130
  93.7 5.4 %collective-permute-done.13 = bf16[48,6144]{1,0:T(8,128)(2,1)S(1)} collective-permute-done((bf16[48,6144]{1,0:T(8,128)(2,1)S(1)}, bf16[48,6144]{1,0:T(8,128)(2,1)S(1)}, u32[]{:S(2)}, u32[]{:S(2)}) %collective-permute-start.13) | collective-permute-done | bytes 589856 | tf_op jit(solution)/shard_map/ppermute | solution.py:130
  107.9 3.8 %collective-permute-done.28 = bf16[48,6144]{1,0:T(8,128)(2,1)S(1)} collective-permute-done((bf16[48,6144]{1,0:T(8,128)(2,1)S(1)}, bf16[48,6144]{1,0:T(8,128)(2,1)S(1)}, u32[]{:S(2)}, u32[]{:S(2)}) %collective-permute-start.28) | collective-permute-done | bytes 589856 | tf_op jit(solution)/shard_map/ppermute | solution.py:130
  116.2 4.8 %collective-permute-done.25 = bf16[72,6144]{1,0:T(8,128)(2,1)S(1)} collective-permute-done((bf16[72,6144]{1,0:T(8,128)(2,1)S(1)}, bf16[72,6144]{1,0:T(8,128)(2,1)S(1)}, u32[]{:S(2)}, u32[]{:S(2)}) %collective-permute-start.25) | collective-permute-done | bytes 884768 | tf_op jit(solution)/shard_map/ppermute | solution.py:130
  121.0 6.3 %collective-permute-done.26 = bf16[24,6144]{1,0:T(8,128)(2,1)S(1)} collective-permute-done((bf16[24,6144]{1,0:T(8,128)(2,1)S(1)}, bf16[24,6144]{1,0:T(8,128)(2,1)S(1)}, u32[]{:S(2)}, u32[]{:S(2)}) %collective-permute-start.26) | collective-permute-done | bytes 294944 | tf_op jit(solution)/shard_map/ppermute | solution.py:130
  127.7 4.3 %collective-permute-done.39 = bf16[48,6144]{1,0:T(8,128)(2,1)S(1)} collective-permute-done((bf16[48,6144]{1,0:T(8,128)(2,1)S(1)}, bf16[48,6144]{1,0:T(8,128)(2,1)S(1)}, u32[]{:S(2)}, u32[]{:S(2)}) %collective-permute-start.39) | collective-permute-done | bytes 589856 | tf_op jit(solution)/shard_map/ppermute | solution.py:130
  132.3 10.4 %collective-permute-done.29 = bf16[48,6144]{1,0:T(8,128)(2,1)S(1)} collective-permute-done((bf16[48,6144]{1,0:T(8,128)(2,1)S(1)}, bf16[48,6144]{1,0:T(8,128)(2,1)S(1)}, u32[]{:S(2)}, u32[]{:S(2)}) %collective-permute-start.29) | collective-permute-done | bytes 589856 | tf_op jit(solution)/shard_map/ppermute | solution.py:130
  142.7 3.3 %collective-permute-start.37 = (bf16[48,6144]{1,0:T(8,128)(2,1)S(1)}, bf16[48,6144]{1,0:T(8,128)(2,1)S(1)}, u32[]{:S(2)}, u32[]{:S(2)}) collective-permute-start(bf16[48,6144]{1,0:T(8,128)(2,1)S(1)} %pad_maximum_fusion.8), channel_id=1, source_target_pairs={{0,3},{1,0},{2,1},{3,2},{4,7},{5,4},{6,5},{7,6},{8,11},{9,8},{10,9... | collective-permute-start | bytes 1769480 | tf_op jit(solution)/shard_map/ppermute | solution.py:130
  147.8 5.0 %collective-permute-done.37 = bf16[48,6144]{1,0:T(8,128)(2,1)S(1)} collective-permute-done((bf16[48,6144]{1,0:T(8,128)(2,1)S(1)}, bf16[48,6144]{1,0:T(8,128)(2,1)S(1)}, u32[]{:S(2)}, u32[]{:S(2)}) %collective-permute-start.37) | collective-permute-done | bytes 589856 | tf_op jit(solution)/shard_map/ppermute | solution.py:130
  153.2 3.5 %collective-permute-start.31 = (bf16[24,6144]{1,0:T(8,128)(2,1)S(1)}, bf16[24,6144]{1,0:T(8,128)(2,1)S(1)}, u32[]{:S(2)}, u32[]{:S(2)}) collective-permute-start(bf16[24,6144]{1,0:T(8,128)(2,1)S(1)} %get-tuple-element.36), channel_id=1, source_target_pairs={{0,3},{1,0},{2,1},{3,2},{4,7},{5,4},{6,5},{7,6},{8,11},{9,8},{10,9... | collective-permute-start | bytes 884744 | tf_op jit(solution)/shard_map/ppermute | solution.py:130
  158.7 6.5 %collective-permute-done.43 = bf16[24,6144]{1,0:T(8,128)(2,1)S(1)} collective-permute-done((bf16[24,6144]{1,0:T(8,128)(2,1)S(1)}, bf16[24,6144]{1,0:T(8,128)(2,1)S(1)}, u32[]{:S(2)}, u32[]{:S(2)}) %collective-permute-start.43) | collective-permute-done | bytes 294944 | tf_op jit(solution)/shard_map/ppermute | solution.py:130
  167.6 3.6 %collective-permute-done.46.across_ref = bf16[24,3072]{1,0:T(8,128)(2,1)S(1)} collective-permute-done((bf16[24,3072]{1,0:T(8,128)(2,1)S(1)}, bf16[24,3072]{1,0:T(8,128)(2,1)S(1)}, u32[]{:S(2)}, u32[]{:S(2)}) %collective-permute-start.46) | collective-permute-done | bytes 147488 | tf_op jit(solution)/shard_map/ppermute | solution.py:118
  172.7 18.5 %collective-permute-start.47 = (bf16[96,3072]{1,0:T(8,128)(2,1)S(1)}, bf16[96,3072]{1,0:T(8,128)(2,1)S(1)}, u32[]{:S(2)}, u32[]{:S(2)}) collective-permute-start(bf16[96,3072]{1,0:T(8,128)(2,1)S(1)} %pad_maximum_fusion.9), channel_id=1, source_target_pairs={{0,16},{16,0},{32,48},{48,32},{64,80},{80,64},{96,112},{112,96},{1... | collective-permute-start | bytes 1769480 | tf_op jit(solution)/shard_map/ppermute | solution.py:122
  (177 shorter events, 61.8 us)
Async XLA Ops:
  21.5 51.8 %collective-permute-start.14 = (bf16[72,6144]{1,0:T(8,128)(2,1)S(1)}, bf16[72,6144]{1,0:T(8,128)(2,1)S(1)}, u32[]{:S(2)}, u32[]{:S(2)}) collective-permute-start(bf16[72,6144]{1,0:T(8,128)(2,1)S(1)} %pad_maximum_fusion.1), channel_id=1, source_target_pairs={{0,3},{1,0},{2,1},{3,2},{4,7},{5,4},{6,5},{7,6},{8,11},{9,8},{10,9... | collective-permute-start | bytes 2654216 | tf_op jit(solution)/shard_map/ppermute | solution.py:130
  24.3 38.9 %collective-permute-start.12 = (bf16[72,6144]{1,0:T(8,128)(2,1)S(1)}, bf16[72,6144]{1,0:T(8,128)(2,1)S(1)}, u32[]{:S(2)}, u32[]{:S(2)}) collective-permute-start(bf16[72,6144]{1,0:T(8,128)(2,1)S(1)} %pad_maximum_fusion.1), channel_id=1, source_target_pairs={{0,1},{1,2},{2,3},{3,0},{4,5},{5,6},{6,7},{7,4},{8,9},{9,10},{10,1... | collective-permute-start | bytes 2654216 | tf_op jit(solution)/shard_map/ppermute | solution.py:130
  24.9 48.7 %collective-permute-start.17 = (bf16[72,6144]{1,0:T(8,128)(2,1)S(1)}, bf16[72,6144]{1,0:T(8,128)(2,1)S(1)}, u32[]{:S(2)}, u32[]{:S(2)}) collective-permute-start(bf16[72,6144]{1,0:T(8,128)(2,1)S(1)} %pad_maximum_fusion.2), channel_id=1, source_target_pairs={{0,4},{1,5},{2,6},{3,7},{4,8},{5,9},{6,10},{7,11},{8,12},{9,13},{1... | collective-permute-start | bytes 2654216 | tf_op jit(solution)/shard_map/ppermute | solution.py:130
  26.3 54.0 %collective-permute-start.19 = (bf16[72,6144]{1,0:T(8,128)(2,1)S(1)}, bf16[72,6144]{1,0:T(8,128)(2,1)S(1)}, u32[]{:S(2)}, u32[]{:S(2)}) collective-permute-start(bf16[72,6144]{1,0:T(8,128)(2,1)S(1)} %pad_maximum_fusion.2), channel_id=1, source_target_pairs={{0,12},{1,13},{2,14},{3,15},{4,0},{5,1},{6,2},{7,3},{8,4},{9,5},{1... | collective-permute-start | bytes 2654216 | tf_op jit(solution)/shard_map/ppermute | solution.py:130
  29.6 18.2 %collective-permute-start.10 = (bf16[24,3072]{1,0:T(8,128)(2,1)S(1)}, bf16[24,3072]{1,0:T(8,128)(2,1)S(1)}, u32[]{:S(2)}, u32[]{:S(2)}) collective-permute-start(bf16[24,3072]{1,0:T(8,128)(2,1)S(1)} %slice.358), channel_id=1, source_target_pairs={{0,1},{1,2},{2,3},{3,0},{4,5},{5,6},{6,7},{7,4},{8,9},{9,10},{10,1... | collective-permute-start | bytes 442376 | tf_op jit(solution)/shard_map/ppermute | solution.py:130
  56.1 17.5 %collective-permute-start.15 = (bf16[24,6144]{1,0:T(8,128)(2,1)S(1)}, bf16[24,6144]{1,0:T(8,128)(2,1)S(1)}, u32[]{:S(2)}, u32[]{:S(2)}) collective-permute-start(bf16[24,6144]{1,0:T(8,128)(2,1)S(1)} %constant_dynamic-update-slice_fusion), channel_id=1, source_target_pairs={{0,3},{1,0},{2,1},{3,2},{4,7},{5,4},{6,5},{7,6},{8,11},{9,8},{10,9... | collective-permute-start | bytes 884744 | tf_op jit(solution)/shard_map/ppermute | solution.py:130
  89.0 10.7 %collective-permute-start.16 = (bf16[48,6144]{1,0:T(8,128)(2,1)S(1)}, bf16[48,6144]{1,0:T(8,128)(2,1)S(1)}, u32[]{:S(2)}, u32[]{:S(2)}) collective-permute-start(bf16[48,6144]{1,0:T(8,128)(2,1)S(1)} %pad_maximum_fusion.5), channel_id=1, source_target_pairs={{0,3},{1,0},{2,1},{3,2},{4,7},{5,4},{6,5},{7,6},{8,11},{9,8},{10,9... | collective-permute-start | bytes 1769480 | tf_op jit(solution)/shard_map/ppermute | solution.py:130
  90.7 11.3 %collective-permute-start.18 = (bf16[48,6144]{1,0:T(8,128)(2,1)S(1)}, bf16[48,6144]{1,0:T(8,128)(2,1)S(1)}, u32[]{:S(2)}, u32[]{:S(2)}) collective-permute-start(bf16[48,6144]{1,0:T(8,128)(2,1)S(1)} %slice.363), channel_id=1, source_target_pairs={{0,4},{1,5},{2,6},{3,7},{4,8},{5,9},{6,10},{7,11},{8,12},{9,13},{1... | collective-permute-start | bytes 1769480 | tf_op jit(solution)/shard_map/ppermute | solution.py:130
  90.8 11.3 %collective-permute-start.21 = (bf16[48,6144]{1,0:T(8,128)(2,1)S(1)}, bf16[48,6144]{1,0:T(8,128)(2,1)S(1)}, u32[]{:S(2)}, u32[]{:S(2)}) collective-permute-start(bf16[48,6144]{1,0:T(8,128)(2,1)S(1)} %pad_maximum_fusion.6), channel_id=1, source_target_pairs={{0,12},{1,13},{2,14},{3,15},{4,0},{5,1},{6,2},{7,3},{8,4},{9,5},{1... | collective-permute-start | bytes 1769480 | tf_op jit(solution)/shard_map/ppermute | solution.py:130
  93.5 18.2 %collective-permute-start.28 = (bf16[48,6144]{1,0:T(8,128)(2,1)S(1)}, bf16[48,6144]{1,0:T(8,128)(2,1)S(1)}, u32[]{:S(2)}, u32[]{:S(2)}) collective-permute-start(bf16[48,6144]{1,0:T(8,128)(2,1)S(1)} %get-tuple-element.19), channel_id=1, source_target_pairs={{0,4},{1,5},{2,6},{3,7},{4,8},{5,9},{6,10},{7,11},{8,12},{9,13},{1... | collective-permute-start | bytes 1769480 | tf_op jit(solution)/shard_map/ppermute | solution.py:130
  99.1 14.3 %collective-permute-start.38 = (bf16[48,6144]{1,0:T(8,128)(2,1)S(1)}, bf16[48,6144]{1,0:T(8,128)(2,1)S(1)}, u32[]{:S(2)}, u32[]{:S(2)}) collective-permute-start(bf16[48,6144]{1,0:T(8,128)(2,1)S(1)} %get-tuple-element.17), channel_id=1, source_target_pairs={{0,1},{1,2},{2,3},{3,0},{4,5},{5,6},{6,7},{7,4},{8,9},{9,10},{10,1... | collective-permute-start | bytes 1769480 | tf_op jit(solution)/shard_map/ppermute | solution.py:130
  99.7 15.5 %collective-permute-start.35 = (bf16[72,6144]{1,0:T(8,128)(2,1)S(1)}, bf16[72,6144]{1,0:T(8,128)(2,1)S(1)}, u32[]{:S(2)}, u32[]{:S(2)}) collective-permute-start(bf16[72,6144]{1,0:T(8,128)(2,1)S(1)} %pad_maximum_fusion.4), channel_id=1, source_target_pairs={{0,3},{1,0},{2,1},{3,2},{4,7},{5,4},{6,5},{7,6},{8,11},{9,8},{10,9... | collective-permute-start | bytes 2654216 | tf_op jit(solution)/shard_map/ppermute | solution.py:130
  102.0 19.1 %collective-permute-start.25 = (bf16[72,6144]{1,0:T(8,128)(2,1)S(1)}, bf16[72,6144]{1,0:T(8,128)(2,1)S(1)}, u32[]{:S(2)}, u32[]{:S(2)}) collective-permute-start(bf16[72,6144]{1,0:T(8,128)(2,1)S(1)} %pad_maximum_fusion.3), channel_id=1, source_target_pairs={{0,12},{1,13},{2,14},{3,15},{4,0},{5,1},{6,2},{7,3},{8,4},{9,5},{1... | collective-permute-start | bytes 2654216 | tf_op jit(solution)/shard_map/ppermute | solution.py:130
  102.1 44.2 %collective-permute-start.34 = (bf16[24,6144]{1,0:T(8,128)(2,1)S(1)}, bf16[24,6144]{1,0:T(8,128)(2,1)S(1)}, u32[]{:S(2)}, u32[]{:S(2)}) collective-permute-start(bf16[24,6144]{1,0:T(8,128)(2,1)S(1)} %get-tuple-element.11), channel_id=1, source_target_pairs={{0,1},{1,2},{2,3},{3,0},{4,5},{5,6},{6,7},{7,4},{8,9},{9,10},{10,1... | collective-permute-start | bytes 884744 | tf_op jit(solution)/shard_map/ppermute | solution.py:130
  111.7 15.6 %collective-permute-start.26 = (bf16[24,6144]{1,0:T(8,128)(2,1)S(1)}, bf16[24,6144]{1,0:T(8,128)(2,1)S(1)}, u32[]{:S(2)}, u32[]{:S(2)}) collective-permute-start(bf16[24,6144]{1,0:T(8,128)(2,1)S(1)} %get-tuple-element.28), channel_id=1, source_target_pairs={{0,12},{1,13},{2,14},{3,15},{4,0},{5,1},{6,2},{7,3},{8,4},{9,5},{1... | collective-permute-start | bytes 884744 | tf_op jit(solution)/shard_map/ppermute | solution.py:130
  113.4 14.0 %collective-permute-start.36 = (bf16[24,6144]{1,0:T(8,128)(2,1)S(1)}, bf16[24,6144]{1,0:T(8,128)(2,1)S(1)}, u32[]{:S(2)}, u32[]{:S(2)}) collective-permute-start(bf16[24,6144]{1,0:T(8,128)(2,1)S(1)} %get-tuple-element.25), channel_id=1, source_target_pairs={{0,3},{1,0},{2,1},{3,2},{4,7},{5,4},{6,5},{7,6},{8,11},{9,8},{10,9... | collective-permute-start | bytes 884744 | tf_op jit(solution)/shard_map/ppermute | solution.py:130
  115.2 37.9 %collective-permute-start.24 = (bf16[24,6144]{1,0:T(8,128)(2,1)S(1)}, bf16[24,6144]{1,0:T(8,128)(2,1)S(1)}, u32[]{:S(2)}, u32[]{:S(2)}) collective-permute-start(bf16[24,6144]{1,0:T(8,128)(2,1)S(1)} %get-tuple-element.14), channel_id=1, source_target_pairs={{0,4},{1,5},{2,6},{3,7},{4,8},{5,9},{6,10},{7,11},{8,12},{9,13},{1... | collective-permute-start | bytes 884744 | tf_op jit(solution)/shard_map/ppermute | solution.py:130
  121.0 11.0 %collective-permute-start.39 = (bf16[48,6144]{1,0:T(8,128)(2,1)S(1)}, bf16[48,6144]{1,0:T(8,128)(2,1)S(1)}, u32[]{:S(2)}, u32[]{:S(2)}) collective-permute-start(bf16[48,6144]{1,0:T(8,128)(2,1)S(1)} %get-tuple-element.15), channel_id=1, source_target_pairs={{0,1},{1,2},{2,3},{3,0},{4,5},{5,6},{6,7},{7,4},{8,9},{9,10},{10,1... | collective-permute-start | bytes 1769480 | tf_op jit(solution)/shard_map/ppermute | solution.py:130
  127.3 19.0 %collective-permute-start.42 = (bf16[24,6144]{1,0:T(8,128)(2,1)S(1)}, bf16[24,6144]{1,0:T(8,128)(2,1)S(1)}, u32[]{:S(2)}, u32[]{:S(2)}) collective-permute-start(bf16[24,6144]{1,0:T(8,128)(2,1)S(1)} %get-tuple-element.26), channel_id=1, source_target_pairs={{0,1},{1,2},{2,3},{3,0},{4,5},{5,6},{6,7},{7,4},{8,9},{9,10},{10,1... | collective-permute-start | bytes 884744 | tf_op jit(solution)/shard_map/ppermute | solution.py:130
  127.4 15.4 %collective-permute-start.29 = (bf16[48,6144]{1,0:T(8,128)(2,1)S(1)}, bf16[48,6144]{1,0:T(8,128)(2,1)S(1)}, u32[]{:S(2)}, u32[]{:S(2)}) collective-permute-start(bf16[48,6144]{1,0:T(8,128)(2,1)S(1)} %get-tuple-element.16), channel_id=1, source_target_pairs={{0,4},{1,5},{2,6},{3,7},{4,8},{5,9},{6,10},{7,11},{8,12},{9,13},{1... | collective-permute-start | bytes 1769480 | tf_op jit(solution)/shard_map/ppermute | solution.py:130
  132.0 21.1 %collective-permute-start.32 = (bf16[24,6144]{1,0:T(8,128)(2,1)S(1)}, bf16[24,6144]{1,0:T(8,128)(2,1)S(1)}, u32[]{:S(2)}, u32[]{:S(2)}) collective-permute-start(bf16[24,6144]{1,0:T(8,128)(2,1)S(1)} %get-tuple-element.27), channel_id=1, source_target_pairs={{0,4},{1,5},{2,6},{3,7},{4,8},{5,9},{6,10},{7,11},{8,12},{9,13},{1... | collective-permute-start | bytes 884744 | tf_op jit(solution)/shard_map/ppermute | solution.py:130
  153.1 12.6 %collective-permute-start.30 = (bf16[24,6144]{1,0:T(8,128)(2,1)S(1)}, bf16[24,6144]{1,0:T(8,128)(2,1)S(1)}, u32[]{:S(2)}, u32[]{:S(2)}) collective-permute-start(bf16[24,6144]{1,0:T(8,128)(2,1)S(1)} %get-tuple-element.35), channel_id=1, source_target_pairs={{0,1},{1,2},{2,3},{3,0},{4,5},{5,6},{6,7},{7,4},{8,9},{9,10},{10,1... | collective-permute-start | bytes 884744 | tf_op jit(solution)/shard_map/ppermute | solution.py:130
  153.2 12.5 %collective-permute-start.31 = (bf16[24,6144]{1,0:T(8,128)(2,1)S(1)}, bf16[24,6144]{1,0:T(8,128)(2,1)S(1)}, u32[]{:S(2)}, u32[]{:S(2)}) collective-permute-start(bf16[24,6144]{1,0:T(8,128)(2,1)S(1)} %get-tuple-element.36), channel_id=1, source_target_pairs={{0,3},{1,0},{2,1},{3,2},{4,7},{5,4},{6,5},{7,6},{8,11},{9,8},{10,9... | collective-permute-start | bytes 884744 | tf_op jit(solution)/shard_map/ppermute | solution.py:130
  172.7 20.1 %collective-permute-start.47 = (bf16[96,3072]{1,0:T(8,128)(2,1)S(1)}, bf16[96,3072]{1,0:T(8,128)(2,1)S(1)}, u32[]{:S(2)}, u32[]{:S(2)}) collective-permute-start(bf16[96,3072]{1,0:T(8,128)(2,1)S(1)} %pad_maximum_fusion.9), channel_id=1, source_target_pairs={{0,16},{16,0},{32,48},{48,32},{64,80},{80,64},{96,112},{112,96},{1... | collective-permute-start | bytes 1769480 | tf_op jit(solution)/shard_map/ppermute | solution.py:122
  (32 other events, 315.1 us)

commit v5 on v4

--- a/solution.py
+++ b/solution.py
@@ -140,10 +140,8 @@
     below, above = [shift(near, second, 1)], [shift(near, second, -1)]
     below.append(shift(far, second, 1))
     above.append(shift(far, second, -1))
-    last = [
-        shift(below[0][: 2 * rows], second, 1),
-        shift(jnp.concatenate([above[0][2 * rows :], above[1]], axis=0), second, -1),
-    ]
+    last = [shift(below[0][: 2 * rows], second, 1)]
+    last.append(shift(jnp.concatenate([above[0][2 * rows :], above[1]], axis=0), second, -1))
     return [near, far], below + above, last
 
 

time: 194 us -> 194 us (level)
  no operation moved by 1% of the time
where the time goes in v5:
time: 194 us
  waiting for transfers between devices  98.1 us (51%)
  starting transfers between devices  68.4 us (35%)
  matrix products  17.2 us (9%)
  Pallas kernels  3.7 us (2%)
  local copies, waits for them, and re-layouts  3.19 us (2%)
  other arithmetic  2.85 us (1%)
    ppermute x40, waiting for transfers between devices, shift(): lax.ppermute(value, 'hidden', [(i, target(i)) for i in range(RING * RING)])  89 us
    ppermute x40, starting transfers between devices, shift(): lax.ppermute(value, 'hidden', [(i, target(i)) for i in range(RING * RING)])  42.3 us
    ppermute x2, starting transfers between devices, other_core(): return lax.ppermute(value, 'expert', [(i, i ^ 1) for i in range(2 * RING)])  19.9 us
    ppermute x6, waiting for transfers between devices, along_x(): return lax.ppermute(value, 'expert', pairs)  6.71 us
    dot_general x4, matrix products, product(): jnp.dot(jnp.concatenate(value, axis=0), down, preferred_element_type=jnp....  6.49 us
    ppermute x6, starting transfers between devices, along_x(): return lax.ppermute(value, 'expert', pairs)  6.22 us
    dot_general x3, matrix products, per_device(): upper = jnp.dot(value, up_local, preferred_element_type=jnp.float32)  5.41 us
    dot_general x3, matrix products, per_device(): gate = jnp.dot(value, gate_local, preferred_element_type=jnp.float32)  5.34 us
  transfers between devices with their start and end apart: 48, of which 24 were waited for; matrix products, arithmetic and copies ran while one was open for 7% of the time, Pallas kernels for 0%

profile of v5, /device:TPU:1, one launch (start us, length us, event | category | flops | bytes accessed | tf_op | source)
XLA Modules:
  0.0 194.3 jit_solution(7185982787428168710)
XLA Ops:
  18.4 3.0 %collective-permute-done.2 = bf16[24,6144]{1,0:T(8,128)(2,1)S(1)} collective-permute-done((bf16[24,6144]{1,0:T(8,128)(2,1)S(1)}, bf16[24,6144]{1,0:T(8,128)(2,1)S(1)}, u32[]{:S(2)}, u32[]{:S(2)}) %collective-permute-start.2) | collective-permute-done | bytes 294944 | tf_op jit(solution)/shard_map/ppermute | solution.py:130
  21.5 2.8 %collective-permute-start.14 = (bf16[72,6144]{1,0:T(8,128)(2,1)S(1)}, bf16[72,6144]{1,0:T(8,128)(2,1)S(1)}, u32[]{:S(2)}, u32[]{:S(2)}) collective-permute-start(bf16[72,6144]{1,0:T(8,128)(2,1)S(1)} %pad_maximum_fusion.1), channel_id=1, source_target_pairs={{0,3},{1,0},{2,1},{3,2},{4,7},{5,4},{6,5},{7,6},{8,11},{9,8},{10,9... | collective-permute-start | bytes 2654216 | tf_op jit(solution)/shard_map/ppermute | solution.py:130
  29.6 18.2 %collective-permute-done.10 = bf16[24,3072]{1,0:T(8,128)(2,1)S(1)} collective-permute-done((bf16[24,3072]{1,0:T(8,128)(2,1)S(1)}, bf16[24,3072]{1,0:T(8,128)(2,1)S(1)}, u32[]{:S(2)}, u32[]{:S(2)}) %collective-permute-start.10) | collective-permute-done | bytes 147488 | tf_op jit(solution)/shard_map/ppermute | solution.py:130
  53.7 2.3 %collective-permute-done.11 = bf16[24,3072]{1,0:T(8,128)(2,1)S(1)} collective-permute-done((bf16[24,3072]{1,0:T(8,128)(2,1)S(1)}, bf16[24,3072]{1,0:T(8,128)(2,1)S(1)}, u32[]{:S(2)}, u32[]{:S(2)}) %collective-permute-start.11) | collective-permute-done | bytes 147488 | tf_op jit(solution)/shard_map/ppermute | solution.py:130
  56.1 2.9 %collective-permute-start.15 = (bf16[24,6144]{1,0:T(8,128)(2,1)S(1)}, bf16[24,6144]{1,0:T(8,128)(2,1)S(1)}, u32[]{:S(2)}, u32[]{:S(2)}) collective-permute-start(bf16[24,6144]{1,0:T(8,128)(2,1)S(1)} %constant_dynamic-update-slice_fusion), channel_id=1, source_target_pairs={{0,3},{1,0},{2,1},{3,2},{4,7},{5,4},{6,5},{7,6},{8,11},{9,8},{10,9... | collective-permute-start | bytes 884744 | tf_op jit(solution)/shard_map/ppermute | solution.py:130
  63.4 6.7 %collective-permute-done.22 = bf16[24,6144]{1,0:T(8,128)(2,1)S(1)} collective-permute-done((bf16[24,6144]{1,0:T(8,128)(2,1)S(1)}, bf16[24,6144]{1,0:T(8,128)(2,1)S(1)}, u32[]{:S(2)}, u32[]{:S(2)}) %collective-permute-start.22) | collective-permute-done | bytes 294944 | tf_op jit(solution)/shard_map/ppermute | solution.py:130
  70.1 3.1 %collective-permute-start.20 = (bf16[24,6144]{1,0:T(8,128)(2,1)S(1)}, bf16[24,6144]{1,0:T(8,128)(2,1)S(1)}, u32[]{:S(2)}, u32[]{:S(2)}) collective-permute-start(bf16[24,6144]{1,0:T(8,128)(2,1)S(1)} %constant_dynamic-update-slice_fusion.2), channel_id=1, source_target_pairs={{0,12},{1,13},{2,14},{3,15},{4,0},{5,1},{6,2},{7,3},{8,4},{9,5},{1... | collective-permute-start | bytes 884744 | tf_op jit(solution)/shard_map/ppermute | solution.py:130
  73.7 6.6 %collective-permute-done.23 = bf16[24,6144]{1,0:T(8,128)(2,1)S(1)} collective-permute-done((bf16[24,6144]{1,0:T(8,128)(2,1)S(1)}, bf16[24,6144]{1,0:T(8,128)(2,1)S(1)}, u32[]{:S(2)}, u32[]{:S(2)}) %collective-permute-start.23) | collective-permute-done | bytes 294944 | tf_op jit(solution)/shard_map/ppermute | solution.py:130
  80.4 2.6 %fusion.10 = f32[384,512]{1,0:T(8,128)S(1)} fusion(bf16[384,6144]{1,0:T(8,128)(2,1)S(1)} %constant_dynamic-update-slice_fusion.8, bf16[1,6144,512]{2,1,0:T(8,128)(2,1)S(1)} %copy-done.3), kind=kOutput, calls=%fused_computation.14 | convolution fusion | flops 2415919104 | bytes 11796480 | tf_op jit(solution)/shard_map/dot_general | solution.py:253
  83.0 2.6 %multiply_convert_fusion = bf16[384,512]{1,0:T(8,128)(2,1)S(1)} fusion(f32[384,512]{1,0:T(8,128)S(1)} %fusion.10, bf16[384,6144]{1,0:T(8,128)(2,1)S(1)} %constant_dynamic-update-slice_fusion.8, bf16[1,6144,512]{2,1,0:T(8,128)(2,1)S(1)} %bitcast.95), kind=kOutput, calls=%fused_computation.29 | convolution fusion | flops 2417098752 | bytes 12189696 | tf_op jit(solution)/shard_map/dot_general | solution.py:254
  85.8 2.8 %convolution_convert_fusion = bf16[384,6144]{1,0:T(8,128)(2,1)S(1)} fusion(bf16[1,512,6144]{2,1,0:T(8,128)(2,1)S(1)} %bitcast.78, bf16[96,512]{1,0:T(8,128)(2,1)S(1)} %bitcast.91, bf16[288,512]{1,0:T(8,128)(2,1)S(1)} %bitcast.81), kind=kOutput, calls=%fused_computation | convolution fusion | flops 2419064832 | bytes 11403264 | tf_op jit(solution)/shard_map/dot_general | solution.py:161
  90.8 2.7 %collective-permute-start.21 = (bf16[48,6144]{1,0:T(8,128)(2,1)S(1)}, bf16[48,6144]{1,0:T(8,128)(2,1)S(1)}, u32[]{:S(2)}, u32[]{:S(2)}) collective-permute-start(bf16[48,6144]{1,0:T(8,128)(2,1)S(1)} %pad_maximum_fusion.6), channel_id=1, source_target_pairs={{0,12},{1,13},{2,14},{3,15},{4,0},{5,1},{6,2},{7,3},{8,4},{9,5},{1... | collective-permute-start | bytes 1769480 | tf_op jit(solution)/shard_map/ppermute | solution.py:130
  93.7 5.4 %collective-permute-done.13 = bf16[48,6144]{1,0:T(8,128)(2,1)S(1)} collective-permute-done((bf16[48,6144]{1,0:T(8,128)(2,1)S(1)}, bf16[48,6144]{1,0:T(8,128)(2,1)S(1)}, u32[]{:S(2)}, u32[]{:S(2)}) %collective-permute-start.13) | collective-permute-done | bytes 589856 | tf_op jit(solution)/shard_map/ppermute | solution.py:130
  107.9 3.8 %collective-permute-done.28 = bf16[48,6144]{1,0:T(8,128)(2,1)S(1)} collective-permute-done((bf16[48,6144]{1,0:T(8,128)(2,1)S(1)}, bf16[48,6144]{1,0:T(8,128)(2,1)S(1)}, u32[]{:S(2)}, u32[]{:S(2)}) %collective-permute-start.28) | collective-permute-done | bytes 589856 | tf_op jit(solution)/shard_map/ppermute | solution.py:130
  116.2 4.8 %collective-permute-done.25 = bf16[72,6144]{1,0:T(8,128)(2,1)S(1)} collective-permute-done((bf16[72,6144]{1,0:T(8,128)(2,1)S(1)}, bf16[72,6144]{1,0:T(8,128)(2,1)S(1)}, u32[]{:S(2)}, u32[]{:S(2)}) %collective-permute-start.25) | collective-permute-done | bytes 884768 | tf_op jit(solution)/shard_map/ppermute | solution.py:130
  121.0 6.3 %collective-permute-done.26 = bf16[24,6144]{1,0:T(8,128)(2,1)S(1)} collective-permute-done((bf16[24,6144]{1,0:T(8,128)(2,1)S(1)}, bf16[24,6144]{1,0:T(8,128)(2,1)S(1)}, u32[]{:S(2)}, u32[]{:S(2)}) %collective-permute-start.26) | collective-permute-done | bytes 294944 | tf_op jit(solution)/shard_map/ppermute | solution.py:130
  127.7 4.3 %collective-permute-done.39 = bf16[48,6144]{1,0:T(8,128)(2,1)S(1)} collective-permute-done((bf16[48,6144]{1,0:T(8,128)(2,1)S(1)}, bf16[48,6144]{1,0:T(8,128)(2,1)S(1)}, u32[]{:S(2)}, u32[]{:S(2)}) %collective-permute-start.39) | collective-permute-done | bytes 589856 | tf_op jit(solution)/shard_map/ppermute | solution.py:130
  132.3 10.4 %collective-permute-done.29 = bf16[48,6144]{1,0:T(8,128)(2,1)S(1)} collective-permute-done((bf16[48,6144]{1,0:T(8,128)(2,1)S(1)}, bf16[48,6144]{1,0:T(8,128)(2,1)S(1)}, u32[]{:S(2)}, u32[]{:S(2)}) %collective-permute-start.29) | collective-permute-done | bytes 589856 | tf_op jit(solution)/shard_map/ppermute | solution.py:130
  142.7 3.3 %collective-permute-start.37 = (bf16[48,6144]{1,0:T(8,128)(2,1)S(1)}, bf16[48,6144]{1,0:T(8,128)(2,1)S(1)}, u32[]{:S(2)}, u32[]{:S(2)}) collective-permute-start(bf16[48,6144]{1,0:T(8,128)(2,1)S(1)} %pad_maximum_fusion.8), channel_id=1, source_target_pairs={{0,3},{1,0},{2,1},{3,2},{4,7},{5,4},{6,5},{7,6},{8,11},{9,8},{10,9... | collective-permute-start | bytes 1769480 | tf_op jit(solution)/shard_map/ppermute | solution.py:130
  147.8 5.0 %collective-permute-done.37 = bf16[48,6144]{1,0:T(8,128)(2,1)S(1)} collective-permute-done((bf16[48,6144]{1,0:T(8,128)(2,1)S(1)}, bf16[48,6144]{1,0:T(8,128)(2,1)S(1)}, u32[]{:S(2)}, u32[]{:S(2)}) %collective-permute-start.37) | collective-permute-done | bytes 589856 | tf_op jit(solution)/shard_map/ppermute | solution.py:130
  153.2 3.5 %collective-permute-start.31 = (bf16[24,6144]{1,0:T(8,128)(2,1)S(1)}, bf16[24,6144]{1,0:T(8,128)(2,1)S(1)}, u32[]{:S(2)}, u32[]{:S(2)}) collective-permute-start(bf16[24,6144]{1,0:T(8,128)(2,1)S(1)} %get-tuple-element.36), channel_id=1, source_target_pairs={{0,3},{1,0},{2,1},{3,2},{4,7},{5,4},{6,5},{7,6},{8,11},{9,8},{10,9... | collective-permute-start | bytes 884744 | tf_op jit(solution)/shard_map/ppermute | solution.py:130
  158.7 6.5 %collective-permute-done.43 = bf16[24,6144]{1,0:T(8,128)(2,1)S(1)} collective-permute-done((bf16[24,6144]{1,0:T(8,128)(2,1)S(1)}, bf16[24,6144]{1,0:T(8,128)(2,1)S(1)}, u32[]{:S(2)}, u32[]{:S(2)}) %collective-permute-start.43) | collective-permute-done | bytes 294944 | tf_op jit(solution)/shard_map/ppermute | solution.py:130
  167.6 3.6 %collective-permute-done.46.across_ref = bf16[24,3072]{1,0:T(8,128)(2,1)S(1)} collective-permute-done((bf16[24,3072]{1,0:T(8,128)(2,1)S(1)}, bf16[24,3072]{1,0:T(8,128)(2,1)S(1)}, u32[]{:S(2)}, u32[]{:S(2)}) %collective-permute-start.46) | collective-permute-done | bytes 147488 | tf_op jit(solution)/shard_map/ppermute | solution.py:118
  172.7 18.5 %collective-permute-start.47 = (bf16[96,3072]{1,0:T(8,128)(2,1)S(1)}, bf16[96,3072]{1,0:T(8,128)(2,1)S(1)}, u32[]{:S(2)}, u32[]{:S(2)}) collective-permute-start(bf16[96,3072]{1,0:T(8,128)(2,1)S(1)} %pad_maximum_fusion.9), channel_id=1, source_target_pairs={{0,16},{16,0},{32,48},{48,32},{64,80},{80,64},{96,112},{112,96},{1... | collective-permute-start | bytes 1769480 | tf_op jit(solution)/shard_map/ppermute | solution.py:122
  (177 shorter events, 61.8 us)
Async XLA Ops:
  21.5 51.8 %collective-permute-start.14 = (bf16[72,6144]{1,0:T(8,128)(2,1)S(1)}, bf16[72,6144]{1,0:T(8,128)(2,1)S(1)}, u32[]{:S(2)}, u32[]{:S(2)}) collective-permute-start(bf16[72,6144]{1,0:T(8,128)(2,1)S(1)} %pad_maximum_fusion.1), channel_id=1, source_target_pairs={{0,3},{1,0},{2,1},{3,2},{4,7},{5,4},{6,5},{7,6},{8,11},{9,8},{10,9... | collective-permute-start | bytes 2654216 | tf_op jit(solution)/shard_map/ppermute | solution.py:130
  24.3 38.9 %collective-permute-start.12 = (bf16[72,6144]{1,0:T(8,128)(2,1)S(1)}, bf16[72,6144]{1,0:T(8,128)(2,1)S(1)}, u32[]{:S(2)}, u32[]{:S(2)}) collective-permute-start(bf16[72,6144]{1,0:T(8,128)(2,1)S(1)} %pad_maximum_fusion.1), channel_id=1, source_target_pairs={{0,1},{1,2},{2,3},{3,0},{4,5},{5,6},{6,7},{7,4},{8,9},{9,10},{10,1... | collective-permute-start | bytes 2654216 | tf_op jit(solution)/shard_map/ppermute | solution.py:130
  24.9 48.7 %collective-permute-start.17 = (bf16[72,6144]{1,0:T(8,128)(2,1)S(1)}, bf16[72,6144]{1,0:T(8,128)(2,1)S(1)}, u32[]{:S(2)}, u32[]{:S(2)}) collective-permute-start(bf16[72,6144]{1,0:T(8,128)(2,1)S(1)} %pad_maximum_fusion.2), channel_id=1, source_target_pairs={{0,4},{1,5},{2,6},{3,7},{4,8},{5,9},{6,10},{7,11},{8,12},{9,13},{1... | collective-permute-start | bytes 2654216 | tf_op jit(solution)/shard_map/ppermute | solution.py:130
  26.3 54.0 %collective-permute-start.19 = (bf16[72,6144]{1,0:T(8,128)(2,1)S(1)}, bf16[72,6144]{1,0:T(8,128)(2,1)S(1)}, u32[]{:S(2)}, u32[]{:S(2)}) collective-permute-start(bf16[72,6144]{1,0:T(8,128)(2,1)S(1)} %pad_maximum_fusion.2), channel_id=1, source_target_pairs={{0,12},{1,13},{2,14},{3,15},{4,0},{5,1},{6,2},{7,3},{8,4},{9,5},{1... | collective-permute-start | bytes 2654216 | tf_op jit(solution)/shard_map/ppermute | solution.py:130
  29.6 18.2 %collective-permute-start.10 = (bf16[24,3072]{1,0:T(8,128)(2,1)S(1)}, bf16[24,3072]{1,0:T(8,128)(2,1)S(1)}, u32[]{:S(2)}, u32[]{:S(2)}) collective-permute-start(bf16[24,3072]{1,0:T(8,128)(2,1)S(1)} %slice.358), channel_id=1, source_target_pairs={{0,1},{1,2},{2,3},{3,0},{4,5},{5,6},{6,7},{7,4},{8,9},{9,10},{10,1... | collective-permute-start | bytes 442376 | tf_op jit(solution)/shard_map/ppermute | solution.py:130
  56.1 17.5 %collective-permute-start.15 = (bf16[24,6144]{1,0:T(8,128)(2,1)S(1)}, bf16[24,6144]{1,0:T(8,128)(2,1)S(1)}, u32[]{:S(2)}, u32[]{:S(2)}) collective-permute-start(bf16[24,6144]{1,0:T(8,128)(2,1)S(1)} %constant_dynamic-update-slice_fusion), channel_id=1, source_target_pairs={{0,3},{1,0},{2,1},{3,2},{4,7},{5,4},{6,5},{7,6},{8,11},{9,8},{10,9... | collective-permute-start | bytes 884744 | tf_op jit(solution)/shard_map/ppermute | solution.py:130
  89.0 10.7 %collective-permute-start.16 = (bf16[48,6144]{1,0:T(8,128)(2,1)S(1)}, bf16[48,6144]{1,0:T(8,128)(2,1)S(1)}, u32[]{:S(2)}, u32[]{:S(2)}) collective-permute-start(bf16[48,6144]{1,0:T(8,128)(2,1)S(1)} %pad_maximum_fusion.5), channel_id=1, source_target_pairs={{0,3},{1,0},{2,1},{3,2},{4,7},{5,4},{6,5},{7,6},{8,11},{9,8},{10,9... | collective-permute-start | bytes 1769480 | tf_op jit(solution)/shard_map/ppermute | solution.py:130
  90.7 11.3 %collective-permute-start.18 = (bf16[48,6144]{1,0:T(8,128)(2,1)S(1)}, bf16[48,6144]{1,0:T(8,128)(2,1)S(1)}, u32[]{:S(2)}, u32[]{:S(2)}) collective-permute-start(bf16[48,6144]{1,0:T(8,128)(2,1)S(1)} %slice.363), channel_id=1, source_target_pairs={{0,4},{1,5},{2,6},{3,7},{4,8},{5,9},{6,10},{7,11},{8,12},{9,13},{1... | collective-permute-start | bytes 1769480 | tf_op jit(solution)/shard_map/ppermute | solution.py:130
  90.8 11.3 %collective-permute-start.21 = (bf16[48,6144]{1,0:T(8,128)(2,1)S(1)}, bf16[48,6144]{1,0:T(8,128)(2,1)S(1)}, u32[]{:S(2)}, u32[]{:S(2)}) collective-permute-start(bf16[48,6144]{1,0:T(8,128)(2,1)S(1)} %pad_maximum_fusion.6), channel_id=1, source_target_pairs={{0,12},{1,13},{2,14},{3,15},{4,0},{5,1},{6,2},{7,3},{8,4},{9,5},{1... | collective-permute-start | bytes 1769480 | tf_op jit(solution)/shard_map/ppermute | solution.py:130
  93.5 18.2 %collective-permute-start.28 = (bf16[48,6144]{1,0:T(8,128)(2,1)S(1)}, bf16[48,6144]{1,0:T(8,128)(2,1)S(1)}, u32[]{:S(2)}, u32[]{:S(2)}) collective-permute-start(bf16[48,6144]{1,0:T(8,128)(2,1)S(1)} %get-tuple-element.19), channel_id=1, source_target_pairs={{0,4},{1,5},{2,6},{3,7},{4,8},{5,9},{6,10},{7,11},{8,12},{9,13},{1... | collective-permute-start | bytes 1769480 | tf_op jit(solution)/shard_map/ppermute | solution.py:130
  99.1 14.3 %collective-permute-start.38 = (bf16[48,6144]{1,0:T(8,128)(2,1)S(1)}, bf16[48,6144]{1,0:T(8,128)(2,1)S(1)}, u32[]{:S(2)}, u32[]{:S(2)}) collective-permute-start(bf16[48,6144]{1,0:T(8,128)(2,1)S(1)} %get-tuple-element.17), channel_id=1, source_target_pairs={{0,1},{1,2},{2,3},{3,0},{4,5},{5,6},{6,7},{7,4},{8,9},{9,10},{10,1... | collective-permute-start | bytes 1769480 | tf_op jit(solution)/shard_map/ppermute | solution.py:130
  99.7 15.5 %collective-permute-start.35 = (bf16[72,6144]{1,0:T(8,128)(2,1)S(1)}, bf16[72,6144]{1,0:T(8,128)(2,1)S(1)}, u32[]{:S(2)}, u32[]{:S(2)}) collective-permute-start(bf16[72,6144]{1,0:T(8,128)(2,1)S(1)} %pad_maximum_fusion.4), channel_id=1, source_target_pairs={{0,3},{1,0},{2,1},{3,2},{4,7},{5,4},{6,5},{7,6},{8,11},{9,8},{10,9... | collective-permute-start | bytes 2654216 | tf_op jit(solution)/shard_map/ppermute | solution.py:130
  102.0 19.1 %collective-permute-start.25 = (bf16[72,6144]{1,0:T(8,128)(2,1)S(1)}, bf16[72,6144]{1,0:T(8,128)(2,1)S(1)}, u32[]{:S(2)}, u32[]{:S(2)}) collective-permute-start(bf16[72,6144]{1,0:T(8,128)(2,1)S(1)} %pad_maximum_fusion.3), channel_id=1, source_target_pairs={{0,12},{1,13},{2,14},{3,15},{4,0},{5,1},{6,2},{7,3},{8,4},{9,5},{1... | collective-permute-start | bytes 2654216 | tf_op jit(solution)/shard_map/ppermute | solution.py:130
  102.1 44.2 %collective-permute-start.34 = (bf16[24,6144]{1,0:T(8,128)(2,1)S(1)}, bf16[24,6144]{1,0:T(8,128)(2,1)S(1)}, u32[]{:S(2)}, u32[]{:S(2)}) collective-permute-start(bf16[24,6144]{1,0:T(8,128)(2,1)S(1)} %get-tuple-element.11), channel_id=1, source_target_pairs={{0,1},{1,2},{2,3},{3,0},{4,5},{5,6},{6,7},{7,4},{8,9},{9,10},{10,1... | collective-permute-start | bytes 884744 | tf_op jit(solution)/shard_map/ppermute | solution.py:130
  111.7 15.6 %collective-permute-start.26 = (bf16[24,6144]{1,0:T(8,128)(2,1)S(1)}, bf16[24,6144]{1,0:T(8,128)(2,1)S(1)}, u32[]{:S(2)}, u32[]{:S(2)}) collective-permute-start(bf16[24,6144]{1,0:T(8,128)(2,1)S(1)} %get-tuple-element.28), channel_id=1, source_target_pairs={{0,12},{1,13},{2,14},{3,15},{4,0},{5,1},{6,2},{7,3},{8,4},{9,5},{1... | collective-permute-start | bytes 884744 | tf_op jit(solution)/shard_map/ppermute | solution.py:130
  113.4 14.0 %collective-permute-start.36 = (bf16[24,6144]{1,0:T(8,128)(2,1)S(1)}, bf16[24,6144]{1,0:T(8,128)(2,1)S(1)}, u32[]{:S(2)}, u32[]{:S(2)}) collective-permute-start(bf16[24,6144]{1,0:T(8,128)(2,1)S(1)} %get-tuple-element.25), channel_id=1, source_target_pairs={{0,3},{1,0},{2,1},{3,2},{4,7},{5,4},{6,5},{7,6},{8,11},{9,8},{10,9... | collective-permute-start | bytes 884744 | tf_op jit(solution)/shard_map/ppermute | solution.py:130
  115.2 37.9 %collective-permute-start.24 = (bf16[24,6144]{1,0:T(8,128)(2,1)S(1)}, bf16[24,6144]{1,0:T(8,128)(2,1)S(1)}, u32[]{:S(2)}, u32[]{:S(2)}) collective-permute-start(bf16[24,6144]{1,0:T(8,128)(2,1)S(1)} %get-tuple-element.14), channel_id=1, source_target_pairs={{0,4},{1,5},{2,6},{3,7},{4,8},{5,9},{6,10},{7,11},{8,12},{9,13},{1... | collective-permute-start | bytes 884744 | tf_op jit(solution)/shard_map/ppermute | solution.py:130
  121.0 11.0 %collective-permute-start.39 = (bf16[48,6144]{1,0:T(8,128)(2,1)S(1)}, bf16[48,6144]{1,0:T(8,128)(2,1)S(1)}, u32[]{:S(2)}, u32[]{:S(2)}) collective-permute-start(bf16[48,6144]{1,0:T(8,128)(2,1)S(1)} %get-tuple-element.15), channel_id=1, source_target_pairs={{0,1},{1,2},{2,3},{3,0},{4,5},{5,6},{6,7},{7,4},{8,9},{9,10},{10,1... | collective-permute-start | bytes 1769480 | tf_op jit(solution)/shard_map/ppermute | solution.py:130
  127.3 19.0 %collective-permute-start.42 = (bf16[24,6144]{1,0:T(8,128)(2,1)S(1)}, bf16[24,6144]{1,0:T(8,128)(2,1)S(1)}, u32[]{:S(2)}, u32[]{:S(2)}) collective-permute-start(bf16[24,6144]{1,0:T(8,128)(2,1)S(1)} %get-tuple-element.26), channel_id=1, source_target_pairs={{0,1},{1,2},{2,3},{3,0},{4,5},{5,6},{6,7},{7,4},{8,9},{9,10},{10,1... | collective-permute-start | bytes 884744 | tf_op jit(solution)/shard_map/ppermute | solution.py:130
  127.4 15.4 %collective-permute-start.29 = (bf16[48,6144]{1,0:T(8,128)(2,1)S(1)}, bf16[48,6144]{1,0:T(8,128)(2,1)S(1)}, u32[]{:S(2)}, u32[]{:S(2)}) collective-permute-start(bf16[48,6144]{1,0:T(8,128)(2,1)S(1)} %get-tuple-element.16), channel_id=1, source_target_pairs={{0,4},{1,5},{2,6},{3,7},{4,8},{5,9},{6,10},{7,11},{8,12},{9,13},{1... | collective-permute-start | bytes 1769480 | tf_op jit(solution)/shard_map/ppermute | solution.py:130
  132.0 21.1 %collective-permute-start.32 = (bf16[24,6144]{1,0:T(8,128)(2,1)S(1)}, bf16[24,6144]{1,0:T(8,128)(2,1)S(1)}, u32[]{:S(2)}, u32[]{:S(2)}) collective-permute-start(bf16[24,6144]{1,0:T(8,128)(2,1)S(1)} %get-tuple-element.27), channel_id=1, source_target_pairs={{0,4},{1,5},{2,6},{3,7},{4,8},{5,9},{6,10},{7,11},{8,12},{9,13},{1... | collective-permute-start | bytes 884744 | tf_op jit(solution)/shard_map/ppermute | solution.py:130
  153.1 12.6 %collective-permute-start.30 = (bf16[24,6144]{1,0:T(8,128)(2,1)S(1)}, bf16[24,6144]{1,0:T(8,128)(2,1)S(1)}, u32[]{:S(2)}, u32[]{:S(2)}) collective-permute-start(bf16[24,6144]{1,0:T(8,128)(2,1)S(1)} %get-tuple-element.35), channel_id=1, source_target_pairs={{0,1},{1,2},{2,3},{3,0},{4,5},{5,6},{6,7},{7,4},{8,9},{9,10},{10,1... | collective-permute-start | bytes 884744 | tf_op jit(solution)/shard_map/ppermute | solution.py:130
  153.2 12.5 %collective-permute-start.31 = (bf16[24,6144]{1,0:T(8,128)(2,1)S(1)}, bf16[24,6144]{1,0:T(8,128)(2,1)S(1)}, u32[]{:S(2)}, u32[]{:S(2)}) collective-permute-start(bf16[24,6144]{1,0:T(8,128)(2,1)S(1)} %get-tuple-element.36), channel_id=1, source_target_pairs={{0,3},{1,0},{2,1},{3,2},{4,7},{5,4},{6,5},{7,6},{8,11},{9,8},{10,9... | collective-permute-start | bytes 884744 | tf_op jit(solution)/shard_map/ppermute | solution.py:130
  172.7 20.1 %collective-permute-start.47 = (bf16[96,3072]{1,0:T(8,128)(2,1)S(1)}, bf16[96,3072]{1,0:T(8,128)(2,1)S(1)}, u32[]{:S(2)}, u32[]{:S(2)}) collective-permute-start(bf16[96,3072]{1,0:T(8,128)(2,1)S(1)} %pad_maximum_fusion.9), channel_id=1, source_target_pairs={{0,16},{16,0},{32,48},{48,32},{64,80},{80,64},{96,112},{112,96},{1... | collective-permute-start | bytes 1769480 | tf_op jit(solution)/shard_map/ppermute | solution.py:122
  (32 other events, 315.1 us)

commit v6 on v5

--- a/solution.py
+++ b/solution.py
@@ -176,13 +176,10 @@
     up_sum = [add(piece(early, 6 * i + 2, 2), up_one[i]) for i in both]
     up_three = [shift(up_sum[i], orders[i][0], 1) for i in both]
     up_two = [shift(piece(late, 3 * i + 1, 1), orders[i][0], 1) for i in both]
-    down_sum = [
-        jnp.concatenate(
-            [add(piece(late, 6 + i, 1), down_one[i][:rows]), add(piece(late, 3 * i, 1), down_two[i])], axis=0
-        )
-        for i in both
-    ]
-    down_three = [shift(down_sum[i], orders[i][0], -1) for i in both]
+    soon = [lax.optimization_barrier(piece(late, 6 + i, 1)) for i in both]
+    down_own = [shift(add(soon[i], down_one[i][:rows]), orders[i][0], -1) for i in both]
+    down_sum = [add(piece(late, 3 * i, 1), down_two[i]) for i in both]
+    down_far = [shift(down_sum[i], orders[i][0], -1) for i in both]
     kept = [product([start[i, 0, 0], end[i, 0, 0], middle[i, :, 0]]) for i in both]
     sides = []
     for i in both:
@@ -190,9 +187,9 @@
         sides.append((shift(inner[rows:], orders[i][1], 1), shift(inner[:rows], orders[i][1], -1)))
     results = []
     for i in both:
-        across = add(kept[i][rows : 2 * rows], up_two[i], down_three[i][rows:])
+        across = add(kept[i][rows : 2 * rows], up_two[i], down_far[i])
         across = shift(across, orders[i][1], 2)
-        own = lax.optimization_barrier(add(kept[i][:rows], up_own[i], down_three[i][:rows]))
+        own = lax.optimization_barrier(add(kept[i][:rows], up_own[i], down_own[i]))
         results.append(add(own, *sides[i], across))
     return results
 

time: 194 us -> 212 us (1.093)
  starting transfers between devices: 68.4 us -> 82.2 us
  waiting for transfers between devices: 98.1 us -> 102 us
    ppermute x2, starting transfers between devices: 19.9 us -> 26 us  [other_core(): return lax.ppermute(value, 'expert', [(i, i ^ 1) for i in range(2 * RING)])]
    ppermute x40 -> x42, starting transfers between devices: 42.3 us -> 48.3 us  [shift(): lax.ppermute(value, 'hidden', [(i, target(i)) for i in range(RING * RING)])]
    ppermute x40 -> x42, waiting for transfers between devices: 89 us -> 92 us  [shift(): lax.ppermute(value, 'hidden', [(i, target(i)) for i in range(RING * RING)])]
  transfers between devices with their start and end apart: 48 -> 50, of which waited for: 24 -> 26; matrix products, arithmetic and copies ran while one was open for 7% -> 6% of each run, Pallas kernels for 0% -> 0%
where the time goes in v6:
time: 212 us
  waiting for transfers between devices  102 us (48%)
  starting transfers between devices  82.2 us (39%)
  matrix products  17.2 us (8%)
  Pallas kernels  3.7 us (2%)
  local copies, waits for them, and re-layouts  3.25 us (2%)
  other arithmetic  2.76 us (1%)
    ppermute x42, waiting for transfers between devices, shift(): lax.ppermute(value, 'hidden', [(i, target(i)) for i in range(RING * RING)])  92 us
    ppermute x42, starting transfers between devices, shift(): lax.ppermute(value, 'hidden', [(i, target(i)) for i in range(RING * RING)])  48.3 us
    ppermute x2, starting transfers between devices, other_core(): return lax.ppermute(value, 'expert', [(i, i ^ 1) for i in range(2 * RING)])  26 us
    ppermute x6, starting transfers between devices, along_x(): return lax.ppermute(value, 'expert', pairs)  7.84 us
    ppermute x6, waiting for transfers between devices, along_x(): return lax.ppermute(value, 'expert', pairs)  7.26 us
    dot_general x4, matrix products, product(): jnp.dot(jnp.concatenate(value, axis=0), down, preferred_element_type=jnp....  6.49 us
    dot_general x3, matrix products, per_device(): upper = jnp.dot(value, up_local, preferred_element_type=jnp.float32)  5.42 us
    dot_general x3, matrix products, per_device(): gate = jnp.dot(value, gate_local, preferred_element_type=jnp.float32)  5.34 us
  transfers between devices with their start and end apart: 50, of which 26 were waited for; matrix products, arithmetic and copies ran while one was open for 6% of the time, Pallas kernels for 0%

profile of v6, /device:TPU:1, one launch (start us, length us, event | category | flops | bytes accessed | tf_op | source)
XLA Modules:
  0.0 211.6 jit_solution(6476321544101080894)
XLA Ops:
  11.4 3.9 %collective-permute-start.3 = (bf16[24,6144]{1,0:T(8,128)(2,1)S(1)}, bf16[24,6144]{1,0:T(8,128)(2,1)S(1)}, u32[]{:S(2)}, u32[]{:S(2)}) collective-permute-start(bf16[24,6144]{1,0:T(8,128)(2,1)S(1)} %maximum_maximum_fusion), channel_id=1, source_target_pairs={{0,12},{1,13},{2,14},{3,15},{4,0},{5,1},{6,2},{7,3},{8,4},{9,5},{1... | collective-permute-start | bytes 884744 | tf_op jit(solution)/shard_map/ppermute | solution.py:130
  15.6 2.8 %collective-permute-start.9 = (bf16[24,6144]{1,0:T(8,128)(2,1)S(1)}, bf16[24,6144]{1,0:T(8,128)(2,1)S(1)}, u32[]{:S(2)}, u32[]{:S(2)}) collective-permute-start(bf16[24,6144]{1,0:T(8,128)(2,1)S(1)} %maximum_maximum_fusion.1), channel_id=1, source_target_pairs={{0,3},{1,0},{2,1},{3,2},{4,7},{5,4},{6,5},{7,6},{8,11},{9,8},{10,9... | collective-permute-start | bytes 884744 | tf_op jit(solution)/shard_map/ppermute | solution.py:130
  20.5 3.1 %collective-permute-done.2 = bf16[24,6144]{1,0:T(8,128)(2,1)S(1)} collective-permute-done((bf16[24,6144]{1,0:T(8,128)(2,1)S(1)}, bf16[24,6144]{1,0:T(8,128)(2,1)S(1)}, u32[]{:S(2)}, u32[]{:S(2)}) %collective-permute-start.2) | collective-permute-done | bytes 294944 | tf_op jit(solution)/shard_map/ppermute | solution.py:130
  23.7 2.8 %collective-permute-start.14 = (bf16[72,6144]{1,0:T(8,128)(2,1)S(1)}, bf16[72,6144]{1,0:T(8,128)(2,1)S(1)}, u32[]{:S(2)}, u32[]{:S(2)}) collective-permute-start(bf16[72,6144]{1,0:T(8,128)(2,1)S(1)} %pad_maximum_fusion.1), channel_id=1, source_target_pairs={{0,3},{1,0},{2,1},{3,2},{4,7},{5,4},{6,5},{7,6},{8,11},{9,8},{10,9... | collective-permute-start | bytes 2654216 | tf_op jit(solution)/shard_map/ppermute | solution.py:130
  26.7 4.0 %collective-permute-start.19 = (bf16[72,6144]{1,0:T(8,128)(2,1)S(1)}, bf16[72,6144]{1,0:T(8,128)(2,1)S(1)}, u32[]{:S(2)}, u32[]{:S(2)}) collective-permute-start(bf16[72,6144]{1,0:T(8,128)(2,1)S(1)} %pad_maximum_fusion.2), channel_id=1, source_target_pairs={{0,12},{1,13},{2,14},{3,15},{4,0},{5,1},{6,2},{7,3},{8,4},{9,5},{1... | collective-permute-start | bytes 2654216 | tf_op jit(solution)/shard_map/ppermute | solution.py:130
  30.8 18.7 %collective-permute-done.10 = bf16[24,3072]{1,0:T(8,128)(2,1)S(1)} collective-permute-done((bf16[24,3072]{1,0:T(8,128)(2,1)S(1)}, bf16[24,3072]{1,0:T(8,128)(2,1)S(1)}, u32[]{:S(2)}, u32[]{:S(2)}) %collective-permute-start.10) | collective-permute-done | bytes 147488 | tf_op jit(solution)/shard_map/ppermute | solution.py:130
  50.5 4.9 %collective-permute-done.4 = bf16[24,3072]{1,0:T(8,128)(2,1)S(1)} collective-permute-done((bf16[24,3072]{1,0:T(8,128)(2,1)S(1)}, bf16[24,3072]{1,0:T(8,128)(2,1)S(1)}, u32[]{:S(2)}, u32[]{:S(2)}) %collective-permute-start.4) | collective-permute-done | bytes 147488 | tf_op jit(solution)/shard_map/ppermute | solution.py:130
  56.5 2.8 %collective-permute-done.11 = bf16[24,3072]{1,0:T(8,128)(2,1)S(1)} collective-permute-done((bf16[24,3072]{1,0:T(8,128)(2,1)S(1)}, bf16[24,3072]{1,0:T(8,128)(2,1)S(1)}, u32[]{:S(2)}, u32[]{:S(2)}) %collective-permute-start.11) | collective-permute-done | bytes 147488 | tf_op jit(solution)/shard_map/ppermute | solution.py:130
  60.8 2.8 %collective-permute-done.5 = bf16[24,3072]{1,0:T(8,128)(2,1)S(1)} collective-permute-done((bf16[24,3072]{1,0:T(8,128)(2,1)S(1)}, bf16[24,3072]{1,0:T(8,128)(2,1)S(1)}, u32[]{:S(2)}, u32[]{:S(2)}) %collective-permute-start.5) | collective-permute-done | bytes 147488 | tf_op jit(solution)/shard_map/ppermute | solution.py:130
  68.1 7.0 %collective-permute-done.22 = bf16[24,6144]{1,0:T(8,128)(2,1)S(1)} collective-permute-done((bf16[24,6144]{1,0:T(8,128)(2,1)S(1)}, bf16[24,6144]{1,0:T(8,128)(2,1)S(1)}, u32[]{:S(2)}, u32[]{:S(2)}) %collective-permute-start.22) | collective-permute-done | bytes 294944 | tf_op jit(solution)/shard_map/ppermute | solution.py:130
  79.0 4.3 %collective-permute-done.15 = bf16[24,6144]{1,0:T(8,128)(2,1)S(1)} collective-permute-done((bf16[24,6144]{1,0:T(8,128)(2,1)S(1)}, bf16[24,6144]{1,0:T(8,128)(2,1)S(1)}, u32[]{:S(2)}, u32[]{:S(2)}) %collective-permute-start.15) | collective-permute-done | bytes 294944 | tf_op jit(solution)/shard_map/ppermute | solution.py:130
  89.0 2.8 %convolution_convert_fusion = bf16[384,6144]{1,0:T(8,128)(2,1)S(1)} fusion(bf16[1,512,6144]{2,1,0:T(8,128)(2,1)S(1)} %bitcast.78, bf16[96,512]{1,0:T(8,128)(2,1)S(1)} %bitcast.91, bf16[288,512]{1,0:T(8,128)(2,1)S(1)} %bitcast.81), kind=kOutput, calls=%fused_computation | convolution fusion | flops 2419064832 | bytes 11403264 | tf_op jit(solution)/shard_map/dot_general | solution.py:161
  96.6 8.1 %collective-permute-done.13 = bf16[48,6144]{1,0:T(8,128)(2,1)S(1)} collective-permute-done((bf16[48,6144]{1,0:T(8,128)(2,1)S(1)}, bf16[48,6144]{1,0:T(8,128)(2,1)S(1)}, u32[]{:S(2)}, u32[]{:S(2)}) %collective-permute-start.13) | collective-permute-done | bytes 589856 | tf_op jit(solution)/shard_map/ppermute | solution.py:130
  113.7 7.7 %collective-permute-done.38 = bf16[48,6144]{1,0:T(8,128)(2,1)S(1)} collective-permute-done((bf16[48,6144]{1,0:T(8,128)(2,1)S(1)}, bf16[48,6144]{1,0:T(8,128)(2,1)S(1)}, u32[]{:S(2)}, u32[]{:S(2)}) %collective-permute-start.38) | collective-permute-done | bytes 589856 | tf_op jit(solution)/shard_map/ppermute | solution.py:130
  128.5 4.6 %collective-permute-done.32 = bf16[24,6144]{1,0:T(8,128)(2,1)S(1)} collective-permute-done((bf16[24,6144]{1,0:T(8,128)(2,1)S(1)}, bf16[24,6144]{1,0:T(8,128)(2,1)S(1)}, u32[]{:S(2)}, u32[]{:S(2)}) %collective-permute-start.32) | collective-permute-done | bytes 294944 | tf_op jit(solution)/shard_map/ppermute | solution.py:130
  133.3 2.7 %collective-permute-start.33 = (bf16[24,6144]{1,0:T(8,128)(2,1)S(1)}, bf16[24,6144]{1,0:T(8,128)(2,1)S(1)}, u32[]{:S(2)}, u32[]{:S(2)}) collective-permute-start(bf16[24,6144]{1,0:T(8,128)(2,1)S(1)} %get-tuple-element.28), channel_id=1, source_target_pairs={{0,12},{1,13},{2,14},{3,15},{4,0},{5,1},{6,2},{7,3},{8,4},{9,5},{1... | collective-permute-start | bytes 884744 | tf_op jit(solution)/shard_map/ppermute | solution.py:130
  136.1 6.5 %collective-permute-done.36 = bf16[72,6144]{1,0:T(8,128)(2,1)S(1)} collective-permute-done((bf16[72,6144]{1,0:T(8,128)(2,1)S(1)}, bf16[72,6144]{1,0:T(8,128)(2,1)S(1)}, u32[]{:S(2)}, u32[]{:S(2)}) %collective-permute-start.36) | collective-permute-done | bytes 884768 | tf_op jit(solution)/shard_map/ppermute | solution.py:130
  148.7 3.1 %collective-permute-start.37 = (bf16[24,6144]{1,0:T(8,128)(2,1)S(1)}, bf16[24,6144]{1,0:T(8,128)(2,1)S(1)}, u32[]{:S(2)}, u32[]{:S(2)}) collective-permute-start(bf16[24,6144]{1,0:T(8,128)(2,1)S(1)} %add_convert_fusion.8), channel_id=1, source_target_pairs={{0,3},{1,0},{2,1},{3,2},{4,7},{5,4},{6,5},{7,6},{8,11},{9,8},{10,9... | collective-permute-start | bytes 884744 | tf_op jit(solution)/shard_map/ppermute | solution.py:130
  152.3 3.5 %collective-permute-done.44 = bf16[24,6144]{1,0:T(8,128)(2,1)S(1)} collective-permute-done((bf16[24,6144]{1,0:T(8,128)(2,1)S(1)}, bf16[24,6144]{1,0:T(8,128)(2,1)S(1)}, u32[]{:S(2)}, u32[]{:S(2)}) %collective-permute-start.44) | collective-permute-done | bytes 294944 | tf_op jit(solution)/shard_map/ppermute | solution.py:130
  155.8 8.3 %collective-permute-done.37 = bf16[24,6144]{1,0:T(8,128)(2,1)S(1)} collective-permute-done((bf16[24,6144]{1,0:T(8,128)(2,1)S(1)}, bf16[24,6144]{1,0:T(8,128)(2,1)S(1)}, u32[]{:S(2)}, u32[]{:S(2)}) %collective-permute-start.37) | collective-permute-done | bytes 294944 | tf_op jit(solution)/shard_map/ppermute | solution.py:130
  164.8 3.5 %collective-permute-start.30 = (bf16[24,6144]{1,0:T(8,128)(2,1)S(1)}, bf16[24,6144]{1,0:T(8,128)(2,1)S(1)}, u32[]{:S(2)}, u32[]{:S(2)}) collective-permute-start(bf16[24,6144]{1,0:T(8,128)(2,1)S(1)} %get-tuple-element.36), channel_id=1, source_target_pairs={{0,3},{1,0},{2,1},{3,2},{4,7},{5,4},{6,5},{7,6},{8,11},{9,8},{10,9... | collective-permute-start | bytes 884744 | tf_op jit(solution)/shard_map/ppermute | solution.py:130
  171.3 3.1 %collective-permute-done.29 = bf16[24,6144]{1,0:T(8,128)(2,1)S(1)} collective-permute-done((bf16[24,6144]{1,0:T(8,128)(2,1)S(1)}, bf16[24,6144]{1,0:T(8,128)(2,1)S(1)}, u32[]{:S(2)}, u32[]{:S(2)}) %collective-permute-start.29) | collective-permute-done | bytes 294944 | tf_op jit(solution)/shard_map/ppermute | solution.py:130
  179.1 4.8 %collective-permute-done.46.below_ref = bf16[24,3072]{1,0:T(8,128)(2,1)S(1)} collective-permute-done((bf16[24,3072]{1,0:T(8,128)(2,1)S(1)}, bf16[24,3072]{1,0:T(8,128)(2,1)S(1)}, u32[]{:S(2)}, u32[]{:S(2)}) %collective-permute-start.46) | collective-permute-done | bytes 147488 | tf_op jit(solution)/shard_map/ppermute | solution.py:118
  183.9 24.6 %collective-permute-start.49 = (bf16[96,3072]{1,0:T(8,128)(2,1)S(1)}, bf16[96,3072]{1,0:T(8,128)(2,1)S(1)}, u32[]{:S(2)}, u32[]{:S(2)}) collective-permute-start(bf16[96,3072]{1,0:T(8,128)(2,1)S(1)} %pad_maximum_fusion.7), channel_id=1, source_target_pairs={{0,16},{16,0},{32,48},{48,32},{64,80},{80,64},{96,112},{112,96},{1... | collective-permute-start | bytes 1769480 | tf_op jit(solution)/shard_map/ppermute | solution.py:122
  (181 shorter events, 70.2 us)
Async XLA Ops:
  15.6 11.0 %collective-permute-start.9 = (bf16[24,6144]{1,0:T(8,128)(2,1)S(1)}, bf16[24,6144]{1,0:T(8,128)(2,1)S(1)}, u32[]{:S(2)}, u32[]{:S(2)}) collective-permute-start(bf16[24,6144]{1,0:T(8,128)(2,1)S(1)} %maximum_maximum_fusion.1), channel_id=1, source_target_pairs={{0,3},{1,0},{2,1},{3,2},{4,7},{5,4},{6,5},{7,6},{8,11},{9,8},{10,9... | collective-permute-start | bytes 884744 | tf_op jit(solution)/shard_map/ppermute | solution.py:130
  23.7 53.8 %collective-permute-start.14 = (bf16[72,6144]{1,0:T(8,128)(2,1)S(1)}, bf16[72,6144]{1,0:T(8,128)(2,1)S(1)}, u32[]{:S(2)}, u32[]{:S(2)}) collective-permute-start(bf16[72,6144]{1,0:T(8,128)(2,1)S(1)} %pad_maximum_fusion.1), channel_id=1, source_target_pairs={{0,3},{1,0},{2,1},{3,2},{4,7},{5,4},{6,5},{7,6},{8,11},{9,8},{10,9... | collective-permute-start | bytes 2654216 | tf_op jit(solution)/shard_map/ppermute | solution.py:130
  26.5 41.4 %collective-permute-start.12 = (bf16[72,6144]{1,0:T(8,128)(2,1)S(1)}, bf16[72,6144]{1,0:T(8,128)(2,1)S(1)}, u32[]{:S(2)}, u32[]{:S(2)}) collective-permute-start(bf16[72,6144]{1,0:T(8,128)(2,1)S(1)} %pad_maximum_fusion.1), channel_id=1, source_target_pairs={{0,1},{1,2},{2,3},{3,0},{4,5},{5,6},{6,7},{7,4},{8,9},{9,10},{10,1... | collective-permute-start | bytes 2654216 | tf_op jit(solution)/shard_map/ppermute | solution.py:130
  26.5 22.9 %collective-permute-start.10 = (bf16[24,3072]{1,0:T(8,128)(2,1)S(1)}, bf16[24,3072]{1,0:T(8,128)(2,1)S(1)}, u32[]{:S(2)}, u32[]{:S(2)}) collective-permute-start(bf16[24,3072]{1,0:T(8,128)(2,1)S(1)} %slice.342), channel_id=1, source_target_pairs={{0,1},{1,2},{2,3},{3,0},{4,5},{5,6},{6,7},{7,4},{8,9},{9,10},{10,1... | collective-permute-start | bytes 442376 | tf_op jit(solution)/shard_map/ppermute | solution.py:130
  26.7 56.8 %collective-permute-start.19 = (bf16[72,6144]{1,0:T(8,128)(2,1)S(1)}, bf16[72,6144]{1,0:T(8,128)(2,1)S(1)}, u32[]{:S(2)}, u32[]{:S(2)}) collective-permute-start(bf16[72,6144]{1,0:T(8,128)(2,1)S(1)} %pad_maximum_fusion.2), channel_id=1, source_target_pairs={{0,12},{1,13},{2,14},{3,15},{4,0},{5,1},{6,2},{7,3},{8,4},{9,5},{1... | collective-permute-start | bytes 2654216 | tf_op jit(solution)/shard_map/ppermute | solution.py:130
  30.7 52.6 %collective-permute-start.17 = (bf16[72,6144]{1,0:T(8,128)(2,1)S(1)}, bf16[72,6144]{1,0:T(8,128)(2,1)S(1)}, u32[]{:S(2)}, u32[]{:S(2)}) collective-permute-start(bf16[72,6144]{1,0:T(8,128)(2,1)S(1)} %pad_maximum_fusion.2), channel_id=1, source_target_pairs={{0,4},{1,5},{2,6},{3,7},{4,8},{5,9},{6,10},{7,11},{8,12},{9,13},{1... | collective-permute-start | bytes 2654216 | tf_op jit(solution)/shard_map/ppermute | solution.py:130
  63.6 19.8 %collective-permute-start.23 = (bf16[24,6144]{1,0:T(8,128)(2,1)S(1)}, bf16[24,6144]{1,0:T(8,128)(2,1)S(1)}, u32[]{:S(2)}, u32[]{:S(2)}) collective-permute-start(bf16[24,6144]{1,0:T(8,128)(2,1)S(1)} %constant_dynamic-update-slice_fusion.2), channel_id=1, source_target_pairs={{0,4},{1,5},{2,6},{3,7},{4,8},{5,9},{6,10},{7,11},{8,12},{9,13},{1... | collective-permute-start | bytes 884744 | tf_op jit(solution)/shard_map/ppermute | solution.py:130
  92.2 12.6 %collective-permute-start.16 = (bf16[48,6144]{1,0:T(8,128)(2,1)S(1)}, bf16[48,6144]{1,0:T(8,128)(2,1)S(1)}, u32[]{:S(2)}, u32[]{:S(2)}) collective-permute-start(bf16[48,6144]{1,0:T(8,128)(2,1)S(1)} %pad_maximum_fusion.5), channel_id=1, source_target_pairs={{0,3},{1,0},{2,1},{3,2},{4,7},{5,4},{6,5},{7,6},{8,11},{9,8},{10,9... | collective-permute-start | bytes 1769480 | tf_op jit(solution)/shard_map/ppermute | solution.py:130
  94.9 10.7 %collective-permute-start.21 = (bf16[48,6144]{1,0:T(8,128)(2,1)S(1)}, bf16[48,6144]{1,0:T(8,128)(2,1)S(1)}, u32[]{:S(2)}, u32[]{:S(2)}) collective-permute-start(bf16[48,6144]{1,0:T(8,128)(2,1)S(1)} %pad_maximum_fusion.6), channel_id=1, source_target_pairs={{0,12},{1,13},{2,14},{3,15},{4,0},{5,1},{6,2},{7,3},{8,4},{9,5},{1... | collective-permute-start | bytes 1769480 | tf_op jit(solution)/shard_map/ppermute | solution.py:130
  96.5 55.6 %collective-permute-start.35 = (bf16[24,6144]{1,0:T(8,128)(2,1)S(1)}, bf16[24,6144]{1,0:T(8,128)(2,1)S(1)}, u32[]{:S(2)}, u32[]{:S(2)}) collective-permute-start(bf16[24,6144]{1,0:T(8,128)(2,1)S(1)} %get-tuple-element.11), channel_id=1, source_target_pairs={{0,1},{1,2},{2,3},{3,0},{4,5},{5,6},{6,7},{7,4},{8,9},{9,10},{10,1... | collective-permute-start | bytes 884744 | tf_op jit(solution)/shard_map/ppermute | solution.py:130
  104.7 40.4 %collective-permute-start.24 = (bf16[24,6144]{1,0:T(8,128)(2,1)S(1)}, bf16[24,6144]{1,0:T(8,128)(2,1)S(1)}, u32[]{:S(2)}, u32[]{:S(2)}) collective-permute-start(bf16[24,6144]{1,0:T(8,128)(2,1)S(1)} %get-tuple-element.14), channel_id=1, source_target_pairs={{0,4},{1,5},{2,6},{3,7},{4,8},{5,9},{6,10},{7,11},{8,12},{9,13},{1... | collective-permute-start | bytes 884744 | tf_op jit(solution)/shard_map/ppermute | solution.py:130
  104.8 16.7 %collective-permute-start.38 = (bf16[48,6144]{1,0:T(8,128)(2,1)S(1)}, bf16[48,6144]{1,0:T(8,128)(2,1)S(1)}, u32[]{:S(2)}, u32[]{:S(2)}) collective-permute-start(bf16[48,6144]{1,0:T(8,128)(2,1)S(1)} %get-tuple-element.16), channel_id=1, source_target_pairs={{0,1},{1,2},{2,3},{3,0},{4,5},{5,6},{6,7},{7,4},{8,9},{9,10},{10,1... | collective-permute-start | bytes 1769480 | tf_op jit(solution)/shard_map/ppermute | solution.py:130
  105.2 19.0 %collective-permute-start.27 = (bf16[48,6144]{1,0:T(8,128)(2,1)S(1)}, bf16[48,6144]{1,0:T(8,128)(2,1)S(1)}, u32[]{:S(2)}, u32[]{:S(2)}) collective-permute-start(bf16[48,6144]{1,0:T(8,128)(2,1)S(1)} %get-tuple-element.17), channel_id=1, source_target_pairs={{0,4},{1,5},{2,6},{3,7},{4,8},{5,9},{6,10},{7,11},{8,12},{9,13},{1... | collective-permute-start | bytes 1769480 | tf_op jit(solution)/shard_map/ppermute | solution.py:130
  105.6 27.7 %collective-permute-start.25 = (bf16[72,6144]{1,0:T(8,128)(2,1)S(1)}, bf16[72,6144]{1,0:T(8,128)(2,1)S(1)}, u32[]{:S(2)}, u32[]{:S(2)}) collective-permute-start(bf16[72,6144]{1,0:T(8,128)(2,1)S(1)} %pad_maximum_fusion.3), channel_id=1, source_target_pairs={{0,12},{1,13},{2,14},{3,15},{4,0},{5,1},{6,2},{7,3},{8,4},{9,5},{1... | collective-permute-start | bytes 2654216 | tf_op jit(solution)/shard_map/ppermute | solution.py:130
  127.3 15.3 %collective-permute-start.36 = (bf16[72,6144]{1,0:T(8,128)(2,1)S(1)}, bf16[72,6144]{1,0:T(8,128)(2,1)S(1)}, u32[]{:S(2)}, u32[]{:S(2)}) collective-permute-start(bf16[72,6144]{1,0:T(8,128)(2,1)S(1)} %pad_maximum_fusion.4), channel_id=1, source_target_pairs={{0,3},{1,0},{2,1},{3,2},{4,7},{5,4},{6,5},{7,6},{8,11},{9,8},{10,9... | collective-permute-start | bytes 2654216 | tf_op jit(solution)/shard_map/ppermute | solution.py:130
  133.2 12.1 %collective-permute-start.31 = (bf16[24,6144]{1,0:T(8,128)(2,1)S(1)}, bf16[24,6144]{1,0:T(8,128)(2,1)S(1)}, u32[]{:S(2)}, u32[]{:S(2)}) collective-permute-start(bf16[24,6144]{1,0:T(8,128)(2,1)S(1)} %get-tuple-element.25), channel_id=1, source_target_pairs={{0,4},{1,5},{2,6},{3,7},{4,8},{5,9},{6,10},{7,11},{8,12},{9,13},{1... | collective-permute-start | bytes 884744 | tf_op jit(solution)/shard_map/ppermute | solution.py:130
  133.3 12.2 %collective-permute-start.33 = (bf16[24,6144]{1,0:T(8,128)(2,1)S(1)}, bf16[24,6144]{1,0:T(8,128)(2,1)S(1)}, u32[]{:S(2)}, u32[]{:S(2)}) collective-permute-start(bf16[24,6144]{1,0:T(8,128)(2,1)S(1)} %get-tuple-element.28), channel_id=1, source_target_pairs={{0,12},{1,13},{2,14},{3,15},{4,0},{5,1},{6,2},{7,3},{8,4},{9,5},{1... | collective-permute-start | bytes 884744 | tf_op jit(solution)/shard_map/ppermute | solution.py:130
  145.3 23.0 %collective-permute-start.39 = (bf16[48,6144]{1,0:T(8,128)(2,1)S(1)}, bf16[48,6144]{1,0:T(8,128)(2,1)S(1)}, u32[]{:S(2)}, u32[]{:S(2)}) collective-permute-start(bf16[48,6144]{1,0:T(8,128)(2,1)S(1)} %get-tuple-element.19), channel_id=1, source_target_pairs={{0,1},{1,2},{2,3},{3,0},{4,5},{5,6},{6,7},{7,4},{8,9},{9,10},{10,1... | collective-permute-start | bytes 1769480 | tf_op jit(solution)/shard_map/ppermute | solution.py:130
  145.6 10.2 %collective-permute-start.44 = (bf16[24,6144]{1,0:T(8,128)(2,1)S(1)}, bf16[24,6144]{1,0:T(8,128)(2,1)S(1)}, u32[]{:S(2)}, u32[]{:S(2)}) collective-permute-start(bf16[24,6144]{1,0:T(8,128)(2,1)S(1)} %get-tuple-element.27), channel_id=1, source_target_pairs={{0,3},{1,0},{2,1},{3,2},{4,7},{5,4},{6,5},{7,6},{8,11},{9,8},{10,9... | collective-permute-start | bytes 884744 | tf_op jit(solution)/shard_map/ppermute | solution.py:130
  148.7 15.3 %collective-permute-start.37 = (bf16[24,6144]{1,0:T(8,128)(2,1)S(1)}, bf16[24,6144]{1,0:T(8,128)(2,1)S(1)}, u32[]{:S(2)}, u32[]{:S(2)}) collective-permute-start(bf16[24,6144]{1,0:T(8,128)(2,1)S(1)} %add_convert_fusion.8), channel_id=1, source_target_pairs={{0,3},{1,0},{2,1},{3,2},{4,7},{5,4},{6,5},{7,6},{8,11},{9,8},{10,9... | collective-permute-start | bytes 884744 | tf_op jit(solution)/shard_map/ppermute | solution.py:130
  152.1 12.3 %collective-permute-start.28 = (bf16[48,6144]{1,0:T(8,128)(2,1)S(1)}, bf16[48,6144]{1,0:T(8,128)(2,1)S(1)}, u32[]{:S(2)}, u32[]{:S(2)}) collective-permute-start(bf16[48,6144]{1,0:T(8,128)(2,1)S(1)} %get-tuple-element.20), channel_id=1, source_target_pairs={{0,4},{1,5},{2,6},{3,7},{4,8},{5,9},{6,10},{7,11},{8,12},{9,13},{1... | collective-permute-start | bytes 1769480 | tf_op jit(solution)/shard_map/ppermute | solution.py:130
  152.3 16.3 %collective-permute-start.34 = (bf16[24,6144]{1,0:T(8,128)(2,1)S(1)}, bf16[24,6144]{1,0:T(8,128)(2,1)S(1)}, u32[]{:S(2)}, u32[]{:S(2)}) collective-permute-start(bf16[24,6144]{1,0:T(8,128)(2,1)S(1)} %get-tuple-element.32), channel_id=1, source_target_pairs={{0,2},{1,3},{2,0},{3,1},{4,6},{5,7},{6,4},{7,5},{8,10},{9,11},{10,... | collective-permute-start | bytes 884744 | tf_op jit(solution)/shard_map/ppermute | solution.py:130
  164.3 12.1 %collective-permute-start.45 = (bf16[24,6144]{1,0:T(8,128)(2,1)S(1)}, bf16[24,6144]{1,0:T(8,128)(2,1)S(1)}, u32[]{:S(2)}, u32[]{:S(2)}) collective-permute-start(bf16[24,6144]{1,0:T(8,128)(2,1)S(1)} %get-tuple-element.30), channel_id=1, source_target_pairs={{0,8},{1,9},{2,10},{3,11},{4,12},{5,13},{6,14},{7,15},{8,0},{9,1},... | collective-permute-start | bytes 884744 | tf_op jit(solution)/shard_map/ppermute | solution.py:130
  183.9 26.2 %collective-permute-start.49 = (bf16[96,3072]{1,0:T(8,128)(2,1)S(1)}, bf16[96,3072]{1,0:T(8,128)(2,1)S(1)}, u32[]{:S(2)}, u32[]{:S(2)}) collective-permute-start(bf16[96,3072]{1,0:T(8,128)(2,1)S(1)} %pad_maximum_fusion.7), channel_id=1, source_target_pairs={{0,16},{16,0},{32,48},{48,32},{64,80},{80,64},{96,112},{112,96},{1... | collective-permute-start | bytes 1769480 | tf_op jit(solution)/shard_map/ppermute | solution.py:122
  (34 other events, 351.0 us)
